TPU v7x, 512 devices: a whole 4x4x16 slice. The times are simulated.
512 devices in a mesh: row: 32 (over z, core), col: 16 (over x, y).
Axes of the slice: x: 4, y: 4, z: 16, core: 2. Of those that a mesh axis runs over, the one named last changes fastest.
Arguments:
- trailing: float32 [16384, 16384], P('row', 'col'), may hold values from -6 to 6
- panel: float32 [16384, 512], P(('row', 'col')), may hold values from -0.25 to 0.25
- inv_factor: float32 [512, 512], P(None, 'col'), as said below
- later_series: float32 [16384, 1024], P('row', 'col'), may hold values from -6 to 6
- fold_series: float32 [512, 1024], P('row', 'col'), may hold values from -6 to 6
- fold_len: int32 [1024], P('col'), may hold values from 1 to 32, as said below
Outputs:
- new_trailing: float32 [16384, 16384], P('row', 'col')
- new_series: float32 [16384, 1024], P('row', 'col')
Inputs may be any that keep to these rules, and one draw needn't show every extreme that they name: inv_factor is lower triangular with a diagonal between 1 and 2. `fold_len`: some series reach all 32 blocks and some only one.
All inputs are finite; a program needn't handle non-finite values.
Results may differ from a plain program's by a relative error of at most 0.0003.
Values sent between devices are 32-bit elements; how exact they have to be, the bound alone decides.
No kernel may reach another device: no remote copies, remote signals or barrier semaphores. Data moves between devices by JAX's collectives and lax.ppermute only.
A program may use at most 64 MiB of HBM per device.

v0:
```python
import jax
import jax.numpy as jnp
from jax import lax
from jax.experimental import pallas as pl
from jax.experimental.pallas import tpu as pltpu
from jax.sharding import PartitionSpec as P


AXES = ("row", "col")
X, Y, Z, CORES = 4, 4, 16, 2
NT = (((1,), (1,)), ((), ()))
NN = (((1,), (0,)), ((), ()))


def device(x, y, z, k):
    return ((z % Z) * CORES + k) * (X * Y) + (x % X) * Y + y % Y


def pairs(move):
    out = []
    for x in range(X):
        for y in range(Y):
            for z in range(Z):
                for k in range(CORES):
                    out.append((device(x, y, z, k), device(*move(x, y, z, k))))
    return out


STEPS = {
    8: (0, 0),
    7: (1, 0), 9: (3, 0), 6: (0, 1), 10: (0, 3),
    5: (1, 1), 11: (1, 3), 4: (3, 1), 12: (3, 3), 3: (2, 0), 13: (0, 2),
    2: (2, 1), 14: (2, 3), 1: (1, 2), 15: (3, 2),
    0: (2, 2),
}
PLACES = {place: step for step, place in STEPS.items()}


def table(axis):
    bits = sum(STEPS[step][axis] << (2 * step) for step in range(Z))
    return bits - (1 << 32) if bits >> 31 else bits


TABLE_X, TABLE_Y = table(0), table(1)


def transpose_move(x, y, z, k):
    cx, cy = z // Y, z % Y
    return cx, cy, z + PLACES[(x - cx) % X, (y - cy) % Y], k


TRANSPOSE = pairs(transpose_move)
SWAP = pairs(lambda x, y, z, k: (x, y, z, 1 - k))
PM2 = pairs(lambda x, y, z, k: (x, y, z + 2 if k == 0 else z - 2, k))


def shift(d):
    return pairs(lambda x, y, z, k: (x, y, z + d, k))


def send(array, moves):
    return lax.ppermute(array, AXES, moves)


def near_memory(array):
    return pltpu.with_memory_space_constraint(array, pltpu.VMEM)


def split(x):
    high = x.astype(jnp.bfloat16)
    return high, (x - high.astype(jnp.float32)).astype(jnp.bfloat16)


def dot3(a, b, dims):
    ah, al = a
    bh, bl = b
    dot = lambda u, v: lax.dot_general(u, v, dims, preferred_element_type=jnp.float32)
    return dot(ah, bh) + (dot(ah, bl) + dot(al, bh))


def pack_body(chunk, fold, out):
    for j in range(4):
        out[32 * j:32 * j + 32, :] = chunk[:, 128 * j:128 * j + 128]
    out[128:136, 0:64] = fold[0:8, :]
    out[128:136, 64:128] = fold[8:16, :]


def weight_body(gathered, other, out, rows, inv):
    k = lax.axis_index("row") % 2
    for c in range(16):
        rows[32 * c:32 * c + 32, :] = gathered[c, 0:32, :]
        inv[pl.ds(pl.multiple_of(32 * c + 16 * k, 16), 16), :] = gathered[c, 32:48, :]
        inv[pl.ds(pl.multiple_of(32 * c + 16 - 16 * k, 16), 16), :] = other[c]
    inverse = split(inv[...])
    solved = dot3(split(rows[...]), inverse, NN)
    out[...] = dot3(split(solved), inverse, NT)


OFFSETS = (0, -4, 4, 8)


def where_am_i():
    row = lax.axis_index("row")
    return row, lax.axis_index("col"), row // 2, row % 2


def place(ref, base, group, core, z, col, cols, fold):
    for slot in range(4):
        step = OFFSETS[slot]
        far = (0, -1, 1)[group] + step if group < 3 else step - 2 + 4 * core
        at = (z + far + 32) & 15
        hop = 2 * ((at - col) & 15)
        px = (col // 4 + (jnp.int32(TABLE_X) >> hop)) & 3
        py = (col + (jnp.int32(TABLE_Y) >> hop)) & 3
        rows = pl.ds(pl.multiple_of(32 * (4 * px + py), 32), 32)
        start = base + 136 * slot
        for j in range(4):
            cols[rows, 128 * j:128 * j + 128] = ref[start + 32 * j:start + 32 * j + 32, :]
        tile = ref[start + 128:start + 136, :]
        first = pl.multiple_of(16 * (2 * at + core), 16)
        fold[pl.ds(first, 8), :] = tile
        fold[pl.ds(first + 8, 8), :] = pltpu.roll(tile, 64, 1)


def join_body(a, b, c, weight, out):
    out[0:544, :] = a[...]
    out[544:1088, :] = b[...]
    out[1088:1632, :] = c[...]


def update(half, w, cols, trailing, out, vin, vout, sem_in, sem_out, row, col):
    span = pl.ds(pl.multiple_of(512 * half, 512), 512)
    lower = 2 * col + half <= row
    pltpu.make_async_copy(trailing.at[:, span], vin, sem_in).wait()

    @pl.when(lower)
    def _():
        vout[...] = vin[...] - dot3(w, split(cols[...]), NT)

    @pl.when(jnp.logical_not(lower))
    def _():
        vout[...] = vin[...]

    copy = pltpu.make_async_copy(vout, out.at[:, span], sem_out)
    copy.start()
    copy.wait()


def first_body(weight, mine0, mine1, mine2, mine3, trailing, out, fold, cols, vin, vout, sem_in, sem_out):
    row, col, z, k = where_am_i()
    span = pl.ds(pl.multiple_of(512 * k, 512), 512)
    pltpu.make_async_copy(trailing.at[:, span], vin, sem_in).start()
    for group, ref in enumerate((mine0, mine1, mine2, mine3)):
        place(ref, 0, group, k, z, col, cols, fold)
    update(k, split(weight[...]), cols, trailing, out, vin, vout, sem_in, sem_out, row, col)


def second_body(weight, other0, others, trailing, part, half_fold, series, length, out, out_s, cols, fold, vin, vout, sem_in, sem_out):
    row, col, z, k = where_am_i()
    span = pl.ds(pl.multiple_of(512 * (1 - k), 512), 512)
    pltpu.make_async_copy(trailing.at[:, span], vin, sem_in).start()
    for at in range(16):
        rows = pl.ds(pl.multiple_of(32 * at + 16 * k, 16), 16)
        fold[rows, :] = half_fold[rows, :]
    place(other0, 0, 0, 1 - k, z, col, cols, fold)
    for group in range(1, 4):
        place(others, 544 * (group - 1), group, 1 - k, z, col, cols, fold)
    w = split(weight[...])
    correction = dot3(w, split(fold[...]), NN)
    active = row < length[...]
    correction = jnp.where(active, correction, 0.0)
    out_s[...] = series[...] - correction.T[0:64, :]
    update(1 - k, w, cols, trailing, out, vin, vout, sem_in, sem_out, row, col)


def spread_body(panel, stripe, out):
    k = lax.axis_index("row") % 2
    half = stripe[pl.ds(pl.multiple_of(16 * k, 16), 16), :]
    for c in range(16):
        out[c, 0:32, :] = panel[...]
        out[c, 32:48, :] = half


VMEM = pl.BlockSpec(memory_space=pltpu.VMEM)
ANY = pl.BlockSpec(memory_space=pl.ANY)


def shape(*dims):
    return jax.ShapeDtypeStruct(dims, jnp.float32)


def kernel(body, out, outs, memory, scratch=(), alias=None):
    def call(*args):
        args = [near_memory(a) if m == "v" else a for a, m in zip(args, memory)]
        return pl.pallas_call(
            body,
            out_shape=out,
            in_specs=[VMEM if m == "v" else ANY for m in memory],
            out_specs=outs,
            scratch_shapes=list(scratch),
            input_output_aliases=alias or {},
        )(*args)

    return call


def block(*dims):
    return pltpu.VMEM(dims, jnp.float32)


def step(trailing, panel, inv_factor, later_series, fold_series, fold_len):
    chunk = send(panel, TRANSPOSE)
    load = kernel(spread_body, shape(16, 48, 512), VMEM, "vv")(panel, inv_factor.T)
    gathered = lax.all_to_all(load, "col", 0, 0, tiled=True)
    packed = kernel(pack_body, shape(136, 128), VMEM, "vv")(chunk, fold_series)
    far = [packed] + [send(packed, shift(d)) for d in (4, -4, 8)]
    near = jnp.concatenate(far, 0)
    mine = [send(near, shift(1)), send(near, shift(-1)), send(near, PM2)]
    other0 = send(near, SWAP)
    other = send(gathered[:, 32:, :], SWAP)
    weight = kernel(weight_body, shape(512, 512), VMEM, "vv", [block(512, 512), block(512, 512)])(gathered, other)
    joined = kernel(join_body, shape(1632, 128), VMEM, "vvva")(*mine, weight)
    others = send(joined, SWAP)
    work = [block(512, 512), block(512, 512), pltpu.SemaphoreType.DMA, pltpu.SemaphoreType.DMA]
    part, half_fold = kernel(
        first_body, (shape(512, 1024), shape(512, 128)), (ANY, VMEM), "vvvvva", [block(512, 512)] + work
    )(weight, near, *mine, trailing)
    length = jnp.pad(fold_len, (0, 64))[None, :]
    out, series = kernel(
        second_body,
        (shape(512, 1024), shape(64, 512)),
        (ANY, VMEM),
        "vvvaavvv",
        [block(512, 512), block(512, 128)] + work,
        {4: 0},
    )(weight, other0, others, trailing, part, half_fold, later_series.T, length)
    return out, series.T


def solution(mesh):
    in_specs = (
        P("row", "col"),
        P(("row", "col"), None),
        P(None, "col"),
        P("row", "col"),
        P("row", "col"),
        P("col"),
    )
    out_specs = (P("row", "col"), P("row", "col"))
    return jax.shard_map(step, mesh=mesh, in_specs=in_specs, out_specs=out_specs, check_vma=False)
```

profile of v0, /device:TPU:1, one launch (start us, length us, event | category | flops | bytes accessed | tf_op | source)
XLA Modules:
  0.0 111.3 jit_solution(17039980895938909968)
XLA Ops:
  2.3 1.3 %shard_map.77 = f32[16,48,512]{2,1,0:T(8,128)} custom-call(f32[32,512]{1,0:T(8,128)S(1)} %copy-done.9, f32[32,512]{1,0:T(8,128)S(1)} %bitcast.6), custom_call_target="tpu_custom_call" | custom-call | tf_op jit(solution)/shard_map/pallas_call | solution.py:195
  3.6 7.7 %all-to-all-start = ((f32[16,48,512]{2,1,0:T(8,128)}), f32[16,48,512]{2,1,0:T(8,128)S(1)}, u32[]{:S(2)}, u32[]{:S(2)}) async-start(f32[16,48,512]{2,1,0:T(8,128)} %shard_map.77), calls=%async_computation | async-start | bytes 3145728 | tf_op jit(solution)/shard_map/all_to_all | solution.py:214
  11.3 15.4 %collective-permute-start.1 = (f32[32,512]{1,0:T(8,128)S(1)}, f32[32,512]{1,0:T(8,128)S(1)}, u32[]{:S(2)}, u32[]{:S(2)}) collective-permute-start(f32[32,512]{1,0:T(8,128)S(1)} %copy-done.10), channel_id=1, source_target_pairs={{0,256},{16,272},{32,353},{48,369},{64,482},{80,498},{96,291},{112... | collective-permute-start | bytes 196616 | tf_op jit(solution)/shard_map/ppermute | solution.py:62
  26.8 4.7 %all-to-all-done.gathered = f32[16,48,512]{2,1,0:T(8,128)S(1)} async-done(((f32[16,48,512]{2,1,0:T(8,128)}), f32[16,48,512]{2,1,0:T(8,128)S(1)}, u32[]{:S(2)}, u32[]{:S(2)}) %all-to-all-start) | async-done | bytes 1572896 | tf_op jit(solution)/shard_map/all_to_all | solution.py:214
  31.5 1.1 %copy-done.2 = f32[16,48,512]{2,1,0:T(8,128)} copy-done((f32[16,48,512]{2,1,0:T(8,128)}, f32[16,48,512]{2,1,0:T(8,128)S(1)}, u32[]{:S(2)}) %copy-start.2) | copy-done | bytes 1572888
  32.6 7.0 %collective-permute-start = (f32[16,16,512]{2,1,0:T(8,128)S(1)}, f32[16,16,512]{2,1,0:T(8,128)S(1)}, u32[]{:S(2)}, u32[]{:S(2)}) collective-permute-start(f32[16,16,512]{2,1,0:T(8,128)S(1)} %slice.4), channel_id=1, source_target_pairs={{0,16},{16,0},{32,48},{48,32},{64,80},{80,64},{96,112},{112,96},{1... | collective-permute-start | bytes 1572872 | tf_op jit(solution)/shard_map/ppermute | solution.py:62
  40.4 14.8 %collective-permute-start.4 = (f32[136,128]{1,0:T(8,128)}, f32[136,128]{1,0:T(8,128)S(1)}, u32[]{:S(2)}, u32[]{:S(2)}) collective-permute-start(f32[136,128]{1,0:T(8,128)} %shard_map.79), channel_id=1, source_target_pairs={{0,256},{16,272},{32,288},{48,304},{64,320},{80,336},{96,352},{112... | collective-permute-start | bytes 208904 | tf_op jit(solution)/shard_map/ppermute | solution.py:62
  55.3 1.9 %collective-permute-start.3 = (f32[136,128]{1,0:T(8,128)}, f32[136,128]{1,0:T(8,128)S(1)}, u32[]{:S(2)}, u32[]{:S(2)}) collective-permute-start(f32[136,128]{1,0:T(8,128)} %shard_map.79), channel_id=1, source_target_pairs={{0,384},{16,400},{32,416},{48,432},{64,448},{80,464},{96,480},{112... | collective-permute-start | bytes 208904 | tf_op jit(solution)/shard_map/ppermute | solution.py:62
  57.2 7.3 %collective-permute-start.2 = (f32[136,128]{1,0:T(8,128)}, f32[136,128]{1,0:T(8,128)S(1)}, u32[]{:S(2)}, u32[]{:S(2)}) collective-permute-start(f32[136,128]{1,0:T(8,128)} %shard_map.79), channel_id=1, source_target_pairs={{0,128},{16,144},{32,160},{48,176},{64,192},{80,208},{96,224},{112... | collective-permute-start | bytes 208904 | tf_op jit(solution)/shard_map/ppermute | solution.py:62
  64.5 2.4 %collective-permute-done.3 = f32[136,128]{1,0:T(8,128)S(1)} collective-permute-done((f32[136,128]{1,0:T(8,128)}, f32[136,128]{1,0:T(8,128)S(1)}, u32[]{:S(2)}, u32[]{:S(2)}) %collective-permute-start.3) | collective-permute-done | bytes 69664 | tf_op jit(solution)/shard_map/ppermute | solution.py:62
  67.8 7.9 %collective-permute-start.8 = (f32[544,128]{1,0:T(8,128)S(1)}, f32[544,128]{1,0:T(8,128)}, u32[]{:S(2)}, u32[]{:S(2)}) collective-permute-start(f32[544,128]{1,0:T(8,128)S(1)} %pad_maximum_fusion.mine0), channel_id=1, source_target_pairs={{0,64},{16,464},{32,96},{48,496},{64,128},{80,16},{96,160},{112,48... | collective-permute-start | bytes 835592 | tf_op jit(solution)/shard_map/ppermute | solution.py:62
  75.7 2.8 %collective-permute-start.7 = (f32[544,128]{1,0:T(8,128)S(1)}, f32[544,128]{1,0:T(8,128)}, u32[]{:S(2)}, u32[]{:S(2)}) collective-permute-start(f32[544,128]{1,0:T(8,128)S(1)} %pad_maximum_fusion.mine0), channel_id=1, source_target_pairs={{0,480},{16,496},{32,0},{48,16},{64,32},{80,48},{96,64},{112,80},{... | collective-permute-start | bytes 835592 | tf_op jit(solution)/shard_map/ppermute | solution.py:62
  78.5 3.1 %collective-permute-start.6 = (f32[544,128]{1,0:T(8,128)S(1)}, f32[544,128]{1,0:T(8,128)}, u32[]{:S(2)}, u32[]{:S(2)}) collective-permute-start(f32[544,128]{1,0:T(8,128)S(1)} %pad_maximum_fusion.mine0), channel_id=1, source_target_pairs={{0,32},{16,48},{32,64},{48,80},{64,96},{80,112},{96,128},{112,144}... | collective-permute-start | bytes 835592 | tf_op jit(solution)/shard_map/ppermute | solution.py:62
  81.7 1.4 %copy-done.3 = f32[16,48,512]{2,1,0:T(8,128)S(1)} copy-done((f32[16,48,512]{2,1,0:T(8,128)S(1)}, f32[16,48,512]{2,1,0:T(8,128)}, u32[]{:S(2)}) %copy-start.3) | copy-done | bytes 1572888
  83.1 2.9 %shard_map.78.weight = f32[512,512]{1,0:T(8,128)} custom-call(f32[16,48,512]{2,1,0:T(8,128)S(1)} %copy-done.3, f32[16,16,512]{2,1,0:T(8,128)S(1)} %collective-permute-done.other), custom_call_target="tpu_custom_call" | custom-call | tf_op jit(solution)/shard_map/pallas_call | solution.py:195
  86.0 2.2 %collective-permute-done.7.b.mine2 = f32[544,128]{1,0:T(8,128)} collective-permute-done((f32[544,128]{1,0:T(8,128)S(1)}, f32[544,128]{1,0:T(8,128)}, u32[]{:S(2)}, u32[]{:S(2)}) %collective-permute-start.7) | collective-permute-done | bytes 278560 | tf_op jit(solution)/shard_map/ppermute | solution.py:62
  88.2 1.4 %collective-permute-done.6.a.mine1 = f32[544,128]{1,0:T(8,128)} collective-permute-done((f32[544,128]{1,0:T(8,128)S(1)}, f32[544,128]{1,0:T(8,128)}, u32[]{:S(2)}, u32[]{:S(2)}) %collective-permute-start.6) | collective-permute-done | bytes 278560 | tf_op jit(solution)/shard_map/ppermute | solution.py:62
  89.7 2.1 %shard_map.80 = f32[1632,128]{1,0:T(8,128)} custom-call(f32[544,128]{1,0:T(8,128)} %collective-permute-done.6.a.mine1, f32[544,128]{1,0:T(8,128)} %collective-permute-done.7.b.mine2, f32[544,128]{1,0:T(8,128)} %collective-permute-done.8.c.mine3, f32[512,512]{1,0:T(8,128)} %shard_map.78.weight), custom_call_target="tpu_custom_call" | custom-call | tf_op jit(solution)/shard_map/pallas_call | solution.py:195
  91.8 3.4 %collective-permute-start.9 = (f32[1632,128]{1,0:T(8,128)}, f32[1632,128]{1,0:T(8,128)}, u32[]{:S(2)}, u32[]{:S(2)}) collective-permute-start(f32[1632,128]{1,0:T(8,128)} %shard_map.80), channel_id=1, source_target_pairs={{0,16},{16,0},{32,48},{48,32},{64,80},{80,64},{96,112},{112,96},{1... | collective-permute-start | bytes 2506760 | tf_op jit(solution)/shard_map/ppermute | solution.py:62
  95.2 1.9 %collective-permute-start.5 = (f32[544,128]{1,0:T(8,128)S(1)}, f32[544,128]{1,0:T(8,128)S(1)}, u32[]{:S(2)}, u32[]{:S(2)}) collective-permute-start(f32[544,128]{1,0:T(8,128)S(1)} %pad_maximum_fusion.mine0), channel_id=1, source_target_pairs={{0,16},{16,0},{32,48},{48,32},{64,80},{80,64},{96,112},{112,96},{1... | collective-permute-start | bytes 835592 | tf_op jit(solution)/shard_map/ppermute | solution.py:62
  97.2 5.4 %shard_map.81 = (f32[512,1024]{1,0:T(8,128)}, f32[512,128]{1,0:T(8,128)}) custom-call(f32[512,512]{1,0:T(8,128)S(1)} %copy-done, f32[544,128]{1,0:T(8,128)S(1)} %pad_maximum_fusion.mine0, f32[544,128]{1,0:T(8,128)} %collective-permute-done.6.a.mine1, f32[544,128]{1,0:T(8,128)} %collective-permute-done.7.b.mine2, f32[544,128]{1,0:T(8,128)} %collective-permute-done.8.c.mine3, ...), custom_call_target="tpu_custom_call" | custom-call | tf_op jit(solution)/shard_map/pallas_call | solution.py:195
  103.3 1.0 copy-done.5
  104.3 0.9 copy-done.6
  106.2 5.1 %shard_map.82 = (f32[512,1024]{1,0:T(8,128)}, f32[64,512]{1,0:T(8,128)}) custom-call(f32[512,512]{1,0:T(8,128)S(1)} %copy-done.1, f32[544,128]{1,0:T(8,128)S(1)} %copy-done.5, f32[1632,128]{1,0:T(8,128)} %collective-permute-done.9.others, f32[512,1024]{1,0:T(8,128)} %trailing.3, f32[512,1024]{1,0:T(8,128)} %get-tuple-element.6.part, ...), custom_call_target="tpu_custom_call", output_to_operand_aliasing={{0}: (4, {})} | custom-call | tf_op jit(solution)/shard_map/pallas_call | solution.py:195
  (33 shorter events, 5.0 us)
Async XLA Ops:
  0.6 0.8 copy-start.8
  1.5 0.8 copy-start.9
  2.3 9.0 %copy-start.10 = (f32[32,512]{1,0:T(8,128)S(1)}, f32[32,512]{1,0:T(8,128)}, u32[]{:S(2)}) copy-start(f32[32,512]{1,0:T(8,128)} %panel.1) | copy-start | bytes 196612
  3.6 36.1 %copy-start.11 = (f32[16,64]{1,0:T(8,128)S(1)}, f32[16,64]{1,0:T(8,128)}, u32[]{:S(2)}) copy-start(f32[16,64]{1,0:T(8,128)} %fold.1) | copy-start | bytes 12292
  3.6 27.9 %all-to-all-start = ((f32[16,48,512]{2,1,0:T(8,128)}), f32[16,48,512]{2,1,0:T(8,128)S(1)}, u32[]{:S(2)}, u32[]{:S(2)}) async-start(f32[16,48,512]{2,1,0:T(8,128)} %shard_map.77), calls=%async_computation | async-start | bytes 3145728 | tf_op jit(solution)/shard_map/all_to_all | solution.py:214
  11.3 28.4 %collective-permute-start.1 = (f32[32,512]{1,0:T(8,128)S(1)}, f32[32,512]{1,0:T(8,128)S(1)}, u32[]{:S(2)}, u32[]{:S(2)}) collective-permute-start(f32[32,512]{1,0:T(8,128)S(1)} %copy-done.10), channel_id=1, source_target_pairs={{0,256},{16,272},{32,353},{48,369},{64,482},{80,498},{96,291},{112... | collective-permute-start | bytes 196616 | tf_op jit(solution)/shard_map/ppermute | solution.py:62
  31.5 1.1 %copy-start.2 = (f32[16,48,512]{2,1,0:T(8,128)}, f32[16,48,512]{2,1,0:T(8,128)S(1)}, u32[]{:S(2)}) copy-start(f32[16,48,512]{2,1,0:T(8,128)S(1)} %all-to-all-done.gathered) | copy-start | bytes 4718596
  32.6 49.0 %collective-permute-start = (f32[16,16,512]{2,1,0:T(8,128)S(1)}, f32[16,16,512]{2,1,0:T(8,128)S(1)}, u32[]{:S(2)}, u32[]{:S(2)}) collective-permute-start(f32[16,16,512]{2,1,0:T(8,128)S(1)} %slice.4), channel_id=1, source_target_pairs={{0,16},{16,0},{32,48},{48,32},{64,80},{80,64},{96,112},{112,96},{1... | collective-permute-start | bytes 1572872 | tf_op jit(solution)/shard_map/ppermute | solution.py:62
  40.4 24.1 %collective-permute-start.4 = (f32[136,128]{1,0:T(8,128)}, f32[136,128]{1,0:T(8,128)S(1)}, u32[]{:S(2)}, u32[]{:S(2)}) collective-permute-start(f32[136,128]{1,0:T(8,128)} %shard_map.79), channel_id=1, source_target_pairs={{0,256},{16,272},{32,288},{48,304},{64,320},{80,336},{96,352},{112... | collective-permute-start | bytes 208904 | tf_op jit(solution)/shard_map/ppermute | solution.py:62
  55.3 11.6 %collective-permute-start.3 = (f32[136,128]{1,0:T(8,128)}, f32[136,128]{1,0:T(8,128)S(1)}, u32[]{:S(2)}, u32[]{:S(2)}) collective-permute-start(f32[136,128]{1,0:T(8,128)} %shard_map.79), channel_id=1, source_target_pairs={{0,384},{16,400},{32,416},{48,432},{64,448},{80,464},{96,480},{112... | collective-permute-start | bytes 208904 | tf_op jit(solution)/shard_map/ppermute | solution.py:62
  57.2 9.7 %collective-permute-start.2 = (f32[136,128]{1,0:T(8,128)}, f32[136,128]{1,0:T(8,128)S(1)}, u32[]{:S(2)}, u32[]{:S(2)}) collective-permute-start(f32[136,128]{1,0:T(8,128)} %shard_map.79), channel_id=1, source_target_pairs={{0,128},{16,144},{32,160},{48,176},{64,192},{80,208},{96,224},{112... | collective-permute-start | bytes 208904 | tf_op jit(solution)/shard_map/ppermute | solution.py:62
  67.8 18.2 %collective-permute-start.8 = (f32[544,128]{1,0:T(8,128)S(1)}, f32[544,128]{1,0:T(8,128)}, u32[]{:S(2)}, u32[]{:S(2)}) collective-permute-start(f32[544,128]{1,0:T(8,128)S(1)} %pad_maximum_fusion.mine0), channel_id=1, source_target_pairs={{0,64},{16,464},{32,96},{48,496},{64,128},{80,16},{96,160},{112,48... | collective-permute-start | bytes 835592 | tf_op jit(solution)/shard_map/ppermute | solution.py:62
  75.7 12.5 %collective-permute-start.7 = (f32[544,128]{1,0:T(8,128)S(1)}, f32[544,128]{1,0:T(8,128)}, u32[]{:S(2)}, u32[]{:S(2)}) collective-permute-start(f32[544,128]{1,0:T(8,128)S(1)} %pad_maximum_fusion.mine0), channel_id=1, source_target_pairs={{0,480},{16,496},{32,0},{48,16},{64,32},{80,48},{96,64},{112,80},{... | collective-permute-start | bytes 835592 | tf_op jit(solution)/shard_map/ppermute | solution.py:62
  78.5 11.1 %collective-permute-start.6 = (f32[544,128]{1,0:T(8,128)S(1)}, f32[544,128]{1,0:T(8,128)}, u32[]{:S(2)}, u32[]{:S(2)}) collective-permute-start(f32[544,128]{1,0:T(8,128)S(1)} %pad_maximum_fusion.mine0), channel_id=1, source_target_pairs={{0,32},{16,48},{32,64},{48,80},{64,96},{80,112},{96,128},{112,144}... | collective-permute-start | bytes 835592 | tf_op jit(solution)/shard_map/ppermute | solution.py:62
  81.7 1.4 %copy-start.3 = (f32[16,48,512]{2,1,0:T(8,128)S(1)}, f32[16,48,512]{2,1,0:T(8,128)}, u32[]{:S(2)}) copy-start(f32[16,48,512]{2,1,0:T(8,128)} %copy-done.2) | copy-start | bytes 4718596
  86.0 11.1 %copy-start.12 = (s32[64]{0:T(128)S(1)}, s32[64]{0:T(128)}, u32[]{:S(2)}) copy-start(s32[64]{0:T(128)} %param.11) | copy-start | bytes 772
  86.0 11.2 %copy-start = (f32[512,512]{1,0:T(8,128)S(1)}, f32[512,512]{1,0:T(8,128)}, u32[]{:S(2)}) copy-start(f32[512,512]{1,0:T(8,128)} %shard_map.78.weight) | copy-start | bytes 3145732
  91.8 11.6 %collective-permute-start.9 = (f32[1632,128]{1,0:T(8,128)}, f32[1632,128]{1,0:T(8,128)}, u32[]{:S(2)}, u32[]{:S(2)}) collective-permute-start(f32[1632,128]{1,0:T(8,128)} %shard_map.80), channel_id=1, source_target_pairs={{0,16},{16,0},{32,48},{48,32},{64,80},{80,64},{96,112},{112,96},{1... | collective-permute-start | bytes 2506760 | tf_op jit(solution)/shard_map/ppermute | solution.py:62
  95.2 7.4 %collective-permute-start.5 = (f32[544,128]{1,0:T(8,128)S(1)}, f32[544,128]{1,0:T(8,128)S(1)}, u32[]{:S(2)}, u32[]{:S(2)}) collective-permute-start(f32[544,128]{1,0:T(8,128)S(1)} %pad_maximum_fusion.mine0), channel_id=1, source_target_pairs={{0,16},{16,0},{32,48},{48,32},{64,80},{80,64},{96,112},{112,96},{1... | collective-permute-start | bytes 835592 | tf_op jit(solution)/shard_map/ppermute | solution.py:62
  97.2 6.2 %copy-start.1 = (f32[512,512]{1,0:T(8,128)S(1)}, f32[512,512]{1,0:T(8,128)}, u32[]{:S(2)}) copy-start(f32[512,512]{1,0:T(8,128)} %shard_map.78.weight) | copy-start | bytes 3145732
  102.6 0.7 copy-start.4
  103.3 1.0 copy-start.5
  104.3 0.9 copy-start.6
  105.2 0.9 copy-start.7
where the time goes:
time: 112 us; the launch traced here: 111 us
  starting transfers between devices  73.4 us (66%)
  Pallas kernels  17.5 us (16%)
  waiting for transfers between devices  10.8 us (10%)
  local copies, waits for them, and re-layouts  7.79 us (7%)
    ppermute x10, starting transfers between devices, send(): return lax.ppermute(array, AXES, moves)  65.7 us
    pallas_call x6, Pallas kernels, call(): pl.pallas_call(body, out_shape=out, in_specs=[VMEM if m == 'v' else ANY f...  17.5 us
    unnamed x26, local copies, waits for them, and re-layouts  7.75 us
    all_to_all x1, starting transfers between devices, step(): gathered = lax.all_to_all(load, 'col', 0, 0, tiled=True)  7.7 us
    ppermute x10, waiting for transfers between devices, send(): return lax.ppermute(array, AXES, moves)  6.11 us
    all_to_all x1, waiting for transfers between devices, step(): gathered = lax.all_to_all(load, 'col', 0, 0, tiled=True)  4.71 us
  transfers between devices with their start and end apart: 11, of which 4 were waited for; matrix products, arithmetic and copies ran while one was open for 1% of the time, Pallas kernels for 8%

commit v1 on v0

v1 whole, which is shorter than its diff:
```python
import jax
import jax.numpy as jnp
from jax import lax
from jax.experimental import pallas as pl
from jax.experimental.pallas import tpu as pltpu
from jax.sharding import PartitionSpec as P


AXES = ("row", "col")
X, Y, Z, CORES = 4, 4, 16, 2
NT = (((1,), (1,)), ((), ()))
NN = (((1,), (0,)), ((), ()))


def device(x, y, z, k):
    return ((z % Z) * CORES + k) * (X * Y) + (x % X) * Y + y % Y


def pairs(move):
    out = []
    for x in range(X):
        for y in range(Y):
            for z in range(Z):
                for k in range(CORES):
                    out.append((device(x, y, z, k), device(*move(x, y, z, k))))
    return out


STEPS = {
    8: (0, 0),
    7: (1, 0), 9: (3, 0), 6: (0, 1), 10: (0, 3),
    5: (1, 1), 11: (1, 3), 4: (3, 1), 12: (3, 3), 3: (2, 0), 13: (0, 2),
    2: (2, 1), 14: (2, 3), 1: (1, 2), 15: (3, 2),
    0: (2, 2),
}
PLACES = {place: step for step, place in STEPS.items()}


def table(axis):
    bits = sum(STEPS[step][axis] << (2 * step) for step in range(Z))
    return bits - (1 << 32) if bits >> 31 else bits


TABLE_X, TABLE_Y = table(0), table(1)


def transpose_move(x, y, z, k):
    cx, cy = z // Y, z % Y
    return cx, cy, z + PLACES[(x - cx) % X, (y - cy) % Y], k


TRANSPOSE = pairs(transpose_move)
SWAP = pairs(lambda x, y, z, k: (x, y, z, 1 - k))
PM2 = pairs(lambda x, y, z, k: (x, y, z + 2 if k == 0 else z - 2, k))


def shift(d):
    return pairs(lambda x, y, z, k: (x, y, z + d, k))


def send(array, moves):
    return lax.ppermute(array, AXES, moves)


def split(x):
    high = x.astype(jnp.bfloat16)
    return high, (x - high.astype(jnp.float32)).astype(jnp.bfloat16)


def dot3(a, b, dims):
    ah, al = a
    bh, bl = b
    dot = lambda u, v: lax.dot_general(u, v, dims, preferred_element_type=jnp.float32)
    return dot(ah, bh) + (dot(ah, bl) + dot(al, bh))


def pack_body(chunk, fold, out):
    for j in range(4):
        out[32 * j:32 * j + 32, :] = chunk[:, 128 * j:128 * j + 128]
    out[128:136, 0:64] = fold[0:8, :]
    out[128:136, 64:128] = fold[8:16, :]


def weight_body(gathered, other, out_high, out_low, rows, inv, sems):
    k = lax.axis_index("row") % 2
    copies = [
        pltpu.make_async_copy(gathered.at[:, 0:32, :], rows, sems.at[0]),
        pltpu.make_async_copy(gathered.at[:, 32:48, :], inv.at[:, k], sems.at[1]),
        pltpu.make_async_copy(other, inv.at[:, 1 - k], sems.at[2]),
    ]
    for copy in copies:
        copy.start()
    for copy in copies:
        copy.wait()
    inverse = split(inv[...].reshape(512, 512))
    solved = dot3(split(rows[...].reshape(512, 512)), inverse, NN)
    high, low = split(dot3(split(solved), inverse, NT))
    out_high[...] = high
    out_low[...] = low


OFFSETS = (0, -4, 4, 8)


def where_am_i():
    row = lax.axis_index("row")
    return row, lax.axis_index("col"), row // 2, row % 2


def place(ref, group, core, z, col, high, low, fold):
    for slot in range(4):
        step = OFFSETS[slot]
        far = (0, -1, 1)[group] + step if group < 3 else step - 2 + 4 * core
        at = (z + far + 32) & 15
        hop = 2 * ((at - col) & 15)
        px = (col // 4 + (jnp.int32(TABLE_X) >> hop)) & 3
        py = (col + (jnp.int32(TABLE_Y) >> hop)) & 3
        rows = pl.ds(pl.multiple_of(32 * (4 * px + py), 32), 32)
        start = 544 * group + 136 * slot
        for j in range(4):
            h, l = split(ref[start + 32 * j:start + 32 * j + 32, :])
            high[rows, 128 * j:128 * j + 128] = h
            low[rows, 128 * j:128 * j + 128] = l
        tile = ref[start + 128:start + 136, :]
        first = pl.multiple_of(16 * (2 * at + core), 16)
        fold[pl.ds(first, 8), :] = tile
        fold[pl.ds(first + 8, 8), :] = pltpu.roll(tile, 64, 1)


def join_body(a, b, c, after, out, sems):
    copies = [pltpu.make_async_copy(ref, out.at[544 * i:544 * i + 544, :], sems.at[i]) for i, ref in enumerate((a, b, c))]
    for copy in copies:
        copy.start()
    for copy in copies:
        copy.wait()


def update(half, w, cols, vin, vout, out, sems, row, col):
    lower = 2 * col + half <= row
    copies = []
    for n in range(2):
        part = slice(256 * n, 256 * n + 256)

        @pl.when(lower)
        def _():
            block = tuple(c[part, :] for c in cols)
            vout[:, part] = vin[:, part] - dot3(w, block, NT)

        @pl.when(jnp.logical_not(lower))
        def _():
            vout[:, part] = vin[:, part]

        span = pl.ds(pl.multiple_of(512 * half + 256 * n, 256), 256)
        copy = pltpu.make_async_copy(vout.at[:, part], out.at[:, span], sems.at[n])
        copy.start()
        copies.append(copy)
    return copies


def begin(copies):
    for copy in copies:
        copy.start()


def end(copies):
    for copy in copies:
        copy.wait()


def first_body(w_high, w_low, mine0, mine1, mine2, mine3, trailing, out, fold, stage, high, low, wh, wl, vin, vout, sems):
    row, col, z, k = where_am_i()
    span = pl.ds(pl.multiple_of(512 * k, 512), 512)
    loads = [
        pltpu.make_async_copy(ref, stage.at[544 * i:544 * i + 544, :], sems.at[i])
        for i, ref in enumerate((mine0, mine1, mine2, mine3))
    ]
    weights = [pltpu.make_async_copy(w_high, wh, sems.at[4]), pltpu.make_async_copy(w_low, wl, sems.at[5])]
    old = [pltpu.make_async_copy(trailing.at[:, span], vin, sems.at[6])]
    begin(loads + weights + old)
    for group in range(4):
        end(loads[group:group + 1])
        place(stage, group, k, z, col, high, low, fold)
    end(weights + old)
    end(update(k, (wh[...], wl[...]), (high, low), vin, vout, out, sems.at[7:9], row, col))


def second_body(w_high, w_low, other0, others, trailing, part, half_fold, series, length, out, out_s,
                stage, high, low, wh, wl, vin, vout, fold, vs, vsout, sems):
    row, col, z, k = where_am_i()
    span = pl.ds(pl.multiple_of(512 * (1 - k), 512), 512)
    loads = [
        pltpu.make_async_copy(half_fold, fold, sems.at[0]),
        pltpu.make_async_copy(other0, stage.at[0:544, :], sems.at[1]),
        pltpu.make_async_copy(others, stage.at[544:2176, :], sems.at[2]),
    ]
    weights = [pltpu.make_async_copy(w_high, wh, sems.at[3]), pltpu.make_async_copy(w_low, wl, sems.at[4])]
    old = [pltpu.make_async_copy(trailing.at[:, span], vin, sems.at[5]), pltpu.make_async_copy(series, vs, sems.at[6])]
    begin(loads + weights + old)
    end(loads[0:2])
    place(stage, 0, 1 - k, z, col, high, low, fold)
    end(loads[2:3])
    for group in range(1, 4):
        place(stage, group, 1 - k, z, col, high, low, fold)
    end(weights + old)
    w = (wh[...], wl[...])
    writes = update(1 - k, w, (high, low), vin, vout, out, sems.at[7:9], row, col)
    correction = dot3(w, split(fold[...]), NN)
    correction = jnp.where(row < length[...], correction, 0.0)
    vsout[...] = vs[...] - correction.T[0:64, :]
    last = pltpu.make_async_copy(vsout, out_s, sems.at[9])
    begin([last])
    end(writes + [last])


def spread_body(panel, stripe, out, sems):
    k = lax.axis_index("row") % 2
    half = stripe.at[pl.ds(pl.multiple_of(16 * k, 16), 16), :]
    copies = []
    for c in range(16):
        copies.append(pltpu.make_async_copy(panel, out.at[c, 0:32, :], sems.at[2 * c]))
        copies.append(pltpu.make_async_copy(half, out.at[c, 32:48, :], sems.at[2 * c + 1]))
    begin(copies)
    end(copies)


VMEM = pl.BlockSpec(memory_space=pltpu.VMEM)
ANY = pl.BlockSpec(memory_space=pl.ANY)


def shape(*dims, dtype=jnp.float32):
    return jax.ShapeDtypeStruct(dims, dtype)


def kernel(body, out, memory, outs, scratch=(), alias=None):
    specs = {"v": VMEM, "a": ANY}
    out_specs = tuple(specs[m] for m in outs) if len(outs) > 1 else specs[outs]

    def call(*args):
        return pl.pallas_call(
            body,
            out_shape=out,
            in_specs=[specs[m] for m in memory],
            out_specs=out_specs,
            scratch_shapes=list(scratch),
            input_output_aliases=alias or {},
        )(*args)

    return call


def block(*dims, dtype=jnp.float32):
    return pltpu.VMEM(dims, dtype)


def sems(n):
    return pltpu.SemaphoreType.DMA((n,))


def step(trailing, panel, inv_factor, later_series, fold_series, fold_len):
    half = jnp.bfloat16
    chunk = send(panel, TRANSPOSE)
    load = kernel(spread_body, shape(16, 48, 512), "aa", "a", [sems(32)])(panel, inv_factor.T)
    gathered = lax.all_to_all(load, "col", 0, 0, tiled=True)
    packed = kernel(pack_body, shape(136, 128), "vv", "v")(chunk, fold_series)
    far = [packed] + [send(packed, shift(d)) for d in (4, -4, 8)]
    near = jnp.concatenate(far, 0)
    mine = [send(near, shift(1)), send(near, shift(-1)), send(near, PM2)]
    other0 = send(near, SWAP)
    other = send(gathered[:, 32:, :], SWAP)
    weight = kernel(
        weight_body,
        (shape(512, 512, dtype=half), shape(512, 512, dtype=half)),
        "aa",
        "vv",
        [block(16, 32, 512), block(16, 2, 16, 512), sems(3)],
    )(gathered, other)
    joined = kernel(join_body, shape(1632, 128), "aaaa", "a", [sems(3)])(*mine, weight[0])
    others = send(joined, SWAP)
    square = block(512, 512, dtype=half)
    work = [block(2176, 128), square, square, square, square, block(512, 512), block(512, 512)]
    part, half_fold = kernel(
        first_body, (shape(512, 1024), shape(512, 128)), "aaaaaaa", "av", work + [sems(9)]
    )(*weight, near, *mine, trailing)
    length = jnp.pad(fold_len, (0, 64))[None, :]
    out, series = kernel(
        second_body,
        (shape(512, 1024), shape(64, 512)),
        "aaaaaaaav",
        "aa",
        work + [block(512, 128), block(64, 512), block(64, 512), sems(10)],
        {5: 0},
    )(*weight, other0, others, trailing, part, half_fold, later_series.T, length)
    return out, series.T


def solution(mesh):
    in_specs = (
        P("row", "col"),
        P(("row", "col"), None),
        P(None, "col"),
        P("row", "col"),
        P("row", "col"),
        P("col"),
    )
    out_specs = (P("row", "col"), P("row", "col"))
    return jax.shard_map(step, mesh=mesh, in_specs=in_specs, out_specs=out_specs, check_vma=False)
```

time: 112 us -> 181 us (1.62)
  Pallas kernels: 17.5 us -> 91.4 us
  local copies, waits for them, and re-layouts: 7.79 us -> 2.86 us
    pallas_call x6, Pallas kernels: 17.5 us -> 91.4 us  [call(): pl.pallas_call(body, out_shape=out, in_specs=[specs[m] for m in memory],...]
    unnamed x26 -> x20, local copies, waits for them, and re-layouts: 7.75 us -> 2.31 us
  transfers between devices with their start and end apart: 11 -> 11, of which waited for: 4 -> 4; matrix products, arithmetic and copies ran while one was open for 1% -> 1% of each run, Pallas kernels for 8% -> 6%
where the time goes in v1:
time: 181 us; the launch traced here: 180 us
  Pallas kernels  91.4 us (50%)
  starting transfers between devices  73.3 us (40%)
  waiting for transfers between devices  10.8 us (6%)
  local copies, waits for them, and re-layouts  2.86 us (2%)
    pallas_call x6, Pallas kernels, call(): pl.pallas_call(body, out_shape=out, in_specs=[specs[m] for m in memory],...  91.4 us
    ppermute x10, starting transfers between devices, send(): return lax.ppermute(array, AXES, moves)  65.7 us
    all_to_all x1, starting transfers between devices, step(): gathered = lax.all_to_all(load, 'col', 0, 0, tiled=True)  7.58 us
    ppermute x10, waiting for transfers between devices, send(): return lax.ppermute(array, AXES, moves)  6.07 us
    all_to_all x1, waiting for transfers between devices, step(): gathered = lax.all_to_all(load, 'col', 0, 0, tiled=True)  4.71 us
  transfers between devices with their start and end apart: 11, of which 4 were waited for; matrix products, arithmetic and copies ran while one was open for 1% of the time, Pallas kernels for 6%

profile of v1, /device:TPU:1, one launch (start us, length us, event | category | flops | bytes accessed | tf_op | source)
XLA Modules:
  0.0 180.1 jit_solution(15806743306180044741)
XLA Ops:
  0.6 49.0 %shard_map.77 = f32[16,48,512]{2,1,0:T(8,128)} custom-call(f32[32,512]{1,0:T(8,128)} %panel.1, f32[32,512]{1,0:T(8,128)} %bitcast.6), custom_call_target="tpu_custom_call" | custom-call | tf_op jit(solution)/shard_map/pallas_call | solution.py:239
  49.7 7.6 %all-to-all-start = ((f32[16,48,512]{2,1,0:T(8,128)}), f32[16,48,512]{2,1,0:T(8,128)S(1)}, u32[]{:S(2)}, u32[]{:S(2)}) async-start(f32[16,48,512]{2,1,0:T(8,128)} %shard_map.77), calls=%async_computation | async-start | bytes 3145728 | tf_op jit(solution)/shard_map/all_to_all | solution.py:263
  57.3 15.4 %collective-permute-start.1 = (f32[32,512]{1,0:T(8,128)S(1)}, f32[32,512]{1,0:T(8,128)S(1)}, u32[]{:S(2)}, u32[]{:S(2)}) collective-permute-start(f32[32,512]{1,0:T(8,128)S(1)} %copy-done.8), channel_id=1, source_target_pairs={{0,256},{16,272},{32,353},{48,369},{64,482},{80,498},{96,291},{112... | collective-permute-start | bytes 196616 | tf_op jit(solution)/shard_map/ppermute | solution.py:62
  72.7 4.7 %all-to-all-done.gathered = f32[16,48,512]{2,1,0:T(8,128)S(1)} async-done(((f32[16,48,512]{2,1,0:T(8,128)}), f32[16,48,512]{2,1,0:T(8,128)S(1)}, u32[]{:S(2)}, u32[]{:S(2)}) %all-to-all-start) | async-done | bytes 1572896 | tf_op jit(solution)/shard_map/all_to_all | solution.py:263
  77.5 7.1 %collective-permute-start = (f32[16,16,512]{2,1,0:T(8,128)S(1)}, f32[16,16,512]{2,1,0:T(8,128)}, u32[]{:S(2)}, u32[]{:S(2)}) collective-permute-start(f32[16,16,512]{2,1,0:T(8,128)S(1)} %slice.4), channel_id=1, source_target_pairs={{0,16},{16,0},{32,48},{48,32},{64,80},{80,64},{96,112},{112,96},{1... | collective-permute-start | bytes 1572872 | tf_op jit(solution)/shard_map/ppermute | solution.py:62
  85.2 1.5 shard_map.79
  86.7 14.8 %collective-permute-start.4 = (f32[136,128]{1,0:T(8,128)}, f32[136,128]{1,0:T(8,128)S(1)}, u32[]{:S(2)}, u32[]{:S(2)}) collective-permute-start(f32[136,128]{1,0:T(8,128)} %shard_map.79), channel_id=1, source_target_pairs={{0,256},{16,272},{32,288},{48,304},{64,320},{80,336},{96,352},{112... | collective-permute-start | bytes 208904 | tf_op jit(solution)/shard_map/ppermute | solution.py:62
  101.6 1.9 %collective-permute-start.3 = (f32[136,128]{1,0:T(8,128)}, f32[136,128]{1,0:T(8,128)S(1)}, u32[]{:S(2)}, u32[]{:S(2)}) collective-permute-start(f32[136,128]{1,0:T(8,128)} %shard_map.79), channel_id=1, source_target_pairs={{0,384},{16,400},{32,416},{48,432},{64,448},{80,464},{96,480},{112... | collective-permute-start | bytes 208904 | tf_op jit(solution)/shard_map/ppermute | solution.py:62
  103.5 7.3 %collective-permute-start.2 = (f32[136,128]{1,0:T(8,128)}, f32[136,128]{1,0:T(8,128)S(1)}, u32[]{:S(2)}, u32[]{:S(2)}) collective-permute-start(f32[136,128]{1,0:T(8,128)} %shard_map.79), channel_id=1, source_target_pairs={{0,128},{16,144},{32,160},{48,176},{64,192},{80,208},{96,224},{112... | collective-permute-start | bytes 208904 | tf_op jit(solution)/shard_map/ppermute | solution.py:62
  110.8 2.4 %collective-permute-done.3 = f32[136,128]{1,0:T(8,128)S(1)} collective-permute-done((f32[136,128]{1,0:T(8,128)}, f32[136,128]{1,0:T(8,128)S(1)}, u32[]{:S(2)}, u32[]{:S(2)}) %collective-permute-start.3) | collective-permute-done | bytes 69664 | tf_op jit(solution)/shard_map/ppermute | solution.py:62
  113.2 0.9 pad_maximum_fusion.mine0
  114.2 8.0 %collective-permute-start.8 = (f32[544,128]{1,0:T(8,128)S(1)}, f32[544,128]{1,0:T(8,128)S(1)}, u32[]{:S(2)}, u32[]{:S(2)}) collective-permute-start(f32[544,128]{1,0:T(8,128)S(1)} %pad_maximum_fusion.mine0), channel_id=1, source_target_pairs={{0,64},{16,464},{32,96},{48,496},{64,128},{80,16},{96,160},{112,48... | collective-permute-start | bytes 835592 | tf_op jit(solution)/shard_map/ppermute | solution.py:62
  122.2 2.8 %collective-permute-start.7 = (f32[544,128]{1,0:T(8,128)S(1)}, f32[544,128]{1,0:T(8,128)S(1)}, u32[]{:S(2)}, u32[]{:S(2)}) collective-permute-start(f32[544,128]{1,0:T(8,128)S(1)} %pad_maximum_fusion.mine0), channel_id=1, source_target_pairs={{0,480},{16,496},{32,0},{48,16},{64,32},{80,48},{96,64},{112,80},{... | collective-permute-start | bytes 835592 | tf_op jit(solution)/shard_map/ppermute | solution.py:62
  125.0 3.1 %collective-permute-start.6 = (f32[544,128]{1,0:T(8,128)S(1)}, f32[544,128]{1,0:T(8,128)S(1)}, u32[]{:S(2)}, u32[]{:S(2)}) collective-permute-start(f32[544,128]{1,0:T(8,128)S(1)} %pad_maximum_fusion.mine0), channel_id=1, source_target_pairs={{0,32},{16,48},{32,64},{48,80},{64,96},{80,112},{96,128},{112,144}... | collective-permute-start | bytes 835592 | tf_op jit(solution)/shard_map/ppermute | solution.py:62
  128.1 4.3 %shard_map.78 = (bf16[512,512]{1,0:T(8,128)(2,1)}, bf16[512,512]{1,0:T(8,128)(2,1)}) custom-call(f32[16,48,512]{2,1,0:T(8,128)} %copy-done, f32[16,16,512]{2,1,0:T(8,128)} %collective-permute-done.other), custom_call_target="tpu_custom_call" | custom-call | tf_op jit(solution)/shard_map/pallas_call | solution.py:239
  132.5 2.1 %collective-permute-done.7.b.mine2 = f32[544,128]{1,0:T(8,128)S(1)} collective-permute-done((f32[544,128]{1,0:T(8,128)S(1)}, f32[544,128]{1,0:T(8,128)S(1)}, u32[]{:S(2)}, u32[]{:S(2)}) %collective-permute-start.7) | collective-permute-done | bytes 278560 | tf_op jit(solution)/shard_map/ppermute | solution.py:62
  134.6 1.5 collective-permute-done.6.a.mine1
  136.1 0.7 copy-done.3
  136.8 26.4 %shard_map.80 = f32[1632,128]{1,0:T(8,128)} custom-call(f32[544,128]{1,0:T(8,128)} %copy-done.3, f32[544,128]{1,0:T(8,128)} %copy-done.2, f32[544,128]{1,0:T(8,128)} %copy-done.1, bf16[512,512]{1,0:T(8,128)(2,1)} %get-tuple-element.8.after.w_high), custom_call_target="tpu_custom_call" | custom-call | tf_op jit(solution)/shard_map/pallas_call | solution.py:239
  163.3 3.4 %collective-permute-start.9 = (f32[1632,128]{1,0:T(8,128)}, f32[1632,128]{1,0:T(8,128)S(1)}, u32[]{:S(2)}, u32[]{:S(2)}) collective-permute-start(f32[1632,128]{1,0:T(8,128)} %shard_map.80), channel_id=1, source_target_pairs={{0,16},{16,0},{32,48},{48,32},{64,80},{80,64},{96,112},{112,96},{1... | collective-permute-start | bytes 2506760 | tf_op jit(solution)/shard_map/ppermute | solution.py:62
  166.7 1.9 %collective-permute-start.5 = (f32[544,128]{1,0:T(8,128)S(1)}, f32[544,128]{1,0:T(8,128)S(1)}, u32[]{:S(2)}, u32[]{:S(2)}) collective-permute-start(f32[544,128]{1,0:T(8,128)S(1)} %pad_maximum_fusion.mine0), channel_id=1, source_target_pairs={{0,16},{16,0},{32,48},{48,32},{64,80},{80,64},{96,112},{112,96},{1... | collective-permute-start | bytes 835592 | tf_op jit(solution)/shard_map/ppermute | solution.py:62
  169.1 4.8 %shard_map.81 = (f32[512,1024]{1,0:T(8,128)}, f32[512,128]{1,0:T(8,128)}) custom-call(bf16[512,512]{1,0:T(8,128)(2,1)} %get-tuple-element.8.after.w_high, bf16[512,512]{1,0:T(8,128)(2,1)} %get-tuple-element.9.w_low, f32[544,128]{1,0:T(8,128)} %copy-done.4, f32[544,128]{1,0:T(8,128)} %copy-done.3, f32[544,128]{1,0:T(8,128)} %copy-done.2, ...), custom_call_target="tpu_custom_call" | custom-call | tf_op jit(solution)/shard_map/pallas_call | solution.py:239
  173.9 0.7 copy-done.6
  174.9 5.2 %shard_map.82 = (f32[512,1024]{1,0:T(8,128)}, f32[64,512]{1,0:T(8,128)}) custom-call(bf16[512,512]{1,0:T(8,128)(2,1)} %get-tuple-element.8.after.w_high, bf16[512,512]{1,0:T(8,128)(2,1)} %get-tuple-element.9.w_low, f32[544,128]{1,0:T(8,128)} %copy-done.6, f32[1632,128]{1,0:T(8,128)} %copy-done.5, ...), custom_call_target="tpu_custom_call", output_to_operand_aliasing={{0}: (5, {})} | custom-call | tf_op jit(solution)/shard_map/pallas_call | solution.py:239
  (27 shorter events, 1.5 us)
Async XLA Ops:
  0.6 56.6 %copy-start.8 = (f32[32,512]{1,0:T(8,128)S(1)}, f32[32,512]{1,0:T(8,128)}, u32[]{:S(2)}) copy-start(f32[32,512]{1,0:T(8,128)} %panel.1) | copy-start | bytes 196612
  49.7 27.8 %all-to-all-start = ((f32[16,48,512]{2,1,0:T(8,128)}), f32[16,48,512]{2,1,0:T(8,128)S(1)}, u32[]{:S(2)}, u32[]{:S(2)}) async-start(f32[16,48,512]{2,1,0:T(8,128)} %shard_map.77), calls=%async_computation | async-start | bytes 3145728 | tf_op jit(solution)/shard_map/all_to_all | solution.py:263
  57.3 27.3 %collective-permute-start.1 = (f32[32,512]{1,0:T(8,128)S(1)}, f32[32,512]{1,0:T(8,128)S(1)}, u32[]{:S(2)}, u32[]{:S(2)}) collective-permute-start(f32[32,512]{1,0:T(8,128)S(1)} %copy-done.8), channel_id=1, source_target_pairs={{0,256},{16,272},{32,353},{48,369},{64,482},{80,498},{96,291},{112... | collective-permute-start | bytes 196616 | tf_op jit(solution)/shard_map/ppermute | solution.py:62
  77.4 50.7 %copy-start = (f32[16,48,512]{2,1,0:T(8,128)}, f32[16,48,512]{2,1,0:T(8,128)S(1)}, u32[]{:S(2)}) copy-start(f32[16,48,512]{2,1,0:T(8,128)S(1)} %all-to-all-done.gathered) | copy-start | bytes 4718596
  77.5 50.6 %collective-permute-start = (f32[16,16,512]{2,1,0:T(8,128)S(1)}, f32[16,16,512]{2,1,0:T(8,128)}, u32[]{:S(2)}, u32[]{:S(2)}) collective-permute-start(f32[16,16,512]{2,1,0:T(8,128)S(1)} %slice.4), channel_id=1, source_target_pairs={{0,16},{16,0},{32,48},{48,32},{64,80},{80,64},{96,112},{112,96},{1... | collective-permute-start | bytes 1572872 | tf_op jit(solution)/shard_map/ppermute | solution.py:62
  84.6 0.6 copy-start.7
  86.7 24.1 %collective-permute-start.4 = (f32[136,128]{1,0:T(8,128)}, f32[136,128]{1,0:T(8,128)S(1)}, u32[]{:S(2)}, u32[]{:S(2)}) collective-permute-start(f32[136,128]{1,0:T(8,128)} %shard_map.79), channel_id=1, source_target_pairs={{0,256},{16,272},{32,288},{48,304},{64,320},{80,336},{96,352},{112... | collective-permute-start | bytes 208904 | tf_op jit(solution)/shard_map/ppermute | solution.py:62
  101.6 11.6 %collective-permute-start.3 = (f32[136,128]{1,0:T(8,128)}, f32[136,128]{1,0:T(8,128)S(1)}, u32[]{:S(2)}, u32[]{:S(2)}) collective-permute-start(f32[136,128]{1,0:T(8,128)} %shard_map.79), channel_id=1, source_target_pairs={{0,384},{16,400},{32,416},{48,432},{64,448},{80,464},{96,480},{112... | collective-permute-start | bytes 208904 | tf_op jit(solution)/shard_map/ppermute | solution.py:62
  103.5 9.7 %collective-permute-start.2 = (f32[136,128]{1,0:T(8,128)}, f32[136,128]{1,0:T(8,128)S(1)}, u32[]{:S(2)}, u32[]{:S(2)}) collective-permute-start(f32[136,128]{1,0:T(8,128)} %shard_map.79), channel_id=1, source_target_pairs={{0,128},{16,144},{32,160},{48,176},{64,192},{80,208},{96,224},{112... | collective-permute-start | bytes 208904 | tf_op jit(solution)/shard_map/ppermute | solution.py:62
  114.2 52.5 %copy-start.4 = (f32[544,128]{1,0:T(8,128)}, f32[544,128]{1,0:T(8,128)S(1)}, u32[]{:S(2)}) copy-start(f32[544,128]{1,0:T(8,128)S(1)} %pad_maximum_fusion.mine0) | copy-start | bytes 835588
  114.2 54.4 %copy-start.9 = (s32[64]{0:T(128)S(1)}, s32[64]{0:T(128)}, u32[]{:S(2)}) copy-start(s32[64]{0:T(128)} %param.11) | copy-start | bytes 772
  114.2 18.3 %collective-permute-start.8 = (f32[544,128]{1,0:T(8,128)S(1)}, f32[544,128]{1,0:T(8,128)S(1)}, u32[]{:S(2)}, u32[]{:S(2)}) collective-permute-start(f32[544,128]{1,0:T(8,128)S(1)} %pad_maximum_fusion.mine0), channel_id=1, source_target_pairs={{0,64},{16,464},{32,96},{48,496},{64,128},{80,16},{96,160},{112,48... | collective-permute-start | bytes 835592 | tf_op jit(solution)/shard_map/ppermute | solution.py:62
  122.2 12.4 %collective-permute-start.7 = (f32[544,128]{1,0:T(8,128)S(1)}, f32[544,128]{1,0:T(8,128)S(1)}, u32[]{:S(2)}, u32[]{:S(2)}) collective-permute-start(f32[544,128]{1,0:T(8,128)S(1)} %pad_maximum_fusion.mine0), channel_id=1, source_target_pairs={{0,480},{16,496},{32,0},{48,16},{64,32},{80,48},{96,64},{112,80},{... | collective-permute-start | bytes 835592 | tf_op jit(solution)/shard_map/ppermute | solution.py:62
  125.0 11.1 %collective-permute-start.6 = (f32[544,128]{1,0:T(8,128)S(1)}, f32[544,128]{1,0:T(8,128)S(1)}, u32[]{:S(2)}, u32[]{:S(2)}) collective-permute-start(f32[544,128]{1,0:T(8,128)S(1)} %pad_maximum_fusion.mine0), channel_id=1, source_target_pairs={{0,32},{16,48},{32,64},{48,80},{64,96},{80,112},{96,128},{112,144}... | collective-permute-start | bytes 835592 | tf_op jit(solution)/shard_map/ppermute | solution.py:62
  132.5 3.6 %copy-start.1 = (f32[544,128]{1,0:T(8,128)}, f32[544,128]{1,0:T(8,128)S(1)}, u32[]{:S(2)}) copy-start(f32[544,128]{1,0:T(8,128)S(1)} %collective-permute-done.8.c.mine3) | copy-start | bytes 835588
  134.6 1.5 copy-start.2
  136.1 0.7 copy-start.3
  163.3 10.6 %collective-permute-start.9 = (f32[1632,128]{1,0:T(8,128)}, f32[1632,128]{1,0:T(8,128)S(1)}, u32[]{:S(2)}, u32[]{:S(2)}) collective-permute-start(f32[1632,128]{1,0:T(8,128)} %shard_map.80), channel_id=1, source_target_pairs={{0,16},{16,0},{32,48},{48,32},{64,80},{80,64},{96,112},{112,96},{1... | collective-permute-start | bytes 2506760 | tf_op jit(solution)/shard_map/ppermute | solution.py:62
  166.7 7.2 %collective-permute-start.5 = (f32[544,128]{1,0:T(8,128)S(1)}, f32[544,128]{1,0:T(8,128)S(1)}, u32[]{:S(2)}, u32[]{:S(2)}) collective-permute-start(f32[544,128]{1,0:T(8,128)S(1)} %pad_maximum_fusion.mine0), channel_id=1, source_target_pairs={{0,16},{16,0},{32,48},{48,32},{64,80},{80,64},{96,112},{112,96},{1... | collective-permute-start | bytes 835592 | tf_op jit(solution)/shard_map/ppermute | solution.py:62
  173.9 0.7 copy-start.6
  173.9 1.0 copy-start.5

commit v2 on v1

--- a/solution.py
+++ b/solution.py
@@ -127,14 +127,6 @@
         fold[pl.ds(first + 8, 8), :] = pltpu.roll(tile, 64, 1)
 
 
-def join_body(a, b, c, after, out, sems):
-    copies = [pltpu.make_async_copy(ref, out.at[544 * i:544 * i + 544, :], sems.at[i]) for i, ref in enumerate((a, b, c))]
-    for copy in copies:
-        copy.start()
-    for copy in copies:
-        copy.wait()
-
-
 def update(half, w, cols, vin, vout, out, sems, row, col):
     lower = 2 * col + half <= row
     copies = []
@@ -205,20 +197,23 @@
     w = (wh[...], wl[...])
     writes = update(1 - k, w, (high, low), vin, vout, out, sems.at[7:9], row, col)
     correction = dot3(w, split(fold[...]), NN)
-    correction = jnp.where(row < length[...], correction, 0.0)
+    lengths = jnp.concatenate([length[...], length[...]], 1)
+    correction = jnp.where(row < lengths, correction, 0.0)
     vsout[...] = vs[...] - correction.T[0:64, :]
     last = pltpu.make_async_copy(vsout, out_s, sems.at[9])
     begin([last])
     end(writes + [last])
 
 
-def spread_body(panel, stripe, out, sems):
+def spread_body(panel, stripe, out, stage, sems):
     k = lax.axis_index("row") % 2
-    half = stripe.at[pl.ds(pl.multiple_of(16 * k, 16), 16), :]
-    copies = []
-    for c in range(16):
-        copies.append(pltpu.make_async_copy(panel, out.at[c, 0:32, :], sems.at[2 * c]))
-        copies.append(pltpu.make_async_copy(half, out.at[c, 32:48, :], sems.at[2 * c + 1]))
+    loads = [
+        pltpu.make_async_copy(panel, stage.at[0:32, :], sems.at[16]),
+        pltpu.make_async_copy(stripe.at[pl.ds(pl.multiple_of(16 * k, 16), 16), :], stage.at[32:48, :], sems.at[17]),
+    ]
+    begin(loads)
+    end(loads)
+    copies = [pltpu.make_async_copy(stage, out.at[c], sems.at[c]) for c in range(16)]
     begin(copies)
     end(copies)
 
@@ -259,7 +254,7 @@
 def step(trailing, panel, inv_factor, later_series, fold_series, fold_len):
     half = jnp.bfloat16
     chunk = send(panel, TRANSPOSE)
-    load = kernel(spread_body, shape(16, 48, 512), "aa", "a", [sems(32)])(panel, inv_factor.T)
+    load = kernel(spread_body, shape(16, 48, 512), "aa", "a", [block(48, 512), sems(18)])(panel, inv_factor.T)
     gathered = lax.all_to_all(load, "col", 0, 0, tiled=True)
     packed = kernel(pack_body, shape(136, 128), "vv", "v")(chunk, fold_series)
     far = [packed] + [send(packed, shift(d)) for d in (4, -4, 8)]
@@ -274,14 +269,12 @@
         "vv",
         [block(16, 32, 512), block(16, 2, 16, 512), sems(3)],
     )(gathered, other)
-    joined = kernel(join_body, shape(1632, 128), "aaaa", "a", [sems(3)])(*mine, weight[0])
-    others = send(joined, SWAP)
+    others = send(jnp.concatenate(mine, 0), SWAP)
     square = block(512, 512, dtype=half)
     work = [block(2176, 128), square, square, square, square, block(512, 512), block(512, 512)]
     part, half_fold = kernel(
         first_body, (shape(512, 1024), shape(512, 128)), "aaaaaaa", "av", work + [sems(9)]
     )(*weight, near, *mine, trailing)
-    length = jnp.pad(fold_len, (0, 64))[None, :]
     out, series = kernel(
         second_body,
         (shape(512, 1024), shape(64, 512)),
@@ -289,7 +282,7 @@
         "aa",
         work + [block(512, 128), block(64, 512), block(64, 512), sems(10)],
         {5: 0},
-    )(*weight, other0, others, trailing, part, half_fold, later_series.T, length)
+    )(*weight, other0, others, trailing, part, half_fold, later_series.T, fold_len[None, :])
     return out, series.T
 
 

time: 181 us -> 104 us (0.57)
  the two profiles are of different devices: /device:TPU:1 before, /device:TPU:13 now
where the time goes in v2:
time: 104 us; the launch traced here: 103 us
  starting transfers between devices  59.6 us (57%)
  waiting for transfers between devices  24.9 us (24%)
  Pallas kernels  16 us (15%)
    ppermute x10, starting transfers between devices, send(): return lax.ppermute(array, AXES, moves)  52.8 us
    ppermute x10, waiting for transfers between devices, send(): return lax.ppermute(array, AXES, moves)  24.9 us
    pallas_call x5, Pallas kernels, call(): pl.pallas_call(body, out_shape=out, in_specs=[specs[m] for m in memory],...  16 us
    all_to_all x1, starting transfers between devices, step(): gathered = lax.all_to_all(load, 'col', 0, 0, tiled=True)  6.79 us
  transfers between devices with their start and end apart: 11, of which 4 were waited for; matrix products, arithmetic and copies ran while one was open for 1% of the time, Pallas kernels for 9%

profile of v2, /device:TPU:13, one launch (start us, length us, event | category | flops | bytes accessed | tf_op | source)
XLA Modules:
  0.0 103.0 jit_solution(13978185155791767505)
XLA Ops:
  0.6 2.2 %shard_map.77 = f32[16,48,512]{2,1,0:T(8,128)} custom-call(f32[32,512]{1,0:T(8,128)} %panel.1, f32[32,512]{1,0:T(8,128)} %bitcast.5), custom_call_target="tpu_custom_call" | custom-call | tf_op jit(solution)/shard_map/pallas_call | solution.py:234
  2.8 6.8 %all-to-all-start = ((f32[16,48,512]{2,1,0:T(8,128)}), f32[16,48,512]{2,1,0:T(8,128)S(1)}, u32[]{:S(2)}, u32[]{:S(2)}) async-start(f32[16,48,512]{2,1,0:T(8,128)} %shard_map.77), calls=%async_computation | async-start | bytes 3145728 | tf_op jit(solution)/shard_map/all_to_all | solution.py:258
  9.6 4.7 %collective-permute-start.1 = (f32[32,512]{1,0:T(8,128)S(1)}, f32[32,512]{1,0:T(8,128)S(1)}, u32[]{:S(2)}, u32[]{:S(2)}) collective-permute-start(f32[32,512]{1,0:T(8,128)S(1)} %copy-done.6), channel_id=1, source_target_pairs={{0,256},{16,272},{32,353},{48,369},{64,482},{80,498},{96,291},{112... | collective-permute-start | bytes 196616 | tf_op jit(solution)/shard_map/ppermute | solution.py:62
  14.4 12.6 %collective-permute-done.1.chunk = f32[32,512]{1,0:T(8,128)S(1)} collective-permute-done((f32[32,512]{1,0:T(8,128)S(1)}, f32[32,512]{1,0:T(8,128)S(1)}, u32[]{:S(2)}, u32[]{:S(2)}) %collective-permute-start.1) | collective-permute-done | bytes 65568 | tf_op jit(solution)/shard_map/ppermute | solution.py:62
  27.0 0.6 copy-done.5
  27.6 1.5 %shard_map.79 = f32[136,128]{1,0:T(8,128)} custom-call(f32[32,512]{1,0:T(8,128)} %copy-done.5, f32[16,64]{1,0:T(8,128)} %fold.1), custom_call_target="tpu_custom_call" | custom-call | tf_op jit(solution)/shard_map/pallas_call | solution.py:234
  29.1 7.7 %collective-permute-start.4 = (f32[136,128]{1,0:T(8,128)}, f32[136,128]{1,0:T(8,128)S(1)}, u32[]{:S(2)}, u32[]{:S(2)}) collective-permute-start(f32[136,128]{1,0:T(8,128)} %shard_map.79), channel_id=1, source_target_pairs={{0,256},{16,272},{32,288},{48,304},{64,320},{80,336},{96,352},{112... | collective-permute-start | bytes 208904 | tf_op jit(solution)/shard_map/ppermute | solution.py:62
  36.9 3.5 %collective-permute-start.3 = (f32[136,128]{1,0:T(8,128)}, f32[136,128]{1,0:T(8,128)S(1)}, u32[]{:S(2)}, u32[]{:S(2)}) collective-permute-start(f32[136,128]{1,0:T(8,128)} %shard_map.79), channel_id=1, source_target_pairs={{0,384},{16,400},{32,416},{48,432},{64,448},{80,464},{96,480},{112... | collective-permute-start | bytes 208904 | tf_op jit(solution)/shard_map/ppermute | solution.py:62
  40.4 5.7 %collective-permute-start.2 = (f32[136,128]{1,0:T(8,128)}, f32[136,128]{1,0:T(8,128)S(1)}, u32[]{:S(2)}, u32[]{:S(2)}) collective-permute-start(f32[136,128]{1,0:T(8,128)} %shard_map.79), channel_id=1, source_target_pairs={{0,128},{16,144},{32,160},{48,176},{64,192},{80,208},{96,224},{112... | collective-permute-start | bytes 208904 | tf_op jit(solution)/shard_map/ppermute | solution.py:62
  46.1 4.6 %collective-permute-done.3 = f32[136,128]{1,0:T(8,128)S(1)} collective-permute-done((f32[136,128]{1,0:T(8,128)}, f32[136,128]{1,0:T(8,128)S(1)}, u32[]{:S(2)}, u32[]{:S(2)}) %collective-permute-start.3) | collective-permute-done | bytes 69664 | tf_op jit(solution)/shard_map/ppermute | solution.py:62
  50.7 0.9 pad_maximum_fusion.1.mine0
  51.7 3.3 %collective-permute-start.8 = (f32[544,128]{1,0:T(8,128)S(1)}, f32[544,128]{1,0:T(8,128)S(1)}, u32[]{:S(2)}, u32[]{:S(2)}) collective-permute-start(f32[544,128]{1,0:T(8,128)S(1)} %pad_maximum_fusion.1.mine0), channel_id=1, source_target_pairs={{0,64},{16,464},{32,96},{48,496},{64,128},{80,16},{96,160},{112,48... | collective-permute-start | bytes 835592 | tf_op jit(solution)/shard_map/ppermute | solution.py:62
  55.0 11.1 %collective-permute-start.7 = (f32[544,128]{1,0:T(8,128)S(1)}, f32[544,128]{1,0:T(8,128)S(1)}, u32[]{:S(2)}, u32[]{:S(2)}) collective-permute-start(f32[544,128]{1,0:T(8,128)S(1)} %pad_maximum_fusion.1.mine0), channel_id=1, source_target_pairs={{0,480},{16,496},{32,0},{48,16},{64,32},{80,48},{96,64},{112,80},{... | collective-permute-start | bytes 835592 | tf_op jit(solution)/shard_map/ppermute | solution.py:62
  66.1 1.9 %collective-permute-start.6 = (f32[544,128]{1,0:T(8,128)S(1)}, f32[544,128]{1,0:T(8,128)S(1)}, u32[]{:S(2)}, u32[]{:S(2)}) collective-permute-start(f32[544,128]{1,0:T(8,128)S(1)} %pad_maximum_fusion.1.mine0), channel_id=1, source_target_pairs={{0,32},{16,48},{32,64},{48,80},{64,96},{80,112},{96,128},{112,144}... | collective-permute-start | bytes 835592 | tf_op jit(solution)/shard_map/ppermute | solution.py:62
  68.0 2.4 %collective-permute-done.7.mine2 = f32[544,128]{1,0:T(8,128)S(1)} collective-permute-done((f32[544,128]{1,0:T(8,128)S(1)}, f32[544,128]{1,0:T(8,128)S(1)}, u32[]{:S(2)}, u32[]{:S(2)}) %collective-permute-start.7) | collective-permute-done | bytes 278560 | tf_op jit(solution)/shard_map/ppermute | solution.py:62
  70.4 5.3 %collective-permute-done.6.mine1 = f32[544,128]{1,0:T(8,128)S(1)} collective-permute-done((f32[544,128]{1,0:T(8,128)S(1)}, f32[544,128]{1,0:T(8,128)S(1)}, u32[]{:S(2)}, u32[]{:S(2)}) %collective-permute-start.6) | collective-permute-done | bytes 278560 | tf_op jit(solution)/shard_map/ppermute | solution.py:62
  75.6 0.1 pad_maximum_fusion
  75.7 10.5 %collective-permute-start.9 = (f32[1632,128]{1,0:T(8,128)S(1)}, f32[1632,128]{1,0:T(8,128)}, u32[]{:S(2)}, u32[]{:S(2)}) collective-permute-start(f32[1632,128]{1,0:T(8,128)S(1)} %pad_maximum_fusion), channel_id=1, source_target_pairs={{0,16},{16,0},{32,48},{48,32},{64,80},{80,64},{96,112},{112,96},{1... | collective-permute-start | bytes 2506760 | tf_op jit(solution)/shard_map/ppermute | solution.py:62
  86.2 0.0 copy-start
  86.3 1.9 %collective-permute-start = (f32[16,16,512]{2,1,0:T(8,128)S(1)}, f32[16,16,512]{2,1,0:T(8,128)}, u32[]{:S(2)}, u32[]{:S(2)}) collective-permute-start(f32[16,16,512]{2,1,0:T(8,128)S(1)} %slice.4), channel_id=1, source_target_pairs={{0,16},{16,0},{32,48},{48,32},{64,80},{80,64},{96,112},{112,96},{1... | collective-permute-start | bytes 1572872 | tf_op jit(solution)/shard_map/ppermute | solution.py:62
  88.2 2.4 %collective-permute-start.5 = (f32[544,128]{1,0:T(8,128)S(1)}, f32[544,128]{1,0:T(8,128)}, u32[]{:S(2)}, u32[]{:S(2)}) collective-permute-start(f32[544,128]{1,0:T(8,128)S(1)} %pad_maximum_fusion.1.mine0), channel_id=1, source_target_pairs={{0,16},{16,0},{32,48},{48,32},{64,80},{80,64},{96,112},{112,96},{1... | collective-permute-start | bytes 835592 | tf_op jit(solution)/shard_map/ppermute | solution.py:62
  90.7 4.4 %shard_map.78 = (bf16[512,512]{1,0:T(8,128)(2,1)}, bf16[512,512]{1,0:T(8,128)(2,1)}) custom-call(f32[16,48,512]{2,1,0:T(8,128)} %copy-done, f32[16,16,512]{2,1,0:T(8,128)} %collective-permute-done.other), custom_call_target="tpu_custom_call" | custom-call | tf_op jit(solution)/shard_map/pallas_call | solution.py:234
  95.1 3.7 %shard_map.80 = (f32[512,1024]{1,0:T(8,128)}, f32[512,128]{1,0:T(8,128)}) custom-call(bf16[512,512]{1,0:T(8,128)(2,1)} %get-tuple-element.8.w_high, bf16[512,512]{1,0:T(8,128)(2,1)} %get-tuple-element.9.w_low, f32[544,128]{1,0:T(8,128)} %copy-done.4, f32[544,128]{1,0:T(8,128)} %copy-done.3, f32[544,128]{1,0:T(8,128)} %copy-done.2, f32[544,128]{1,0:T(8,128)} %copy-done.1, ...), custom_call_target="tpu_custom_call" | custom-call | tf_op jit(solution)/shard_map/pallas_call | solution.py:234
  98.8 4.1 %shard_map.81 = (f32[512,1024]{1,0:T(8,128)}, f32[64,512]{1,0:T(8,128)}) custom-call(bf16[512,512]{1,0:T(8,128)(2,1)} %get-tuple-element.8.w_high, bf16[512,512]{1,0:T(8,128)(2,1)} %get-tuple-element.9.w_low, f32[544,128]{1,0:T(8,128)} %collective-permute-done.5.other0, f32[1632,128]{1,0:T(8,128)} %collective-permute-done.9.others, ...), custom_call_target="tpu_custom_call", output_to_operand_aliasing={{0}: (5, {})} | custom-call | tf_op jit(solution)/shard_map/pallas_call | solution.py:234
  (20 shorter events, 0.1 us)
Async XLA Ops:
  0.6 9.0 %copy-start.6 = (f32[32,512]{1,0:T(8,128)S(1)}, f32[32,512]{1,0:T(8,128)}, u32[]{:S(2)}) copy-start(f32[32,512]{1,0:T(8,128)} %panel.1) | copy-start | bytes 196612
  2.8 83.4 %all-to-all-start = ((f32[16,48,512]{2,1,0:T(8,128)}), f32[16,48,512]{2,1,0:T(8,128)S(1)}, u32[]{:S(2)}, u32[]{:S(2)}) async-start(f32[16,48,512]{2,1,0:T(8,128)} %shard_map.77), calls=%async_computation | async-start | bytes 3145728 | tf_op jit(solution)/shard_map/all_to_all | solution.py:258
  9.6 17.4 %collective-permute-start.1 = (f32[32,512]{1,0:T(8,128)S(1)}, f32[32,512]{1,0:T(8,128)S(1)}, u32[]{:S(2)}, u32[]{:S(2)}) collective-permute-start(f32[32,512]{1,0:T(8,128)S(1)} %copy-done.6), channel_id=1, source_target_pairs={{0,256},{16,272},{32,353},{48,369},{64,482},{80,498},{96,291},{112... | collective-permute-start | bytes 196616 | tf_op jit(solution)/shard_map/ppermute | solution.py:62
  27.0 0.6 copy-start.5
  29.1 16.9 %collective-permute-start.4 = (f32[136,128]{1,0:T(8,128)}, f32[136,128]{1,0:T(8,128)S(1)}, u32[]{:S(2)}, u32[]{:S(2)}) collective-permute-start(f32[136,128]{1,0:T(8,128)} %shard_map.79), channel_id=1, source_target_pairs={{0,256},{16,272},{32,288},{48,304},{64,320},{80,336},{96,352},{112... | collective-permute-start | bytes 208904 | tf_op jit(solution)/shard_map/ppermute | solution.py:62
  36.9 13.8 %collective-permute-start.3 = (f32[136,128]{1,0:T(8,128)}, f32[136,128]{1,0:T(8,128)S(1)}, u32[]{:S(2)}, u32[]{:S(2)}) collective-permute-start(f32[136,128]{1,0:T(8,128)} %shard_map.79), channel_id=1, source_target_pairs={{0,384},{16,400},{32,416},{48,432},{64,448},{80,464},{96,480},{112... | collective-permute-start | bytes 208904 | tf_op jit(solution)/shard_map/ppermute | solution.py:62
  40.4 10.4 %collective-permute-start.2 = (f32[136,128]{1,0:T(8,128)}, f32[136,128]{1,0:T(8,128)S(1)}, u32[]{:S(2)}, u32[]{:S(2)}) collective-permute-start(f32[136,128]{1,0:T(8,128)} %shard_map.79), channel_id=1, source_target_pairs={{0,128},{16,144},{32,160},{48,176},{64,192},{80,208},{96,224},{112... | collective-permute-start | bytes 208904 | tf_op jit(solution)/shard_map/ppermute | solution.py:62
  51.6 43.4 %copy-start.4 = (f32[544,128]{1,0:T(8,128)}, f32[544,128]{1,0:T(8,128)S(1)}, u32[]{:S(2)}) copy-start(f32[544,128]{1,0:T(8,128)S(1)} %pad_maximum_fusion.1.mine0) | copy-start | bytes 835588
  51.7 16.3 %collective-permute-start.8 = (f32[544,128]{1,0:T(8,128)S(1)}, f32[544,128]{1,0:T(8,128)S(1)}, u32[]{:S(2)}, u32[]{:S(2)}) collective-permute-start(f32[544,128]{1,0:T(8,128)S(1)} %pad_maximum_fusion.1.mine0), channel_id=1, source_target_pairs={{0,64},{16,464},{32,96},{48,496},{64,128},{80,16},{96,160},{112,48... | collective-permute-start | bytes 835592 | tf_op jit(solution)/shard_map/ppermute | solution.py:62
  55.0 15.4 %collective-permute-start.7 = (f32[544,128]{1,0:T(8,128)S(1)}, f32[544,128]{1,0:T(8,128)S(1)}, u32[]{:S(2)}, u32[]{:S(2)}) collective-permute-start(f32[544,128]{1,0:T(8,128)S(1)} %pad_maximum_fusion.1.mine0), channel_id=1, source_target_pairs={{0,480},{16,496},{32,0},{48,16},{64,32},{80,48},{96,64},{112,80},{... | collective-permute-start | bytes 835592 | tf_op jit(solution)/shard_map/ppermute | solution.py:62
  66.1 9.6 %collective-permute-start.6 = (f32[544,128]{1,0:T(8,128)S(1)}, f32[544,128]{1,0:T(8,128)S(1)}, u32[]{:S(2)}, u32[]{:S(2)}) collective-permute-start(f32[544,128]{1,0:T(8,128)S(1)} %pad_maximum_fusion.1.mine0), channel_id=1, source_target_pairs={{0,32},{16,48},{32,64},{48,80},{64,96},{80,112},{96,128},{112,144}... | collective-permute-start | bytes 835592 | tf_op jit(solution)/shard_map/ppermute | solution.py:62
  68.0 27.0 %copy-start.1 = (f32[544,128]{1,0:T(8,128)}, f32[544,128]{1,0:T(8,128)S(1)}, u32[]{:S(2)}) copy-start(f32[544,128]{1,0:T(8,128)S(1)} %collective-permute-done.8.mine3) | copy-start | bytes 835588
  70.4 24.7 %copy-start.2 = (f32[544,128]{1,0:T(8,128)}, f32[544,128]{1,0:T(8,128)S(1)}, u32[]{:S(2)}) copy-start(f32[544,128]{1,0:T(8,128)S(1)} %collective-permute-done.7.mine2) | copy-start | bytes 835588
  75.6 19.4 %copy-start.3 = (f32[544,128]{1,0:T(8,128)}, f32[544,128]{1,0:T(8,128)S(1)}, u32[]{:S(2)}) copy-start(f32[544,128]{1,0:T(8,128)S(1)} %collective-permute-done.6.mine1) | copy-start | bytes 835588
  75.7 23.1 %collective-permute-start.9 = (f32[1632,128]{1,0:T(8,128)S(1)}, f32[1632,128]{1,0:T(8,128)}, u32[]{:S(2)}, u32[]{:S(2)}) collective-permute-start(f32[1632,128]{1,0:T(8,128)S(1)} %pad_maximum_fusion), channel_id=1, source_target_pairs={{0,16},{16,0},{32,48},{48,32},{64,80},{80,64},{96,112},{112,96},{1... | collective-permute-start | bytes 2506760 | tf_op jit(solution)/shard_map/ppermute | solution.py:62
  86.2 4.4 %copy-start = (f32[16,48,512]{2,1,0:T(8,128)}, f32[16,48,512]{2,1,0:T(8,128)S(1)}, u32[]{:S(2)}) copy-start(f32[16,48,512]{2,1,0:T(8,128)S(1)} %all-to-all-done.gathered) | copy-start | bytes 4718596
  86.3 4.3 %collective-permute-start = (f32[16,16,512]{2,1,0:T(8,128)S(1)}, f32[16,16,512]{2,1,0:T(8,128)}, u32[]{:S(2)}, u32[]{:S(2)}) collective-permute-start(f32[16,16,512]{2,1,0:T(8,128)S(1)} %slice.4), channel_id=1, source_target_pairs={{0,16},{16,0},{32,48},{48,32},{64,80},{80,64},{96,112},{112,96},{1... | collective-permute-start | bytes 1572872 | tf_op jit(solution)/shard_map/ppermute | solution.py:62
  88.2 10.6 %collective-permute-start.5 = (f32[544,128]{1,0:T(8,128)S(1)}, f32[544,128]{1,0:T(8,128)}, u32[]{:S(2)}, u32[]{:S(2)}) collective-permute-start(f32[544,128]{1,0:T(8,128)S(1)} %pad_maximum_fusion.1.mine0), channel_id=1, source_target_pairs={{0,16},{16,0},{32,48},{48,32},{64,80},{80,64},{96,112},{112,96},{1... | collective-permute-start | bytes 835592 | tf_op jit(solution)/shard_map/ppermute | solution.py:62

commit v3 on v2

--- a/solution.py
+++ b/solution.py
@@ -27,11 +27,11 @@
 
 
 STEPS = {
+    4: (2, 2),
+    12: (2, 1), 3: (2, 3), 13: (1, 2), 5: (3, 2),
+    11: (1, 1), 2: (1, 3), 14: (3, 1), 6: (3, 3), 10: (2, 0), 1: (0, 2),
+    15: (1, 0), 7: (3, 0), 9: (0, 1), 0: (0, 3),
     8: (0, 0),
-    7: (1, 0), 9: (3, 0), 6: (0, 1), 10: (0, 3),
-    5: (1, 1), 11: (1, 3), 4: (3, 1), 12: (3, 3), 3: (2, 0), 13: (0, 2),
-    2: (2, 1), 14: (2, 3), 1: (1, 2), 15: (3, 2),
-    0: (2, 2),
 }
 PLACES = {place: step for step, place in STEPS.items()}
 
@@ -44,12 +44,16 @@
 TABLE_X, TABLE_Y = table(0), table(1)
 
 
-def transpose_move(x, y, z, k):
-    cx, cy = z // Y, z % Y
-    return cx, cy, z + PLACES[(x - cx) % X, (y - cy) % Y], k
-
-
-TRANSPOSE = pairs(transpose_move)
+def transpose_move(extra):
+    def move(x, y, z, k):
+        cx, cy = z // Y, z % Y
+        return cx, cy, z + extra + PLACES[(x - cx) % X, (y - cy) % Y], k
+
+    return move
+
+
+TURN_A = pairs(transpose_move(0))
+TURN_B = pairs(transpose_move(8))
 SWAP = pairs(lambda x, y, z, k: (x, y, z, 1 - k))
 PM2 = pairs(lambda x, y, z, k: (x, y, z + 2 if k == 0 else z - 2, k))
 
@@ -72,13 +76,6 @@
     bh, bl = b
     dot = lambda u, v: lax.dot_general(u, v, dims, preferred_element_type=jnp.float32)
     return dot(ah, bh) + (dot(ah, bl) + dot(al, bh))
-
-
-def pack_body(chunk, fold, out):
-    for j in range(4):
-        out[32 * j:32 * j + 32, :] = chunk[:, 128 * j:128 * j + 128]
-    out[128:136, 0:64] = fold[0:8, :]
-    out[128:136, 64:128] = fold[8:16, :]
 
 
 def weight_body(gathered, other, out_high, out_low, rows, inv, sems):
@@ -100,6 +97,8 @@
 
 
 OFFSETS = (0, -4, 4, 8)
+CHUNK_ROWS = (0, 136, 280, 416)
+FOLD_ROWS = (128, 264, 408, 272)
 
 
 def where_am_i():
@@ -116,12 +115,14 @@
         px = (col // 4 + (jnp.int32(TABLE_X) >> hop)) & 3
         py = (col + (jnp.int32(TABLE_Y) >> hop)) & 3
         rows = pl.ds(pl.multiple_of(32 * (4 * px + py), 32), 32)
-        start = 544 * group + 136 * slot
+        start = 544 * group + CHUNK_ROWS[slot]
         for j in range(4):
-            h, l = split(ref[start + 32 * j:start + 32 * j + 32, :])
+            tiles = [ref[start + 8 * (4 * i + j):start + 8 * (4 * i + j) + 8, :] for i in range(4)]
+            h, l = split(jnp.concatenate(tiles, 0))
             high[rows, 128 * j:128 * j + 128] = h
             low[rows, 128 * j:128 * j + 128] = l
-        tile = ref[start + 128:start + 136, :]
+        start = 544 * group + FOLD_ROWS[slot]
+        tile = ref[start:start + 8, :]
         first = pl.multiple_of(16 * (2 * at + core), 16)
         fold[pl.ds(first, 8), :] = tile
         fold[pl.ds(first + 8, 8), :] = pltpu.roll(tile, 64, 1)
@@ -251,14 +252,22 @@
     return pltpu.SemaphoreType.DMA((n,))
 
 
+def tile_order(chunk):
+    return chunk.reshape(4, 8, 4, 128).transpose(0, 2, 1, 3).reshape(128, 128)
+
+
 def step(trailing, panel, inv_factor, later_series, fold_series, fold_len):
     half = jnp.bfloat16
-    chunk = send(panel, TRANSPOSE)
+    chunk_a = tile_order(send(panel, TURN_A))
     load = kernel(spread_body, shape(16, 48, 512), "aa", "a", [block(48, 512), sems(18)])(panel, inv_factor.T)
     gathered = lax.all_to_all(load, "col", 0, 0, tiled=True)
-    packed = kernel(pack_body, shape(136, 128), "vv", "v")(chunk, fold_series)
-    far = [packed] + [send(packed, shift(d)) for d in (4, -4, 8)]
-    near = jnp.concatenate(far, 0)
+    chunk_b = tile_order(send(panel, TURN_B))
+    fold = jnp.concatenate([fold_series[0:8], fold_series[8:16]], 1)
+    fold_back = send(fold, shift(4))
+    base = jnp.concatenate([chunk_a, fold], 0)
+    up = send(jnp.concatenate([base, fold_back], 0), shift(4))
+    down = send(base, shift(-4))
+    near = jnp.concatenate([base, up, down, chunk_b], 0)
     mine = [send(near, shift(1)), send(near, shift(-1)), send(near, PM2)]
     other0 = send(near, SWAP)
     other = send(gathered[:, 32:, :], SWAP)

time: 104 us -> 95.3 us (0.916)
  the two profiles are of different devices: /device:TPU:13 before, /device:TPU:1 now
where the time goes in v3:
time: 95.3 us; the launch traced here: 94.8 us
  starting transfers between devices  62.5 us (66%)
  Pallas kernels  16.6 us (17%)
  waiting for transfers between devices  14.4 us (15%)
    ppermute x11, starting transfers between devices, send(): return lax.ppermute(array, AXES, moves)  58.8 us
    pallas_call x4, Pallas kernels, call(): pl.pallas_call(body, out_shape=out, in_specs=[specs[m] for m in memory],...  16.6 us
    ppermute x11, waiting for transfers between devices, send(): return lax.ppermute(array, AXES, moves)  14.4 us
    all_to_all x1, starting transfers between devices, step(): gathered = lax.all_to_all(load, 'col', 0, 0, tiled=True)  3.72 us
  transfers between devices with their start and end apart: 12, of which 6 were waited for; matrix products, arithmetic and copies ran while one was open for 0% of the time, Pallas kernels for 12%

profile of v3, /device:TPU:1, one launch (start us, length us, event | category | flops | bytes accessed | tf_op | source)
XLA Modules:
  0.0 94.8 jit_solution(11474013249494872633)
XLA Ops:
  0.6 16.3 %collective-permute-start.1 = (f32[32,512]{1,0:T(8,128)}, f32[32,512]{1,0:T(8,128)S(1)}, u32[]{:S(2)}, u32[]{:S(2)}) collective-permute-start(f32[32,512]{1,0:T(8,128)} %panel.1), channel_id=1, source_target_pairs={{0,256},{16,272},{32,33},{48,49},{64,98},{80,114},{96,387},{112,40... | collective-permute-start | bytes 196616 | tf_op jit(solution)/shard_map/ppermute | solution.py:66
  16.9 2.2 %shard_map.77 = f32[16,48,512]{2,1,0:T(8,128)} custom-call(f32[32,512]{1,0:T(8,128)} %panel.1, f32[32,512]{1,0:T(8,128)} %bitcast.19), custom_call_target="tpu_custom_call" | custom-call | tf_op jit(solution)/shard_map/pallas_call | solution.py:235
  19.1 3.7 %all-to-all-start = ((f32[16,48,512]{2,1,0:T(8,128)}), f32[16,48,512]{2,1,0:T(8,128)S(1)}, u32[]{:S(2)}, u32[]{:S(2)}) async-start(f32[16,48,512]{2,1,0:T(8,128)} %shard_map.77), calls=%async_computation | async-start | bytes 3145728 | tf_op jit(solution)/shard_map/all_to_all | solution.py:263
  22.9 0.1 constant_dynamic-update-slice_fusion.3
  23.0 5.6 %collective-permute-start.2 = (f32[8,128]{1,0:T(8,128)S(1)}, f32[8,128]{1,0:T(8,128)S(1)}, u32[]{:S(2)}, u32[]{:S(2)}) collective-permute-start(f32[8,128]{1,0:T(8,128)S(1)} %get-tuple-element.15), channel_id=1, source_target_pairs={{0,128},{16,144},{32,160},{48,176},{64,192},{80,208},{96,224},{112... | collective-permute-start | bytes 12296 | tf_op jit(solution)/shard_map/ppermute | solution.py:66
  28.6 0.7 collective-permute-start.5
  29.2 2.0 %collective-permute-done.2 = f32[8,128]{1,0:T(8,128)S(1)} collective-permute-done((f32[8,128]{1,0:T(8,128)S(1)}, f32[8,128]{1,0:T(8,128)S(1)}, u32[]{:S(2)}, u32[]{:S(2)}) %collective-permute-start.2) | collective-permute-done | bytes 4128 | tf_op jit(solution)/shard_map/ppermute | solution.py:66
  31.2 0.1 pad_maximum_fusion.1
  31.3 6.8 %collective-permute-start.3 = (f32[144,128]{1,0:T(8,128)S(1)}, f32[144,128]{1,0:T(8,128)S(1)}, u32[]{:S(2)}, u32[]{:S(2)}) collective-permute-start(f32[144,128]{1,0:T(8,128)S(1)} %pad_maximum_fusion.1), channel_id=1, source_target_pairs={{0,128},{16,144},{32,160},{48,176},{64,192},{80,208},{96,224},{112... | collective-permute-start | bytes 221192 | tf_op jit(solution)/shard_map/ppermute | solution.py:66
  38.2 5.8 %collective-permute-start.4 = (f32[136,128]{1,0:T(8,128)S(1)}, f32[136,128]{1,0:T(8,128)S(1)}, u32[]{:S(2)}, u32[]{:S(2)}) collective-permute-start(f32[136,128]{1,0:T(8,128)S(1)} %maximum_maximum_fusion), channel_id=1, source_target_pairs={{0,384},{16,400},{32,416},{48,432},{64,448},{80,464},{96,480},{112... | collective-permute-start | bytes 208904 | tf_op jit(solution)/shard_map/ppermute | solution.py:66
  44.0 1.3 %collective-permute-done.3 = f32[144,128]{1,0:T(8,128)S(1)} collective-permute-done((f32[144,128]{1,0:T(8,128)S(1)}, f32[144,128]{1,0:T(8,128)S(1)}, u32[]{:S(2)}, u32[]{:S(2)}) %collective-permute-start.3) | collective-permute-done | bytes 73760 | tf_op jit(solution)/shard_map/ppermute | solution.py:66
  45.3 1.8 %collective-permute-done.4 = f32[136,128]{1,0:T(8,128)S(1)} collective-permute-done((f32[136,128]{1,0:T(8,128)S(1)}, f32[136,128]{1,0:T(8,128)S(1)}, u32[]{:S(2)}, u32[]{:S(2)}) %collective-permute-start.4) | collective-permute-done | bytes 69664 | tf_op jit(solution)/shard_map/ppermute | solution.py:66
  47.1 9.9 %collective-permute-start.9 = (f32[544,128]{1,0:T(8,128)S(1)}, f32[544,128]{1,0:T(8,128)S(1)}, u32[]{:S(2)}, u32[]{:S(2)}) collective-permute-start(f32[544,128]{1,0:T(8,128)S(1)} %constant_dynamic-update-slice_fusion.mine0), channel_id=1, source_target_pairs={{0,64},{16,464},{32,96},{48,496},{64,128},{80,16},{96,160},{112,48... | collective-permute-start | bytes 835592 | tf_op jit(solution)/shard_map/ppermute | solution.py:66
  57.0 2.8 %collective-permute-start.8 = (f32[544,128]{1,0:T(8,128)S(1)}, f32[544,128]{1,0:T(8,128)S(1)}, u32[]{:S(2)}, u32[]{:S(2)}) collective-permute-start(f32[544,128]{1,0:T(8,128)S(1)} %constant_dynamic-update-slice_fusion.mine0), channel_id=1, source_target_pairs={{0,480},{16,496},{32,0},{48,16},{64,32},{80,48},{96,64},{112,80},{... | collective-permute-start | bytes 835592 | tf_op jit(solution)/shard_map/ppermute | solution.py:66
  59.8 3.1 %collective-permute-start.7 = (f32[544,128]{1,0:T(8,128)S(1)}, f32[544,128]{1,0:T(8,128)S(1)}, u32[]{:S(2)}, u32[]{:S(2)}) collective-permute-start(f32[544,128]{1,0:T(8,128)S(1)} %constant_dynamic-update-slice_fusion.mine0), channel_id=1, source_target_pairs={{0,32},{16,48},{32,64},{48,80},{64,96},{80,112},{96,128},{112,144}... | collective-permute-start | bytes 835592 | tf_op jit(solution)/shard_map/ppermute | solution.py:66
  62.9 1.0 %collective-permute-done.9.mine3 = f32[544,128]{1,0:T(8,128)S(1)} collective-permute-done((f32[544,128]{1,0:T(8,128)S(1)}, f32[544,128]{1,0:T(8,128)S(1)}, u32[]{:S(2)}, u32[]{:S(2)}) %collective-permute-start.9) | collective-permute-done | bytes 278560 | tf_op jit(solution)/shard_map/ppermute | solution.py:66
  64.0 5.5 %collective-permute-done.8.mine2 = f32[544,128]{1,0:T(8,128)S(1)} collective-permute-done((f32[544,128]{1,0:T(8,128)S(1)}, f32[544,128]{1,0:T(8,128)S(1)}, u32[]{:S(2)}, u32[]{:S(2)}) %collective-permute-start.8) | collective-permute-done | bytes 278560 | tf_op jit(solution)/shard_map/ppermute | solution.py:66
  69.5 2.7 %collective-permute-done.7.mine1 = f32[544,128]{1,0:T(8,128)S(1)} collective-permute-done((f32[544,128]{1,0:T(8,128)S(1)}, f32[544,128]{1,0:T(8,128)S(1)}, u32[]{:S(2)}, u32[]{:S(2)}) %collective-permute-start.7) | collective-permute-done | bytes 278560 | tf_op jit(solution)/shard_map/ppermute | solution.py:66
  72.2 3.6 %collective-permute-start.10 = (f32[1632,128]{1,0:T(8,128)S(1)}, f32[1632,128]{1,0:T(8,128)}, u32[]{:S(2)}, u32[]{:S(2)}) collective-permute-start(f32[1632,128]{1,0:T(8,128)S(1)} %pad_maximum_fusion), channel_id=1, source_target_pairs={{0,16},{16,0},{32,48},{48,32},{64,80},{80,64},{96,112},{112,96},{1... | collective-permute-start | bytes 2506760 | tf_op jit(solution)/shard_map/ppermute | solution.py:66
  75.9 1.9 %collective-permute-start = (f32[16,16,512]{2,1,0:T(8,128)S(1)}, f32[16,16,512]{2,1,0:T(8,128)}, u32[]{:S(2)}, u32[]{:S(2)}) collective-permute-start(f32[16,16,512]{2,1,0:T(8,128)S(1)} %slice.12), channel_id=1, source_target_pairs={{0,16},{16,0},{32,48},{48,32},{64,80},{80,64},{96,112},{112,96},{1... | collective-permute-start | bytes 1572872 | tf_op jit(solution)/shard_map/ppermute | solution.py:66
  77.9 2.4 %collective-permute-start.6 = (f32[544,128]{1,0:T(8,128)S(1)}, f32[544,128]{1,0:T(8,128)}, u32[]{:S(2)}, u32[]{:S(2)}) collective-permute-start(f32[544,128]{1,0:T(8,128)S(1)} %constant_dynamic-update-slice_fusion.mine0), channel_id=1, source_target_pairs={{0,16},{16,0},{32,48},{48,32},{64,80},{80,64},{96,112},{112,96},{1... | collective-permute-start | bytes 835592 | tf_op jit(solution)/shard_map/ppermute | solution.py:66
  80.3 4.3 %shard_map.78 = (bf16[512,512]{1,0:T(8,128)(2,1)}, bf16[512,512]{1,0:T(8,128)(2,1)}) custom-call(f32[16,48,512]{2,1,0:T(8,128)} %copy-done, f32[16,16,512]{2,1,0:T(8,128)} %collective-permute-done.other), custom_call_target="tpu_custom_call" | custom-call | tf_op jit(solution)/shard_map/pallas_call | solution.py:235
  84.7 4.7 %shard_map.79 = (f32[512,1024]{1,0:T(8,128)}, f32[512,128]{1,0:T(8,128)}) custom-call(bf16[512,512]{1,0:T(8,128)(2,1)} %get-tuple-element.8.w_high, bf16[512,512]{1,0:T(8,128)(2,1)} %get-tuple-element.9.w_low, f32[544,128]{1,0:T(8,128)} %copy-done.4, f32[544,128]{1,0:T(8,128)} %copy-done.3, f32[544,128]{1,0:T(8,128)} %copy-done.2, f32[544,128]{1,0:T(8,128)} %copy-done.1, ...), custom_call_target="tpu_custom_call" | custom-call | tf_op jit(solution)/shard_map/pallas_call | solution.py:235
  89.5 5.3 %shard_map.80 = (f32[512,1024]{1,0:T(8,128)}, f32[64,512]{1,0:T(8,128)}) custom-call(bf16[512,512]{1,0:T(8,128)(2,1)} %get-tuple-element.8.w_high, bf16[512,512]{1,0:T(8,128)(2,1)} %get-tuple-element.9.w_low, f32[544,128]{1,0:T(8,128)} %collective-permute-done.6.other0, f32[1632,128]{1,0:T(8,128)} %collective-permute-done.10.others, ...), custom_call_target="tpu_custom_call", output_to_operand_aliasing={{0}: (5, {})} | custom-call | tf_op jit(solution)/shard_map/pallas_call | solution.py:235
  (28 shorter events, 0.2 us)
Async XLA Ops:
  0.6 22.2 %collective-permute-start.1 = (f32[32,512]{1,0:T(8,128)}, f32[32,512]{1,0:T(8,128)S(1)}, u32[]{:S(2)}, u32[]{:S(2)}) collective-permute-start(f32[32,512]{1,0:T(8,128)} %panel.1), channel_id=1, source_target_pairs={{0,256},{16,272},{32,33},{48,49},{64,98},{80,114},{96,387},{112,40... | collective-permute-start | bytes 196616 | tf_op jit(solution)/shard_map/ppermute | solution.py:66
  16.9 5.9 %copy-start.6 = (f32[16,64]{1,0:T(8,128)S(1)}, f32[16,64]{1,0:T(8,128)}, u32[]{:S(2)}) copy-start(f32[16,64]{1,0:T(8,128)} %param.10) | copy-start | bytes 12292
  16.9 11.6 %copy-start.5 = (f32[32,512]{1,0:T(8,128)S(1)}, f32[32,512]{1,0:T(8,128)}, u32[]{:S(2)}) copy-start(f32[32,512]{1,0:T(8,128)} %panel.1) | copy-start | bytes 196612
  19.1 56.8 %all-to-all-start = ((f32[16,48,512]{2,1,0:T(8,128)}), f32[16,48,512]{2,1,0:T(8,128)S(1)}, u32[]{:S(2)}, u32[]{:S(2)}) async-start(f32[16,48,512]{2,1,0:T(8,128)} %shard_map.77), calls=%async_computation | async-start | bytes 3145728 | tf_op jit(solution)/shard_map/all_to_all | solution.py:263
  23.0 8.2 %collective-permute-start.2 = (f32[8,128]{1,0:T(8,128)S(1)}, f32[8,128]{1,0:T(8,128)S(1)}, u32[]{:S(2)}, u32[]{:S(2)}) collective-permute-start(f32[8,128]{1,0:T(8,128)S(1)} %get-tuple-element.15), channel_id=1, source_target_pairs={{0,128},{16,144},{32,160},{48,176},{64,192},{80,208},{96,224},{112... | collective-permute-start | bytes 12296 | tf_op jit(solution)/shard_map/ppermute | solution.py:66
  28.6 18.6 %collective-permute-start.5 = (f32[32,512]{1,0:T(8,128)S(1)}, f32[32,512]{1,0:T(8,128)S(1)}, u32[]{:S(2)}, u32[]{:S(2)}) collective-permute-start(f32[32,512]{1,0:T(8,128)S(1)} %copy-done.5), channel_id=1, source_target_pairs={{0,0},{16,16},{32,289},{48,305},{64,354},{80,370},{96,131},{112,14... | collective-permute-start | bytes 196616 | tf_op jit(solution)/shard_map/ppermute | solution.py:66
  31.3 14.0 %collective-permute-start.3 = (f32[144,128]{1,0:T(8,128)S(1)}, f32[144,128]{1,0:T(8,128)S(1)}, u32[]{:S(2)}, u32[]{:S(2)}) collective-permute-start(f32[144,128]{1,0:T(8,128)S(1)} %pad_maximum_fusion.1), channel_id=1, source_target_pairs={{0,128},{16,144},{32,160},{48,176},{64,192},{80,208},{96,224},{112... | collective-permute-start | bytes 221192 | tf_op jit(solution)/shard_map/ppermute | solution.py:66
  38.2 8.9 %collective-permute-start.4 = (f32[136,128]{1,0:T(8,128)S(1)}, f32[136,128]{1,0:T(8,128)S(1)}, u32[]{:S(2)}, u32[]{:S(2)}) collective-permute-start(f32[136,128]{1,0:T(8,128)S(1)} %maximum_maximum_fusion), channel_id=1, source_target_pairs={{0,384},{16,400},{32,416},{48,432},{64,448},{80,464},{96,480},{112... | collective-permute-start | bytes 208904 | tf_op jit(solution)/shard_map/ppermute | solution.py:66
  47.1 37.5 %copy-start.4 = (f32[544,128]{1,0:T(8,128)}, f32[544,128]{1,0:T(8,128)S(1)}, u32[]{:S(2)}) copy-start(f32[544,128]{1,0:T(8,128)S(1)} %constant_dynamic-update-slice_fusion.mine0) | copy-start | bytes 835588
  47.1 16.8 %collective-permute-start.9 = (f32[544,128]{1,0:T(8,128)S(1)}, f32[544,128]{1,0:T(8,128)S(1)}, u32[]{:S(2)}, u32[]{:S(2)}) collective-permute-start(f32[544,128]{1,0:T(8,128)S(1)} %constant_dynamic-update-slice_fusion.mine0), channel_id=1, source_target_pairs={{0,64},{16,464},{32,96},{48,496},{64,128},{80,16},{96,160},{112,48... | collective-permute-start | bytes 835592 | tf_op jit(solution)/shard_map/ppermute | solution.py:66
  57.0 12.4 %collective-permute-start.8 = (f32[544,128]{1,0:T(8,128)S(1)}, f32[544,128]{1,0:T(8,128)S(1)}, u32[]{:S(2)}, u32[]{:S(2)}) collective-permute-start(f32[544,128]{1,0:T(8,128)S(1)} %constant_dynamic-update-slice_fusion.mine0), channel_id=1, source_target_pairs={{0,480},{16,496},{32,0},{48,16},{64,32},{80,48},{96,64},{112,80},{... | collective-permute-start | bytes 835592 | tf_op jit(solution)/shard_map/ppermute | solution.py:66
  59.8 12.4 %collective-permute-start.7 = (f32[544,128]{1,0:T(8,128)S(1)}, f32[544,128]{1,0:T(8,128)S(1)}, u32[]{:S(2)}, u32[]{:S(2)}) collective-permute-start(f32[544,128]{1,0:T(8,128)S(1)} %constant_dynamic-update-slice_fusion.mine0), channel_id=1, source_target_pairs={{0,32},{16,48},{32,64},{48,80},{64,96},{80,112},{96,128},{112,144}... | collective-permute-start | bytes 835592 | tf_op jit(solution)/shard_map/ppermute | solution.py:66
  64.0 20.7 %copy-start.1 = (f32[544,128]{1,0:T(8,128)}, f32[544,128]{1,0:T(8,128)S(1)}, u32[]{:S(2)}) copy-start(f32[544,128]{1,0:T(8,128)S(1)} %collective-permute-done.9.mine3) | copy-start | bytes 835588
  69.5 15.2 %copy-start.2 = (f32[544,128]{1,0:T(8,128)}, f32[544,128]{1,0:T(8,128)S(1)}, u32[]{:S(2)}) copy-start(f32[544,128]{1,0:T(8,128)S(1)} %collective-permute-done.8.mine2) | copy-start | bytes 835588
  72.2 12.5 %copy-start.3 = (f32[544,128]{1,0:T(8,128)}, f32[544,128]{1,0:T(8,128)S(1)}, u32[]{:S(2)}) copy-start(f32[544,128]{1,0:T(8,128)S(1)} %collective-permute-done.7.mine1) | copy-start | bytes 835588
  72.2 17.2 %collective-permute-start.10 = (f32[1632,128]{1,0:T(8,128)S(1)}, f32[1632,128]{1,0:T(8,128)}, u32[]{:S(2)}, u32[]{:S(2)}) collective-permute-start(f32[1632,128]{1,0:T(8,128)S(1)} %pad_maximum_fusion), channel_id=1, source_target_pairs={{0,16},{16,0},{32,48},{48,32},{64,80},{80,64},{96,112},{112,96},{1... | collective-permute-start | bytes 2506760 | tf_op jit(solution)/shard_map/ppermute | solution.py:66
  75.9 4.4 %copy-start = (f32[16,48,512]{2,1,0:T(8,128)}, f32[16,48,512]{2,1,0:T(8,128)S(1)}, u32[]{:S(2)}) copy-start(f32[16,48,512]{2,1,0:T(8,128)S(1)} %all-to-all-done.gathered) | copy-start | bytes 4718596
  75.9 4.3 %collective-permute-start = (f32[16,16,512]{2,1,0:T(8,128)S(1)}, f32[16,16,512]{2,1,0:T(8,128)}, u32[]{:S(2)}, u32[]{:S(2)}) collective-permute-start(f32[16,16,512]{2,1,0:T(8,128)S(1)} %slice.12), channel_id=1, source_target_pairs={{0,16},{16,0},{32,48},{48,32},{64,80},{80,64},{96,112},{112,96},{1... | collective-permute-start | bytes 1572872 | tf_op jit(solution)/shard_map/ppermute | solution.py:66
  77.9 11.6 %collective-permute-start.6 = (f32[544,128]{1,0:T(8,128)S(1)}, f32[544,128]{1,0:T(8,128)}, u32[]{:S(2)}, u32[]{:S(2)}) collective-permute-start(f32[544,128]{1,0:T(8,128)S(1)} %constant_dynamic-update-slice_fusion.mine0), channel_id=1, source_target_pairs={{0,16},{16,0},{32,48},{48,32},{64,80},{80,64},{96,112},{112,96},{1... | collective-permute-start | bytes 835592 | tf_op jit(solution)/shard_map/ppermute | solution.py:66

commit v4 on v2

--- a/solution.py
+++ b/solution.py
@@ -49,7 +49,7 @@
     return cx, cy, z + PLACES[(x - cx) % X, (y - cy) % Y], k
 
 
-TRANSPOSE = pairs(transpose_move)
+TURN = pairs(transpose_move)
 SWAP = pairs(lambda x, y, z, k: (x, y, z, 1 - k))
 PM2 = pairs(lambda x, y, z, k: (x, y, z + 2 if k == 0 else z - 2, k))
 
@@ -74,24 +74,13 @@
     return dot(ah, bh) + (dot(ah, bl) + dot(al, bh))
 
 
-def pack_body(chunk, fold, out):
-    for j in range(4):
-        out[32 * j:32 * j + 32, :] = chunk[:, 128 * j:128 * j + 128]
-    out[128:136, 0:64] = fold[0:8, :]
-    out[128:136, 64:128] = fold[8:16, :]
-
-
-def weight_body(gathered, other, out_high, out_low, rows, inv, sems):
-    k = lax.axis_index("row") % 2
+def weight_body(gathered, out_high, out_low, rows, inv, sems):
     copies = [
         pltpu.make_async_copy(gathered.at[:, 0:32, :], rows, sems.at[0]),
-        pltpu.make_async_copy(gathered.at[:, 32:48, :], inv.at[:, k], sems.at[1]),
-        pltpu.make_async_copy(other, inv.at[:, 1 - k], sems.at[2]),
-    ]
-    for copy in copies:
-        copy.start()
-    for copy in copies:
-        copy.wait()
+        pltpu.make_async_copy(gathered.at[:, 32:64, :], inv, sems.at[1]),
+    ]
+    begin(copies)
+    end(copies)
     inverse = split(inv[...].reshape(512, 512))
     solved = dot3(split(rows[...].reshape(512, 512)), inverse, NN)
     high, low = split(dot3(split(solved), inverse, NT))
@@ -118,7 +107,8 @@
         rows = pl.ds(pl.multiple_of(32 * (4 * px + py), 32), 32)
         start = 544 * group + 136 * slot
         for j in range(4):
-            h, l = split(ref[start + 32 * j:start + 32 * j + 32, :])
+            tiles = [ref[start + 8 * (4 * i + j):start + 8 * (4 * i + j) + 8, :] for i in range(4)]
+            h, l = split(jnp.concatenate(tiles, 0))
             high[rows, 128 * j:128 * j + 128] = h
             low[rows, 128 * j:128 * j + 128] = l
         tile = ref[start + 128:start + 136, :]
@@ -206,10 +196,9 @@
 
 
 def spread_body(panel, stripe, out, stage, sems):
-    k = lax.axis_index("row") % 2
     loads = [
         pltpu.make_async_copy(panel, stage.at[0:32, :], sems.at[16]),
-        pltpu.make_async_copy(stripe.at[pl.ds(pl.multiple_of(16 * k, 16), 16), :], stage.at[32:48, :], sems.at[17]),
+        pltpu.make_async_copy(stripe, stage.at[32:64, :], sems.at[17]),
     ]
     begin(loads)
     end(loads)
@@ -251,30 +240,33 @@
     return pltpu.SemaphoreType.DMA((n,))
 
 
+def tile_order(chunk):
+    return chunk.reshape(4, 8, 4, 128).transpose(0, 2, 1, 3).reshape(128, 128)
+
+
 def step(trailing, panel, inv_factor, later_series, fold_series, fold_len):
     half = jnp.bfloat16
-    chunk = send(panel, TRANSPOSE)
-    load = kernel(spread_body, shape(16, 48, 512), "aa", "a", [block(48, 512), sems(18)])(panel, inv_factor.T)
+    chunk = tile_order(send(panel, TURN))
+    load = kernel(spread_body, shape(16, 64, 512), "aa", "a", [block(64, 512), sems(18)])(panel, inv_factor.T)
     gathered = lax.all_to_all(load, "col", 0, 0, tiled=True)
-    packed = kernel(pack_body, shape(136, 128), "vv", "v")(chunk, fold_series)
-    far = [packed] + [send(packed, shift(d)) for d in (4, -4, 8)]
-    near = jnp.concatenate(far, 0)
-    mine = [send(near, shift(1)), send(near, shift(-1)), send(near, PM2)]
-    other0 = send(near, SWAP)
-    other = send(gathered[:, 32:, :], SWAP)
+    fold = jnp.concatenate([fold_series[0:8], fold_series[8:16]], 1)
+    base = jnp.concatenate([chunk, fold], 0)
+    near = jnp.concatenate([base] + [send(base, shift(d)) for d in (4, -4, 8)], 0)
+    mine = [near, send(near, shift(1)), send(near, shift(-1)), send(near, PM2)]
     weight = kernel(
         weight_body,
         (shape(512, 512, dtype=half), shape(512, 512, dtype=half)),
-        "aa",
+        "a",
         "vv",
-        [block(16, 32, 512), block(16, 2, 16, 512), sems(3)],
-    )(gathered, other)
-    others = send(jnp.concatenate(mine, 0), SWAP)
+        [block(16, 32, 512), block(16, 32, 512), sems(2)],
+    )(gathered)
+    other0 = send(near, SWAP)
+    others = send(jnp.concatenate(mine[1:], 0), SWAP)
     square = block(512, 512, dtype=half)
     work = [block(2176, 128), square, square, square, square, block(512, 512), block(512, 512)]
     part, half_fold = kernel(
         first_body, (shape(512, 1024), shape(512, 128)), "aaaaaaa", "av", work + [sems(9)]
-    )(*weight, near, *mine, trailing)
+    )(*weight, *mine, trailing)
     out, series = kernel(
         second_body,
         (shape(512, 1024), shape(64, 512)),

time: 104 us -> 89.3 us (0.86)
  the two profiles are of different devices: /device:TPU:13 before, /device:TPU:1 now
where the time goes in v4:
time: 89.3 us; the launch traced here: 88.8 us
  starting transfers between devices  54.4 us (61%)
  Pallas kernels  16.7 us (19%)
  waiting for transfers between devices  13.6 us (15%)
  local copies, waits for them, and re-layouts  2.08 us (2%)
  other arithmetic  1.14 us (1%)
    ppermute x9, starting transfers between devices, send(): return lax.ppermute(array, AXES, moves)  50.7 us
    pallas_call x4, Pallas kernels, call(): pl.pallas_call(body, out_shape=out, in_specs=[specs[m] for m in memory],...  16.7 us
    ppermute x9, waiting for transfers between devices, send(): return lax.ppermute(array, AXES, moves)  13.6 us
    all_to_all x1, starting transfers between devices, step(): gathered = lax.all_to_all(load, 'col', 0, 0, tiled=True)  3.73 us
    unnamed x17, local copies, waits for them, and re-layouts  2.07 us
  transfers between devices with their start and end apart: 10, of which 4 were waited for; matrix products, arithmetic and copies ran while one was open for 1% of the time, Pallas kernels for 13%

profile of v4, /device:TPU:1, one launch (start us, length us, event | category | flops | bytes accessed | tf_op | source)
XLA Modules:
  0.0 88.8 jit_solution(12961293071922657926)
XLA Ops:
  0.6 16.3 %collective-permute-start = (f32[32,512]{1,0:T(8,128)}, f32[32,512]{1,0:T(8,128)S(1)}, u32[]{:S(2)}, u32[]{:S(2)}) collective-permute-start(f32[32,512]{1,0:T(8,128)} %panel.1), channel_id=1, source_target_pairs={{0,256},{16,272},{32,353},{48,369},{64,482},{80,498},{96,291},{112... | collective-permute-start | bytes 196616 | tf_op jit(solution)/shard_map/ppermute | solution.py:62
  16.9 2.3 %shard_map.77 = f32[16,64,512]{2,1,0:T(8,128)} custom-call(f32[32,512]{1,0:T(8,128)} %panel.1, f32[32,512]{1,0:T(8,128)} %bitcast.12), custom_call_target="tpu_custom_call" | custom-call | tf_op jit(solution)/shard_map/pallas_call | solution.py:223
  19.2 3.7 %all-to-all-start = ((f32[16,64,512]{2,1,0:T(8,128)}), f32[16,64,512]{2,1,0:T(8,128)S(1)}, u32[]{:S(2)}, u32[]{:S(2)}) async-start(f32[16,64,512]{2,1,0:T(8,128)} %shard_map.77), calls=%async_computation | async-start | bytes 4194304 | tf_op jit(solution)/shard_map/all_to_all | solution.py:251
  23.0 0.1 maximum_maximum_fusion
  23.1 9.8 %collective-permute-start.3 = (f32[136,128]{1,0:T(8,128)S(1)}, f32[136,128]{1,0:T(8,128)S(1)}, u32[]{:S(2)}, u32[]{:S(2)}) collective-permute-start(f32[136,128]{1,0:T(8,128)S(1)} %maximum_maximum_fusion), channel_id=1, source_target_pairs={{0,256},{16,272},{32,288},{48,304},{64,320},{80,336},{96,352},{112... | collective-permute-start | bytes 208904 | tf_op jit(solution)/shard_map/ppermute | solution.py:62
  32.9 2.4 %collective-permute-start.2 = (f32[136,128]{1,0:T(8,128)S(1)}, f32[136,128]{1,0:T(8,128)S(1)}, u32[]{:S(2)}, u32[]{:S(2)}) collective-permute-start(f32[136,128]{1,0:T(8,128)S(1)} %maximum_maximum_fusion), channel_id=1, source_target_pairs={{0,384},{16,400},{32,416},{48,432},{64,448},{80,464},{96,480},{112... | collective-permute-start | bytes 208904 | tf_op jit(solution)/shard_map/ppermute | solution.py:62
  35.3 6.8 %collective-permute-start.1 = (f32[136,128]{1,0:T(8,128)S(1)}, f32[136,128]{1,0:T(8,128)S(1)}, u32[]{:S(2)}, u32[]{:S(2)}) collective-permute-start(f32[136,128]{1,0:T(8,128)S(1)} %maximum_maximum_fusion), channel_id=1, source_target_pairs={{0,128},{16,144},{32,160},{48,176},{64,192},{80,208},{96,224},{112... | collective-permute-start | bytes 208904 | tf_op jit(solution)/shard_map/ppermute | solution.py:62
  42.1 0.1 constant_dynamic-update-slice_fusion.3
  42.2 2.4 %collective-permute-done.1 = f32[136,128]{1,0:T(8,128)S(1)} collective-permute-done((f32[136,128]{1,0:T(8,128)S(1)}, f32[136,128]{1,0:T(8,128)S(1)}, u32[]{:S(2)}, u32[]{:S(2)}) %collective-permute-start.1) | collective-permute-done | bytes 69664 | tf_op jit(solution)/shard_map/ppermute | solution.py:62
  44.5 3.2 %collective-permute-done.2 = f32[136,128]{1,0:T(8,128)S(1)} collective-permute-done((f32[136,128]{1,0:T(8,128)S(1)}, f32[136,128]{1,0:T(8,128)S(1)}, u32[]{:S(2)}, u32[]{:S(2)}) %collective-permute-start.2) | collective-permute-done | bytes 69664 | tf_op jit(solution)/shard_map/ppermute | solution.py:62
  47.8 2.5 %collective-permute-start.7 = (f32[544,128]{1,0:T(8,128)S(1)}, f32[544,128]{1,0:T(8,128)S(1)}, u32[]{:S(2)}, u32[]{:S(2)}) collective-permute-start(f32[544,128]{1,0:T(8,128)S(1)} %constant_dynamic-update-slice_fusion.mine0), channel_id=1, source_target_pairs={{0,64},{16,464},{32,96},{48,496},{64,128},{80,16},{96,160},{112,48... | collective-permute-start | bytes 835592 | tf_op jit(solution)/shard_map/ppermute | solution.py:62
  50.3 4.7 %collective-permute-start.6 = (f32[544,128]{1,0:T(8,128)S(1)}, f32[544,128]{1,0:T(8,128)S(1)}, u32[]{:S(2)}, u32[]{:S(2)}) collective-permute-start(f32[544,128]{1,0:T(8,128)S(1)} %constant_dynamic-update-slice_fusion.mine0), channel_id=1, source_target_pairs={{0,480},{16,496},{32,0},{48,16},{64,32},{80,48},{96,64},{112,80},{... | collective-permute-start | bytes 835592 | tf_op jit(solution)/shard_map/ppermute | solution.py:62
  55.0 3.1 %collective-permute-start.5 = (f32[544,128]{1,0:T(8,128)S(1)}, f32[544,128]{1,0:T(8,128)S(1)}, u32[]{:S(2)}, u32[]{:S(2)}) collective-permute-start(f32[544,128]{1,0:T(8,128)S(1)} %constant_dynamic-update-slice_fusion.mine0), channel_id=1, source_target_pairs={{0,32},{16,48},{32,64},{48,80},{64,96},{80,112},{96,128},{112,144}... | collective-permute-start | bytes 835592 | tf_op jit(solution)/shard_map/ppermute | solution.py:62
  58.1 7.2 %collective-permute-done.6.mine2 = f32[544,128]{1,0:T(8,128)S(1)} collective-permute-done((f32[544,128]{1,0:T(8,128)S(1)}, f32[544,128]{1,0:T(8,128)S(1)}, u32[]{:S(2)}, u32[]{:S(2)}) %collective-permute-start.6) | collective-permute-done | bytes 278560 | tf_op jit(solution)/shard_map/ppermute | solution.py:62
  65.3 0.8 collective-permute-done.5.mine1
  66.1 1.0 %pad_maximum_fusion = f32[1632,128]{1,0:T(8,128)} fusion(f32[544,128]{1,0:T(8,128)S(1)} %collective-permute-done.7.mine3, f32[544,128]{1,0:T(8,128)S(1)} %collective-permute-done.6.mine2, f32[544,128]{1,0:T(8,128)S(1)} %collective-permute-done.5.mine1), kind=kLoop, calls=%fused_computation | loop fusion | flops 417792 | bytes 1671168 | tf_op jit(solution)/shard_map/concatenate | solution.py:264
  67.0 3.3 %collective-permute-start.8 = (f32[1632,128]{1,0:T(8,128)}, f32[1632,128]{1,0:T(8,128)}, u32[]{:S(2)}, u32[]{:S(2)}) collective-permute-start(f32[1632,128]{1,0:T(8,128)} %pad_maximum_fusion), channel_id=1, source_target_pairs={{0,16},{16,0},{32,48},{48,32},{64,80},{80,64},{96,112},{112,96},{1... | collective-permute-start | bytes 2506760 | tf_op jit(solution)/shard_map/ppermute | solution.py:62
  70.3 1.9 %collective-permute-start.4 = (f32[544,128]{1,0:T(8,128)S(1)}, f32[544,128]{1,0:T(8,128)S(1)}, u32[]{:S(2)}, u32[]{:S(2)}) collective-permute-start(f32[544,128]{1,0:T(8,128)S(1)} %constant_dynamic-update-slice_fusion.mine0), channel_id=1, source_target_pairs={{0,16},{16,0},{32,48},{48,32},{64,80},{80,64},{96,112},{112,96},{1... | collective-permute-start | bytes 835592 | tf_op jit(solution)/shard_map/ppermute | solution.py:62
  72.3 0.0 copy-start
  72.3 1.3 %copy-done = f32[16,64,512]{2,1,0:T(8,128)} copy-done((f32[16,64,512]{2,1,0:T(8,128)}, f32[16,64,512]{2,1,0:T(8,128)S(1)}, u32[]{:S(2)}) %copy-start) | copy-done | bytes 2097176
  73.6 4.3 %shard_map.78 = (bf16[512,512]{1,0:T(8,128)(2,1)}, bf16[512,512]{1,0:T(8,128)(2,1)}) custom-call(f32[16,64,512]{2,1,0:T(8,128)} %copy-done), custom_call_target="tpu_custom_call" | custom-call | tf_op jit(solution)/shard_map/pallas_call | solution.py:223
  78.0 4.7 %shard_map.79 = (f32[512,1024]{1,0:T(8,128)}, f32[512,128]{1,0:T(8,128)}) custom-call(bf16[512,512]{1,0:T(8,128)(2,1)} %get-tuple-element.8.w_high, bf16[512,512]{1,0:T(8,128)(2,1)} %get-tuple-element.9.w_low, f32[544,128]{1,0:T(8,128)} %copy-done.4, f32[544,128]{1,0:T(8,128)} %copy-done.3, f32[544,128]{1,0:T(8,128)} %copy-done.2, f32[544,128]{1,0:T(8,128)} %copy-done.1, ...), custom_call_target="tpu_custom_call" | custom-call | tf_op jit(solution)/shard_map/pallas_call | solution.py:223
  82.8 0.7 copy-done.5
  83.5 5.3 %shard_map.80 = (f32[512,1024]{1,0:T(8,128)}, f32[64,512]{1,0:T(8,128)}) custom-call(bf16[512,512]{1,0:T(8,128)(2,1)} %get-tuple-element.8.w_high, bf16[512,512]{1,0:T(8,128)(2,1)} %get-tuple-element.9.w_low, f32[544,128]{1,0:T(8,128)} %copy-done.5, f32[1632,128]{1,0:T(8,128)} %collective-permute-done.8.others, ...), custom_call_target="tpu_custom_call", output_to_operand_aliasing={{0}: (5, {})} | custom-call | tf_op jit(solution)/shard_map/pallas_call | solution.py:223
  (22 shorter events, 0.1 us)
Async XLA Ops:
  0.6 22.4 %collective-permute-start = (f32[32,512]{1,0:T(8,128)}, f32[32,512]{1,0:T(8,128)S(1)}, u32[]{:S(2)}, u32[]{:S(2)}) collective-permute-start(f32[32,512]{1,0:T(8,128)} %panel.1), channel_id=1, source_target_pairs={{0,256},{16,272},{32,353},{48,369},{64,482},{80,498},{96,291},{112... | collective-permute-start | bytes 196616 | tf_op jit(solution)/shard_map/ppermute | solution.py:62
  19.2 3.8 %copy-start.6 = (f32[16,64]{1,0:T(8,128)S(1)}, f32[16,64]{1,0:T(8,128)}, u32[]{:S(2)}) copy-start(f32[16,64]{1,0:T(8,128)} %param.10) | copy-start | bytes 12292
  19.2 53.0 %all-to-all-start = ((f32[16,64,512]{2,1,0:T(8,128)}), f32[16,64,512]{2,1,0:T(8,128)S(1)}, u32[]{:S(2)}, u32[]{:S(2)}) async-start(f32[16,64,512]{2,1,0:T(8,128)} %shard_map.77), calls=%async_computation | async-start | bytes 4194304 | tf_op jit(solution)/shard_map/all_to_all | solution.py:251
  23.1 24.7 %collective-permute-start.3 = (f32[136,128]{1,0:T(8,128)S(1)}, f32[136,128]{1,0:T(8,128)S(1)}, u32[]{:S(2)}, u32[]{:S(2)}) collective-permute-start(f32[136,128]{1,0:T(8,128)S(1)} %maximum_maximum_fusion), channel_id=1, source_target_pairs={{0,256},{16,272},{32,288},{48,304},{64,320},{80,336},{96,352},{112... | collective-permute-start | bytes 208904 | tf_op jit(solution)/shard_map/ppermute | solution.py:62
  32.9 14.9 %collective-permute-start.2 = (f32[136,128]{1,0:T(8,128)S(1)}, f32[136,128]{1,0:T(8,128)S(1)}, u32[]{:S(2)}, u32[]{:S(2)}) collective-permute-start(f32[136,128]{1,0:T(8,128)S(1)} %maximum_maximum_fusion), channel_id=1, source_target_pairs={{0,384},{16,400},{32,416},{48,432},{64,448},{80,464},{96,480},{112... | collective-permute-start | bytes 208904 | tf_op jit(solution)/shard_map/ppermute | solution.py:62
  35.3 9.3 %collective-permute-start.1 = (f32[136,128]{1,0:T(8,128)S(1)}, f32[136,128]{1,0:T(8,128)S(1)}, u32[]{:S(2)}, u32[]{:S(2)}) collective-permute-start(f32[136,128]{1,0:T(8,128)S(1)} %maximum_maximum_fusion), channel_id=1, source_target_pairs={{0,128},{16,144},{32,160},{48,176},{64,192},{80,208},{96,224},{112... | collective-permute-start | bytes 208904 | tf_op jit(solution)/shard_map/ppermute | solution.py:62
  47.8 30.1 %copy-start.4 = (f32[544,128]{1,0:T(8,128)}, f32[544,128]{1,0:T(8,128)S(1)}, u32[]{:S(2)}) copy-start(f32[544,128]{1,0:T(8,128)S(1)} %constant_dynamic-update-slice_fusion.mine0) | copy-start | bytes 835588
  47.8 10.3 %collective-permute-start.7 = (f32[544,128]{1,0:T(8,128)S(1)}, f32[544,128]{1,0:T(8,128)S(1)}, u32[]{:S(2)}, u32[]{:S(2)}) collective-permute-start(f32[544,128]{1,0:T(8,128)S(1)} %constant_dynamic-update-slice_fusion.mine0), channel_id=1, source_target_pairs={{0,64},{16,464},{32,96},{48,496},{64,128},{80,16},{96,160},{112,48... | collective-permute-start | bytes 835592 | tf_op jit(solution)/shard_map/ppermute | solution.py:62
  50.3 15.0 %collective-permute-start.6 = (f32[544,128]{1,0:T(8,128)S(1)}, f32[544,128]{1,0:T(8,128)S(1)}, u32[]{:S(2)}, u32[]{:S(2)}) collective-permute-start(f32[544,128]{1,0:T(8,128)S(1)} %constant_dynamic-update-slice_fusion.mine0), channel_id=1, source_target_pairs={{0,480},{16,496},{32,0},{48,16},{64,32},{80,48},{96,64},{112,80},{... | collective-permute-start | bytes 835592 | tf_op jit(solution)/shard_map/ppermute | solution.py:62
  55.0 11.1 %collective-permute-start.5 = (f32[544,128]{1,0:T(8,128)S(1)}, f32[544,128]{1,0:T(8,128)S(1)}, u32[]{:S(2)}, u32[]{:S(2)}) collective-permute-start(f32[544,128]{1,0:T(8,128)S(1)} %constant_dynamic-update-slice_fusion.mine0), channel_id=1, source_target_pairs={{0,32},{16,48},{32,64},{48,80},{64,96},{80,112},{96,128},{112,144}... | collective-permute-start | bytes 835592 | tf_op jit(solution)/shard_map/ppermute | solution.py:62
  58.1 19.8 %copy-start.1 = (f32[544,128]{1,0:T(8,128)}, f32[544,128]{1,0:T(8,128)S(1)}, u32[]{:S(2)}) copy-start(f32[544,128]{1,0:T(8,128)S(1)} %collective-permute-done.7.mine3) | copy-start | bytes 835588
  65.3 12.7 %copy-start.2 = (f32[544,128]{1,0:T(8,128)}, f32[544,128]{1,0:T(8,128)S(1)}, u32[]{:S(2)}) copy-start(f32[544,128]{1,0:T(8,128)S(1)} %collective-permute-done.6.mine2) | copy-start | bytes 835588
  66.1 11.9 %copy-start.3 = (f32[544,128]{1,0:T(8,128)}, f32[544,128]{1,0:T(8,128)S(1)}, u32[]{:S(2)}) copy-start(f32[544,128]{1,0:T(8,128)S(1)} %collective-permute-done.5.mine1) | copy-start | bytes 835588
  67.0 15.7 %collective-permute-start.8 = (f32[1632,128]{1,0:T(8,128)}, f32[1632,128]{1,0:T(8,128)}, u32[]{:S(2)}, u32[]{:S(2)}) collective-permute-start(f32[1632,128]{1,0:T(8,128)} %pad_maximum_fusion), channel_id=1, source_target_pairs={{0,16},{16,0},{32,48},{48,32},{64,80},{80,64},{96,112},{112,96},{1... | collective-permute-start | bytes 2506760 | tf_op jit(solution)/shard_map/ppermute | solution.py:62
  70.3 12.4 %collective-permute-start.4 = (f32[544,128]{1,0:T(8,128)S(1)}, f32[544,128]{1,0:T(8,128)S(1)}, u32[]{:S(2)}, u32[]{:S(2)}) collective-permute-start(f32[544,128]{1,0:T(8,128)S(1)} %constant_dynamic-update-slice_fusion.mine0), channel_id=1, source_target_pairs={{0,16},{16,0},{32,48},{48,32},{64,80},{80,64},{96,112},{112,96},{1... | collective-permute-start | bytes 835592 | tf_op jit(solution)/shard_map/ppermute | solution.py:62
  72.3 1.3 %copy-start = (f32[16,64,512]{2,1,0:T(8,128)}, f32[16,64,512]{2,1,0:T(8,128)S(1)}, u32[]{:S(2)}) copy-start(f32[16,64,512]{2,1,0:T(8,128)S(1)} %all-to-all-done.gathered) | copy-start | bytes 6291460
  82.7 0.7 copy-start.5

commit v5 on v4

v5 whole, which is shorter than its diff:
```python
import jax
import jax.numpy as jnp
from jax import lax
from jax.experimental import pallas as pl
from jax.experimental.pallas import tpu as pltpu
from jax.sharding import PartitionSpec as P


AXES = ("row", "col")
X, Y, Z, CORES = 4, 4, 16, 2
NT = (((1,), (1,)), ((), ()))
NN = (((1,), (0,)), ((), ()))


def device(x, y, z, k):
    return ((z % Z) * CORES + k) * (X * Y) + (x % X) * Y + y % Y


def pairs(move):
    out = []
    for x in range(X):
        for y in range(Y):
            for z in range(Z):
                for k in range(CORES):
                    out.append((device(x, y, z, k), device(*move(x, y, z, k))))
    return out


STEPS = {
    8: (0, 0),
    7: (1, 0), 9: (3, 0), 6: (0, 1), 10: (0, 3),
    5: (1, 1), 11: (1, 3), 4: (3, 1), 12: (3, 3), 3: (2, 0), 13: (0, 2),
    2: (2, 1), 14: (2, 3), 1: (1, 2), 15: (3, 2),
    0: (2, 2),
}
PLACES = {place: step for step, place in STEPS.items()}


def table(axis):
    bits = sum(STEPS[step][axis] << (2 * step) for step in range(Z))
    return bits - (1 << 32) if bits >> 31 else bits


TABLE_X, TABLE_Y = table(0), table(1)


def transpose_move(x, y, z, k):
    cx, cy = z // Y, z % Y
    return cx, cy, z + PLACES[(x - cx) % X, (y - cy) % Y], k


TURN = pairs(transpose_move)
SWAP = pairs(lambda x, y, z, k: (x, y, z, 1 - k))
PM2 = pairs(lambda x, y, z, k: (x, y, z + 2 if k == 0 else z - 2, k))


def shift(d):
    return pairs(lambda x, y, z, k: (x, y, z + d, k))


def send(array, moves):
    return lax.ppermute(array, AXES, moves)


def fast(array):
    return pltpu.with_memory_space_constraint(array, pltpu.VMEM)


def split(x):
    high = x.astype(jnp.bfloat16)
    return high, (x - high.astype(jnp.float32)).astype(jnp.bfloat16)


def dot3(a, b, dims):
    ah, al = a
    bh, bl = b
    dot = lambda u, v: lax.dot_general(u, v, dims, preferred_element_type=jnp.float32)
    return dot(ah, bh) + (dot(ah, bl) + dot(al, bh))


def weight_body(gathered, out_high, out_low):
    inverse = split(gathered[:, 32:64, :].reshape(512, 512))
    solved = dot3(split(gathered[:, 0:32, :].reshape(512, 512)), inverse, NN)
    high, low = split(dot3(split(solved), inverse, NT))
    out_high[...] = high
    out_low[...] = low


OFFSETS = (0, -4, 4, 8)


def where_am_i():
    row = lax.axis_index("row")
    return row, lax.axis_index("col"), row // 2, row % 2


def place(ref, base, group, core, z, col, high, low, fold):
    for slot in range(4):
        step = OFFSETS[slot]
        far = (0, -1, 1)[group] + step if group < 3 else step - 2 + 4 * core
        at = (z + far + 32) & 15
        hop = 2 * ((at - col) & 15)
        px = (col // 4 + (jnp.int32(TABLE_X) >> hop)) & 3
        py = (col + (jnp.int32(TABLE_Y) >> hop)) & 3
        rows = pl.ds(pl.multiple_of(32 * (4 * px + py), 32), 32)
        start = base + 136 * slot
        for j in range(4):
            tiles = [ref[start + 8 * (4 * i + j):start + 8 * (4 * i + j) + 8, :] for i in range(4)]
            h, l = split(jnp.concatenate(tiles, 0))
            high[rows, 128 * j:128 * j + 128] = h
            low[rows, 128 * j:128 * j + 128] = l
        tile = ref[start + 128:start + 136, :]
        first = pl.multiple_of(16 * (2 * at + core), 16)
        fold[pl.ds(first, 8), :] = tile
        fold[pl.ds(first + 8, 8), :] = pltpu.roll(tile, 64, 1)


def update(half, w, cols, vin, vout, out, sems, row, col):
    lower = 2 * col + half <= row
    copies = []
    for n in range(2):
        part = slice(256 * n, 256 * n + 256)
        span = pl.ds(pl.multiple_of(512 * half + 256 * n, 256), 256)

        @pl.when(lower)
        def _():
            block = tuple(c[part, :] for c in cols)
            vout[:, part] = vin[:, span] - dot3(w, block, NT)

        @pl.when(jnp.logical_not(lower))
        def _():
            vout[:, part] = vin[:, span]

        copy = pltpu.make_async_copy(vout.at[:, part], out.at[:, span], sems.at[n])
        copy.start()
        copies.append(copy)
    return copies


def begin(copies):
    for copy in copies:
        copy.start()


def end(copies):
    for copy in copies:
        copy.wait()


def first_body(wh, wl, vin, mine0, mine1, mine2, mine3, out, fold, high, low, vout, sems):
    row, col, z, k = where_am_i()
    for group, ref in enumerate((mine0, mine1, mine2, mine3)):
        place(ref, 0, group, k, z, col, high, low, fold)
    end(update(k, (wh[...], wl[...]), (high, low), vin, vout, out, sems, row, col))


def second_body(wh, wl, vin, others, half_fold, series, length, part, out, out_s, high, low, vout, fold, vsout, sems):
    row, col, z, k = where_am_i()
    for group in range(4):
        place(others, 544 * group, group, 1 - k, z, col, high, low, fold)
    w = (wh[...], wl[...])
    writes = update(1 - k, w, (high, low), vin, vout, out, sems.at[0:2], row, col)
    for at in range(16):
        rows = pl.ds(pl.multiple_of(32 * at + 16 * k, 16), 16)
        fold[rows, :] = half_fold[rows, :]
    correction = dot3(w, split(fold[...]), NN)
    lengths = jnp.concatenate([length[...], length[...]], 1)
    correction = jnp.where(row < lengths, correction, 0.0)
    vsout[...] = series[...] - correction.T[0:64, :]
    last = pltpu.make_async_copy(vsout, out_s, sems.at[2])
    begin([last])
    end(writes + [last])


def spread_body(panel, stripe, out, stage, sems):
    loads = [
        pltpu.make_async_copy(panel, stage.at[0:32, :], sems.at[16]),
        pltpu.make_async_copy(stripe, stage.at[32:64, :], sems.at[17]),
    ]
    begin(loads)
    end(loads)
    copies = [pltpu.make_async_copy(stage, out.at[c], sems.at[c]) for c in range(16)]
    begin(copies)
    end(copies)


VMEM = pl.BlockSpec(memory_space=pltpu.VMEM)
ANY = pl.BlockSpec(memory_space=pl.ANY)


def shape(*dims, dtype=jnp.float32):
    return jax.ShapeDtypeStruct(dims, dtype)


def kernel(body, out, memory, outs, scratch=(), alias=None, room=24):
    specs = {"v": VMEM, "a": ANY}
    out_specs = tuple(specs[m] for m in outs) if len(outs) > 1 else specs[outs]
    limit = room << 20 if room else None

    def call(*args):
        args = [fast(a) if m == "v" else a for a, m in zip(args, memory)]
        return pl.pallas_call(
            body,
            out_shape=out,
            in_specs=[specs[m] for m in memory],
            out_specs=out_specs,
            scratch_shapes=list(scratch),
            input_output_aliases=alias or {},
            compiler_params=pltpu.CompilerParams(vmem_limit_bytes=limit),
        )(*args)

    return call


def block(*dims, dtype=jnp.float32):
    return pltpu.VMEM(dims, dtype)


def sems(n):
    return pltpu.SemaphoreType.DMA((n,))


def tile_order(chunk):
    return chunk.reshape(4, 8, 4, 128).transpose(0, 2, 1, 3).reshape(128, 128)


def step(trailing, panel, inv_factor, later_series, fold_series, fold_len):
    half = jnp.bfloat16
    chunk = tile_order(send(panel, TURN))
    load = kernel(
        spread_body, shape(16, 64, 512), "aa", "a", [block(64, 512), sems(18)], room=0
    )(panel, inv_factor.T)
    gathered = lax.all_to_all(load, "col", 0, 0, tiled=True)
    fold = jnp.concatenate([fold_series[0:8], fold_series[8:16]], 1)
    base = jnp.concatenate([chunk, fold], 0)
    near = jnp.concatenate([base] + [send(base, shift(d)) for d in (4, -4, 8)], 0)
    mine = [near, send(near, shift(1)), send(near, shift(-1)), send(near, PM2)]
    halves = (shape(512, 512, dtype=half), shape(512, 512, dtype=half))
    weight = kernel(weight_body, halves, "v", "vv")(gathered)
    held = lax.optimization_barrier(near)
    others = send(jnp.concatenate([held] + mine[1:], 0), SWAP)
    square = block(512, 512, dtype=half)
    work = [square, square, block(512, 512)]
    part, half_fold = kernel(
        first_body, (shape(512, 1024), shape(512, 128)), "vvvvvvv", "av", work + [sems(2)]
    )(*weight, trailing, *mine)
    out, series = kernel(
        second_body,
        (shape(512, 1024), shape(64, 512)),
        "vvvvvvva",
        "aa",
        work + [block(512, 128), block(64, 512), sems(3)],
        {7: 0},
    )(*weight, trailing, others, half_fold, later_series.T, fold_len[None, :], part)
    return out, series.T


def solution(mesh):
    in_specs = (
        P("row", "col"),
        P(("row", "col"), None),
        P(None, "col"),
        P("row", "col"),
        P("row", "col"),
        P("col"),
    )
    out_specs = (P("row", "col"), P("row", "col"))
    return jax.shard_map(step, mesh=mesh, in_specs=in_specs, out_specs=out_specs, check_vma=False)
```

time: 89.3 us -> 81.7 us (0.915)
  Pallas kernels: 16.7 us -> 12.1 us
  local copies, waits for them, and re-layouts: 2.08 us -> 0.05 us
    pallas_call x4, Pallas kernels: 16.7 us -> 12.1 us  [call(): pl.pallas_call(body, out_shape=out, in_specs=[specs[m] for m in memory],...]
    unnamed x17 -> x11, local copies, waits for them, and re-layouts: 2.07 us -> 0.04 us
    ppermute x9 -> x8, starting transfers between devices: 50.7 us -> 49.2 us  [send(): return lax.ppermute(array, AXES, moves)]
    ppermute x9 -> x8, waiting for transfers between devices: 13.6 us -> 13.4 us  [send(): return lax.ppermute(array, AXES, moves)]
  transfers between devices with their start and end apart: 10 -> 9, of which waited for: 4 -> 4; matrix products, arithmetic and copies ran while one was open for 1% -> 2% of each run, Pallas kernels for 13% -> 10%
where the time goes in v5:
time: 81.7 us; the launch traced here: 81.2 us
  starting transfers between devices  53.6 us (66%)
  waiting for transfers between devices  13.4 us (16%)
  Pallas kernels  12.1 us (15%)
  other arithmetic  1.22 us (1%)
  between operations  0.84 us (1%)
    ppermute x8, starting transfers between devices, send(): return lax.ppermute(array, AXES, moves)  49.2 us
    ppermute x8, waiting for transfers between devices, send(): return lax.ppermute(array, AXES, moves)  13.4 us
    pallas_call x4, Pallas kernels, call(): pl.pallas_call(body, out_shape=out, in_specs=[specs[m] for m in memory],...  12.1 us
    all_to_all x1, starting transfers between devices, step(): gathered = lax.all_to_all(load, 'col', 0, 0, tiled=True)  4.45 us
  transfers between devices with their start and end apart: 9, of which 4 were waited for; matrix products, arithmetic and copies ran while one was open for 2% of the time, Pallas kernels for 10%

profile of v5, /device:TPU:1, one launch (start us, length us, event | category | flops | bytes accessed | tf_op | source)
XLA Modules:
  0.0 81.2 jit_solution(11289342510452275493)
XLA Ops:
  0.6 16.3 %collective-permute-start = (f32[32,512]{1,0:T(8,128)}, f32[32,512]{1,0:T(8,128)S(1)}, u32[]{:S(2)}, u32[]{:S(2)}) collective-permute-start(f32[32,512]{1,0:T(8,128)} %panel.1), channel_id=1, source_target_pairs={{0,256},{16,272},{32,353},{48,369},{64,482},{80,498},{96,291},{112... | collective-permute-start | bytes 196616 | tf_op jit(solution)/shard_map/ppermute | solution.py:62
  16.9 2.3 %shard_map.77 = f32[16,64,512]{2,1,0:T(8,128)} custom-call(f32[32,512]{1,0:T(8,128)} %panel.1, f32[32,512]{1,0:T(8,128)} %bitcast.13), custom_call_target="tpu_custom_call" | custom-call | tf_op jit(solution)/shard_map/pallas_call | solution.py:202
  19.2 0.0 copy-start.3
  19.2 4.5 %all-to-all-start = ((f32[16,64,512]{2,1,0:T(8,128)}), f32[16,64,512]{2,1,0:T(8,128)}, u32[]{:S(2)}, u32[]{:S(2)}) async-start(f32[16,64,512]{2,1,0:T(8,128)} %shard_map.77), calls=%async_computation | async-start | bytes 4194304 | tf_op jit(solution)/shard_map/all_to_all | solution.py:233
  23.7 0.1 maximum_maximum_fusion
  23.8 9.0 %collective-permute-start.3 = (f32[136,128]{1,0:T(8,128)S(1)}, f32[136,128]{1,0:T(8,128)S(1)}, u32[]{:S(2)}, u32[]{:S(2)}) collective-permute-start(f32[136,128]{1,0:T(8,128)S(1)} %maximum_maximum_fusion), channel_id=1, source_target_pairs={{0,256},{16,272},{32,288},{48,304},{64,320},{80,336},{96,352},{112... | collective-permute-start | bytes 208904 | tf_op jit(solution)/shard_map/ppermute | solution.py:62
  32.9 2.4 %collective-permute-start.2 = (f32[136,128]{1,0:T(8,128)S(1)}, f32[136,128]{1,0:T(8,128)S(1)}, u32[]{:S(2)}, u32[]{:S(2)}) collective-permute-start(f32[136,128]{1,0:T(8,128)S(1)} %maximum_maximum_fusion), channel_id=1, source_target_pairs={{0,384},{16,400},{32,416},{48,432},{64,448},{80,464},{96,480},{112... | collective-permute-start | bytes 208904 | tf_op jit(solution)/shard_map/ppermute | solution.py:62
  35.3 6.7 %collective-permute-start.1 = (f32[136,128]{1,0:T(8,128)S(1)}, f32[136,128]{1,0:T(8,128)S(1)}, u32[]{:S(2)}, u32[]{:S(2)}) collective-permute-start(f32[136,128]{1,0:T(8,128)S(1)} %maximum_maximum_fusion), channel_id=1, source_target_pairs={{0,128},{16,144},{32,160},{48,176},{64,192},{80,208},{96,224},{112... | collective-permute-start | bytes 208904 | tf_op jit(solution)/shard_map/ppermute | solution.py:62
  42.1 0.1 constant_dynamic-update-slice_fusion.3
  42.2 2.4 %collective-permute-done.1 = f32[136,128]{1,0:T(8,128)S(1)} collective-permute-done((f32[136,128]{1,0:T(8,128)S(1)}, f32[136,128]{1,0:T(8,128)S(1)}, u32[]{:S(2)}, u32[]{:S(2)}) %collective-permute-start.1) | collective-permute-done | bytes 69664 | tf_op jit(solution)/shard_map/ppermute | solution.py:62
  44.5 3.4 %collective-permute-done.2 = f32[136,128]{1,0:T(8,128)S(1)} collective-permute-done((f32[136,128]{1,0:T(8,128)S(1)}, f32[136,128]{1,0:T(8,128)S(1)}, u32[]{:S(2)}, u32[]{:S(2)}) %collective-permute-start.2) | collective-permute-done | bytes 69664 | tf_op jit(solution)/shard_map/ppermute | solution.py:62
  48.0 2.8 %collective-permute-start.6 = (f32[544,128]{1,0:T(8,128)S(1)}, f32[544,128]{1,0:T(8,128)S(1)}, u32[]{:S(2)}, u32[]{:S(2)}) collective-permute-start(f32[544,128]{1,0:T(8,128)S(1)} %constant_dynamic-update-slice_fusion.mine0), channel_id=1, source_target_pairs={{0,64},{16,464},{32,96},{48,496},{64,128},{80,16},{96,160},{112,48... | collective-permute-start | bytes 835592 | tf_op jit(solution)/shard_map/ppermute | solution.py:62
  50.8 5.3 %collective-permute-start.5 = (f32[544,128]{1,0:T(8,128)S(1)}, f32[544,128]{1,0:T(8,128)S(1)}, u32[]{:S(2)}, u32[]{:S(2)}) collective-permute-start(f32[544,128]{1,0:T(8,128)S(1)} %constant_dynamic-update-slice_fusion.mine0), channel_id=1, source_target_pairs={{0,480},{16,496},{32,0},{48,16},{64,32},{80,48},{96,64},{112,80},{... | collective-permute-start | bytes 835592 | tf_op jit(solution)/shard_map/ppermute | solution.py:62
  56.1 3.1 %collective-permute-start.4 = (f32[544,128]{1,0:T(8,128)S(1)}, f32[544,128]{1,0:T(8,128)S(1)}, u32[]{:S(2)}, u32[]{:S(2)}) collective-permute-start(f32[544,128]{1,0:T(8,128)S(1)} %constant_dynamic-update-slice_fusion.mine0), channel_id=1, source_target_pairs={{0,32},{16,48},{32,64},{48,80},{64,96},{80,112},{96,128},{112,144}... | collective-permute-start | bytes 835592 | tf_op jit(solution)/shard_map/ppermute | solution.py:62
  59.2 6.6 %collective-permute-done.5.mine2 = f32[544,128]{1,0:T(8,128)S(1)} collective-permute-done((f32[544,128]{1,0:T(8,128)S(1)}, f32[544,128]{1,0:T(8,128)S(1)}, u32[]{:S(2)}, u32[]{:S(2)}) %collective-permute-start.5) | collective-permute-done | bytes 278560 | tf_op jit(solution)/shard_map/ppermute | solution.py:62
  65.7 1.0 %collective-permute-done.4.mine1 = f32[544,128]{1,0:T(8,128)S(1)} collective-permute-done((f32[544,128]{1,0:T(8,128)S(1)}, f32[544,128]{1,0:T(8,128)S(1)}, u32[]{:S(2)}, u32[]{:S(2)}) %collective-permute-start.4) | collective-permute-done | bytes 278560 | tf_op jit(solution)/shard_map/ppermute | solution.py:62
  66.7 1.1 %pad_maximum_fusion = f32[2176,128]{1,0:T(8,128)} fusion(f32[544,128]{1,0:T(8,128)S(1)} %collective-permute-done.6.mine3, f32[544,128]{1,0:T(8,128)S(1)} %collective-permute-done.5.mine2, f32[544,128]{1,0:T(8,128)S(1)} %collective-permute-done.4.mine1, f32[544,128]{1,0:T(8,128)S(1)} %constant_dynamic-update-slice_fusion.mine0), kind=kLoop, calls=%fused_computation | loop fusion | flops 835584 | bytes 2228224 | tf_op jit(solution)/shard_map/concatenate | solution.py:241
  67.8 3.5 %collective-permute-start.7 = (f32[2176,128]{1,0:T(8,128)}, f32[2176,128]{1,0:T(8,128)}, u32[]{:S(2)}, u32[]{:S(2)}) collective-permute-start(f32[2176,128]{1,0:T(8,128)} %pad_maximum_fusion), channel_id=1, source_target_pairs={{0,16},{16,0},{32,48},{48,32},{64,80},{80,64},{96,112},{112,96},{1... | collective-permute-start | bytes 3342344 | tf_op jit(solution)/shard_map/ppermute | solution.py:62
  71.3 0.0 all-to-all-done.gathered
  71.3 3.4 %shard_map.78 = (bf16[512,512]{1,0:T(8,128)(2,1)S(1)}, bf16[512,512]{1,0:T(8,128)(2,1)S(1)}) custom-call(f32[16,64,512]{2,1,0:T(8,128)} %all-to-all-done.gathered), custom_call_target="tpu_custom_call" | custom-call | tf_op jit(solution)/shard_map/pallas_call | solution.py:202
  74.8 0.0 copy-start.1
  74.8 0.0 copy-start.2
  74.8 2.3 %shard_map.79 = (f32[512,1024]{1,0:T(8,128)}, f32[512,128]{1,0:T(8,128)S(1)}) custom-call(bf16[512,512]{1,0:T(8,128)(2,1)S(1)} %get-tuple-element.8.wh, bf16[512,512]{1,0:T(8,128)(2,1)S(1)} %get-tuple-element.9.wl, f32[512,1024]{1,0:T(8,128)S(1)} %copy-done, f32[544,128]{1,0:T(8,128)S(1)} %constant_dynamic-update-slice_fusion.mine0, ...), custom_call_target="tpu_custom_call" | custom-call | tf_op jit(solution)/shard_map/pallas_call | solution.py:202
  77.1 4.1 %shard_map.80 = (f32[512,1024]{1,0:T(8,128)}, f32[64,512]{1,0:T(8,128)}) custom-call(bf16[512,512]{1,0:T(8,128)(2,1)S(1)} %get-tuple-element.8.wh, bf16[512,512]{1,0:T(8,128)(2,1)S(1)} %get-tuple-element.9.wl, f32[512,1024]{1,0:T(8,128)S(1)} %copy-done, f32[2176,128]{1,0:T(8,128)} %collective-permute-done.7.others, ...), custom_call_target="tpu_custom_call", output_to_operand_aliasing={{0}: (7, {})} | custom-call | tf_op jit(solution)/shard_map/pallas_call | solution.py:202
  (14 shorter events, 0.0 us)
Async XLA Ops:
  0.6 23.1 %collective-permute-start = (f32[32,512]{1,0:T(8,128)}, f32[32,512]{1,0:T(8,128)S(1)}, u32[]{:S(2)}, u32[]{:S(2)}) collective-permute-start(f32[32,512]{1,0:T(8,128)} %panel.1), channel_id=1, source_target_pairs={{0,256},{16,272},{32,353},{48,369},{64,482},{80,498},{96,291},{112... | collective-permute-start | bytes 196616 | tf_op jit(solution)/shard_map/ppermute | solution.py:62
  19.2 4.5 %copy-start.3 = (f32[16,64]{1,0:T(8,128)S(1)}, f32[16,64]{1,0:T(8,128)}, u32[]{:S(2)}) copy-start(f32[16,64]{1,0:T(8,128)} %param.10) | copy-start | bytes 12292
  19.2 52.1 %all-to-all-start = ((f32[16,64,512]{2,1,0:T(8,128)}), f32[16,64,512]{2,1,0:T(8,128)}, u32[]{:S(2)}, u32[]{:S(2)}) async-start(f32[16,64,512]{2,1,0:T(8,128)} %shard_map.77), calls=%async_computation | async-start | bytes 4194304 | tf_op jit(solution)/shard_map/all_to_all | solution.py:233
  23.8 24.2 %collective-permute-start.3 = (f32[136,128]{1,0:T(8,128)S(1)}, f32[136,128]{1,0:T(8,128)S(1)}, u32[]{:S(2)}, u32[]{:S(2)}) collective-permute-start(f32[136,128]{1,0:T(8,128)S(1)} %maximum_maximum_fusion), channel_id=1, source_target_pairs={{0,256},{16,272},{32,288},{48,304},{64,320},{80,336},{96,352},{112... | collective-permute-start | bytes 208904 | tf_op jit(solution)/shard_map/ppermute | solution.py:62
  32.9 15.1 %collective-permute-start.2 = (f32[136,128]{1,0:T(8,128)S(1)}, f32[136,128]{1,0:T(8,128)S(1)}, u32[]{:S(2)}, u32[]{:S(2)}) collective-permute-start(f32[136,128]{1,0:T(8,128)S(1)} %maximum_maximum_fusion), channel_id=1, source_target_pairs={{0,384},{16,400},{32,416},{48,432},{64,448},{80,464},{96,480},{112... | collective-permute-start | bytes 208904 | tf_op jit(solution)/shard_map/ppermute | solution.py:62
  35.3 9.2 %collective-permute-start.1 = (f32[136,128]{1,0:T(8,128)S(1)}, f32[136,128]{1,0:T(8,128)S(1)}, u32[]{:S(2)}, u32[]{:S(2)}) collective-permute-start(f32[136,128]{1,0:T(8,128)S(1)} %maximum_maximum_fusion), channel_id=1, source_target_pairs={{0,128},{16,144},{32,160},{48,176},{64,192},{80,208},{96,224},{112... | collective-permute-start | bytes 208904 | tf_op jit(solution)/shard_map/ppermute | solution.py:62
  48.0 11.2 %collective-permute-start.6 = (f32[544,128]{1,0:T(8,128)S(1)}, f32[544,128]{1,0:T(8,128)S(1)}, u32[]{:S(2)}, u32[]{:S(2)}) collective-permute-start(f32[544,128]{1,0:T(8,128)S(1)} %constant_dynamic-update-slice_fusion.mine0), channel_id=1, source_target_pairs={{0,64},{16,464},{32,96},{48,496},{64,128},{80,16},{96,160},{112,48... | collective-permute-start | bytes 835592 | tf_op jit(solution)/shard_map/ppermute | solution.py:62
  50.8 14.9 %collective-permute-start.5 = (f32[544,128]{1,0:T(8,128)S(1)}, f32[544,128]{1,0:T(8,128)S(1)}, u32[]{:S(2)}, u32[]{:S(2)}) collective-permute-start(f32[544,128]{1,0:T(8,128)S(1)} %constant_dynamic-update-slice_fusion.mine0), channel_id=1, source_target_pairs={{0,480},{16,496},{32,0},{48,16},{64,32},{80,48},{96,64},{112,80},{... | collective-permute-start | bytes 835592 | tf_op jit(solution)/shard_map/ppermute | solution.py:62
  56.1 10.7 %collective-permute-start.4 = (f32[544,128]{1,0:T(8,128)S(1)}, f32[544,128]{1,0:T(8,128)S(1)}, u32[]{:S(2)}, u32[]{:S(2)}) collective-permute-start(f32[544,128]{1,0:T(8,128)S(1)} %constant_dynamic-update-slice_fusion.mine0), channel_id=1, source_target_pairs={{0,32},{16,48},{32,64},{48,80},{64,96},{80,112},{96,128},{112,144}... | collective-permute-start | bytes 835592 | tf_op jit(solution)/shard_map/ppermute | solution.py:62
  67.8 6.9 %copy-start = (f32[512,1024]{1,0:T(8,128)S(1)}, f32[512,1024]{1,0:T(8,128)}, u32[]{:S(2)}) copy-start(f32[512,1024]{1,0:T(8,128)} %vin.3) | copy-start | bytes 6291460
  67.8 9.3 %collective-permute-start.7 = (f32[2176,128]{1,0:T(8,128)}, f32[2176,128]{1,0:T(8,128)}, u32[]{:S(2)}, u32[]{:S(2)}) collective-permute-start(f32[2176,128]{1,0:T(8,128)} %pad_maximum_fusion), channel_id=1, source_target_pairs={{0,16},{16,0},{32,48},{48,32},{64,80},{80,64},{96,112},{112,96},{1... | collective-permute-start | bytes 3342344 | tf_op jit(solution)/shard_map/ppermute | solution.py:62
  74.8 2.3 %copy-start.1 = (f32[512,64]{0,1:T(8,128)S(1)}, f32[512,64]{0,1:T(8,128)}, u32[]{:S(2)}) copy-start(f32[512,64]{0,1:T(8,128)} %param.9) | copy-start | bytes 393220
  74.8 2.3 %copy-start.2 = (s32[64]{0:T(128)S(1)}, s32[64]{0:T(128)}, u32[]{:S(2)}) copy-start(s32[64]{0:T(128)} %param.11) | copy-start | bytes 772

commit v6 on v5

--- a/solution.py
+++ b/solution.py
@@ -51,11 +51,10 @@
 
 TURN = pairs(transpose_move)
 SWAP = pairs(lambda x, y, z, k: (x, y, z, 1 - k))
-PM2 = pairs(lambda x, y, z, k: (x, y, z + 2 if k == 0 else z - 2, k))
-
-
-def shift(d):
-    return pairs(lambda x, y, z, k: (x, y, z + d, k))
+
+
+def onward(d):
+    return pairs(lambda x, y, z, k: (x, y, z + d if k == 0 else z - d, k))
 
 
 def send(array, moves):
@@ -86,7 +85,8 @@
     out_low[...] = low
 
 
-OFFSETS = (0, -4, 4, 8)
+BEYOND = (0, -4, 4, -8)
+AROUND = (0, -1, 1, -2)
 
 
 def where_am_i():
@@ -96,9 +96,8 @@
 
 def place(ref, base, group, core, z, col, high, low, fold):
     for slot in range(4):
-        step = OFFSETS[slot]
-        far = (0, -1, 1)[group] + step if group < 3 else step - 2 + 4 * core
-        at = (z + far + 32) & 15
+        way = 1 - 2 * core
+        at = (z + way * (AROUND[group] + BEYOND[slot]) + 32) & 15
         hop = 2 * ((at - col) & 15)
         px = (col // 4 + (jnp.int32(TABLE_X) >> hop)) & 3
         py = (col + (jnp.int32(TABLE_Y) >> hop)) & 3
@@ -233,8 +232,12 @@
     gathered = lax.all_to_all(load, "col", 0, 0, tiled=True)
     fold = jnp.concatenate([fold_series[0:8], fold_series[8:16]], 1)
     base = jnp.concatenate([chunk, fold], 0)
-    near = jnp.concatenate([base] + [send(base, shift(d)) for d in (4, -4, 8)], 0)
-    mine = [near, send(near, shift(1)), send(near, shift(-1)), send(near, PM2)]
+    behind = send(base, onward(4))
+    ahead = send(base, onward(-4))
+    near = jnp.concatenate([base, behind, ahead, send(behind, onward(4))], 0)
+    behind = send(near, onward(1))
+    ahead = send(near, onward(-1))
+    mine = [near, behind, ahead, send(behind, onward(1))]
     halves = (shape(512, 512, dtype=half), shape(512, 512, dtype=half))
     weight = kernel(weight_body, halves, "v", "vv")(gathered)
     held = lax.optimization_barrier(near)

time: 81.7 us -> 100 us (1.22)
  the two profiles are of different devices: /device:TPU:1 before, /device:TPU:32 now
where the time goes in v6:
time: 100 us; the launch traced here: 99.5 us
  starting transfers between devices  48 us (48%)
  waiting for transfers between devices  36.6 us (37%)
  Pallas kernels  12.1 us (12%)
  other arithmetic  1.22 us (1%)
    ppermute x8, starting transfers between devices, send(): return lax.ppermute(array, AXES, moves)  40 us
    ppermute x8, waiting for transfers between devices, send(): return lax.ppermute(array, AXES, moves)  23.8 us
    all_to_all x1, waiting for transfers between devices, step(): gathered = lax.all_to_all(load, 'col', 0, 0, tiled=True)  12.9 us
    pallas_call x4, Pallas kernels, call(): pl.pallas_call(body, out_shape=out, in_specs=[specs[m] for m in memory],...  12.1 us
    all_to_all x1, starting transfers between devices, step(): gathered = lax.all_to_all(load, 'col', 0, 0, tiled=True)  8.04 us
  transfers between devices with their start and end apart: 9, of which 6 were waited for; matrix products, arithmetic and copies ran while one was open for 2% of the time, Pallas kernels for 8%

profile of v6, /device:TPU:32, one launch (start us, length us, event | category | flops | bytes accessed | tf_op | source)
XLA Modules:
  0.0 99.5 jit_solution(17443647459826403638)
XLA Ops:
  0.6 14.9 %collective-permute-start = (f32[32,512]{1,0:T(8,128)}, f32[32,512]{1,0:T(8,128)S(1)}, u32[]{:S(2)}, u32[]{:S(2)}) collective-permute-start(f32[32,512]{1,0:T(8,128)} %panel.1), channel_id=1, source_target_pairs={{0,256},{16,272},{32,353},{48,369},{64,482},{80,498},{96,291},{112... | collective-permute-start | bytes 196616 | tf_op jit(solution)/shard_map/ppermute | solution.py:61
  15.6 0.7 fusion
  16.3 3.3 %collective-permute-done = f32[32,512]{1,0:T(8,128)S(1)} collective-permute-done((f32[32,512]{1,0:T(8,128)}, f32[32,512]{1,0:T(8,128)S(1)}, u32[]{:S(2)}, u32[]{:S(2)}) %collective-permute-start) | collective-permute-done | bytes 65568 | tf_op jit(solution)/shard_map/ppermute | solution.py:61
  19.6 0.1 maximum_maximum_fusion
  19.7 4.6 %collective-permute-start.2 = (f32[136,128]{1,0:T(8,128)S(1)}, f32[136,128]{1,0:T(8,128)S(1)}, u32[]{:S(2)}, u32[]{:S(2)}) collective-permute-start(f32[136,128]{1,0:T(8,128)S(1)} %maximum_maximum_fusion), channel_id=1, source_target_pairs={{0,384},{16,144},{32,416},{48,176},{64,448},{80,208},{96,480},{112... | collective-permute-start | bytes 208904 | tf_op jit(solution)/shard_map/ppermute | solution.py:61
  24.3 5.1 %collective-permute-start.1 = (f32[136,128]{1,0:T(8,128)S(1)}, f32[136,128]{1,0:T(8,128)S(1)}, u32[]{:S(2)}, u32[]{:S(2)}) collective-permute-start(f32[136,128]{1,0:T(8,128)S(1)} %maximum_maximum_fusion), channel_id=1, source_target_pairs={{0,128},{16,400},{32,160},{48,432},{64,192},{80,464},{96,224},{112... | collective-permute-start | bytes 208904 | tf_op jit(solution)/shard_map/ppermute | solution.py:61
  29.4 0.1 constant_dynamic-update-slice_fusion.3
  29.5 7.4 %collective-permute-done.1 = f32[136,128]{1,0:T(8,128)S(1)} collective-permute-done((f32[136,128]{1,0:T(8,128)S(1)}, f32[136,128]{1,0:T(8,128)S(1)}, u32[]{:S(2)}, u32[]{:S(2)}) %collective-permute-start.1) | collective-permute-done | bytes 69664 | tf_op jit(solution)/shard_map/ppermute | solution.py:61
  36.9 3.4 %collective-permute-start.3 = (f32[136,128]{1,0:T(8,128)S(1)}, f32[136,128]{1,0:T(8,128)S(1)}, u32[]{:S(2)}, u32[]{:S(2)}) collective-permute-start(f32[136,128]{1,0:T(8,128)S(1)} %collective-permute-done.1), channel_id=1, source_target_pairs={{0,128},{16,400},{32,160},{48,432},{64,192},{80,464},{96,224},{112... | collective-permute-start | bytes 208904 | tf_op jit(solution)/shard_map/ppermute | solution.py:61
  40.4 8.2 %collective-permute-done.3 = f32[136,128]{1,0:T(8,128)S(1)} collective-permute-done((f32[136,128]{1,0:T(8,128)S(1)}, f32[136,128]{1,0:T(8,128)S(1)}, u32[]{:S(2)}, u32[]{:S(2)}) %collective-permute-start.3) | collective-permute-done | bytes 69664 | tf_op jit(solution)/shard_map/ppermute | solution.py:61
  48.6 4.0 %collective-permute-start.4 = (f32[544,128]{1,0:T(8,128)S(1)}, f32[544,128]{1,0:T(8,128)S(1)}, u32[]{:S(2)}, u32[]{:S(2)}) collective-permute-start(f32[544,128]{1,0:T(8,128)S(1)} %constant_dynamic-update-slice_fusion.mine0), channel_id=1, source_target_pairs={{0,32},{16,496},{32,64},{48,16},{64,96},{80,48},{96,128},{112,80},... | collective-permute-start | bytes 835592 | tf_op jit(solution)/shard_map/ppermute | solution.py:61
  52.7 2.3 %shard_map.77 = f32[16,64,512]{2,1,0:T(8,128)} custom-call(f32[32,512]{1,0:T(8,128)} %panel.1, f32[32,512]{1,0:T(8,128)} %bitcast.13), custom_call_target="tpu_custom_call" | custom-call | tf_op jit(solution)/shard_map/pallas_call | solution.py:201
  55.0 8.0 %all-to-all-start = ((f32[16,64,512]{2,1,0:T(8,128)}), f32[16,64,512]{2,1,0:T(8,128)}, u32[]{:S(2)}, u32[]{:S(2)}) async-start(f32[16,64,512]{2,1,0:T(8,128)} %shard_map.77), calls=%async_computation | async-start | bytes 4194304 | tf_op jit(solution)/shard_map/all_to_all | solution.py:232
  63.0 1.9 %collective-permute-start.5 = (f32[544,128]{1,0:T(8,128)S(1)}, f32[544,128]{1,0:T(8,128)S(1)}, u32[]{:S(2)}, u32[]{:S(2)}) collective-permute-start(f32[544,128]{1,0:T(8,128)S(1)} %constant_dynamic-update-slice_fusion.mine0), channel_id=1, source_target_pairs={{0,480},{16,48},{32,0},{48,80},{64,32},{80,112},{96,64},{112,144},... | collective-permute-start | bytes 835592 | tf_op jit(solution)/shard_map/ppermute | solution.py:61
  65.0 3.9 %collective-permute-start.6 = (f32[544,128]{1,0:T(8,128)S(1)}, f32[544,128]{1,0:T(8,128)S(1)}, u32[]{:S(2)}, u32[]{:S(2)}) collective-permute-start(f32[544,128]{1,0:T(8,128)S(1)} %collective-permute-done.4.mine1), channel_id=1, source_target_pairs={{0,32},{16,496},{32,64},{48,16},{64,96},{80,48},{96,128},{112,80},... | collective-permute-start | bytes 835592 | tf_op jit(solution)/shard_map/ppermute | solution.py:61
  68.9 4.0 %collective-permute-done.5.mine2 = f32[544,128]{1,0:T(8,128)S(1)} collective-permute-done((f32[544,128]{1,0:T(8,128)S(1)}, f32[544,128]{1,0:T(8,128)S(1)}, u32[]{:S(2)}, u32[]{:S(2)}) %collective-permute-start.5) | collective-permute-done | bytes 278560 | tf_op jit(solution)/shard_map/ppermute | solution.py:61
  72.9 0.8 collective-permute-done.6.mine3
  73.7 1.1 %pad_maximum_fusion = f32[2176,128]{1,0:T(8,128)} fusion(f32[544,128]{1,0:T(8,128)S(1)} %collective-permute-done.6.mine3, f32[544,128]{1,0:T(8,128)S(1)} %collective-permute-done.5.mine2, f32[544,128]{1,0:T(8,128)S(1)} %collective-permute-done.4.mine1, f32[544,128]{1,0:T(8,128)S(1)} %constant_dynamic-update-slice_fusion.mine0), kind=kLoop, calls=%fused_computation | loop fusion | flops 835584 | bytes 2228224 | tf_op jit(solution)/shard_map/concatenate | solution.py:244
  74.8 2.0 %collective-permute-start.7 = (f32[2176,128]{1,0:T(8,128)}, f32[2176,128]{1,0:T(8,128)}, u32[]{:S(2)}, u32[]{:S(2)}) collective-permute-start(f32[2176,128]{1,0:T(8,128)} %pad_maximum_fusion), channel_id=1, source_target_pairs={{0,16},{16,0},{32,48},{48,32},{64,80},{80,64},{96,112},{112,96},{1... | collective-permute-start | bytes 3342344 | tf_op jit(solution)/shard_map/ppermute | solution.py:61
  76.8 12.9 %all-to-all-done.gathered = f32[16,64,512]{2,1,0:T(8,128)} async-done(((f32[16,64,512]{2,1,0:T(8,128)}), f32[16,64,512]{2,1,0:T(8,128)}, u32[]{:S(2)}, u32[]{:S(2)}) %all-to-all-start) | async-done | bytes 2097184 | tf_op jit(solution)/shard_map/all_to_all | solution.py:232
  89.7 3.4 %shard_map.78 = (bf16[512,512]{1,0:T(8,128)(2,1)S(1)}, bf16[512,512]{1,0:T(8,128)(2,1)S(1)}) custom-call(f32[16,64,512]{2,1,0:T(8,128)} %all-to-all-done.gathered), custom_call_target="tpu_custom_call" | custom-call | tf_op jit(solution)/shard_map/pallas_call | solution.py:201
  93.1 0.0 copy-start.1
  93.1 2.3 %shard_map.79 = (f32[512,1024]{1,0:T(8,128)}, f32[512,128]{1,0:T(8,128)S(1)}) custom-call(bf16[512,512]{1,0:T(8,128)(2,1)S(1)} %get-tuple-element.8.wh, bf16[512,512]{1,0:T(8,128)(2,1)S(1)} %get-tuple-element.9.wl, f32[512,1024]{1,0:T(8,128)S(1)} %copy-done, f32[544,128]{1,0:T(8,128)S(1)} %constant_dynamic-update-slice_fusion.mine0, ...), custom_call_target="tpu_custom_call" | custom-call | tf_op jit(solution)/shard_map/pallas_call | solution.py:201
  95.5 4.1 %shard_map.80 = (f32[512,1024]{1,0:T(8,128)}, f32[64,512]{1,0:T(8,128)}) custom-call(bf16[512,512]{1,0:T(8,128)(2,1)S(1)} %get-tuple-element.8.wh, bf16[512,512]{1,0:T(8,128)(2,1)S(1)} %get-tuple-element.9.wl, f32[512,1024]{1,0:T(8,128)S(1)} %copy-done, f32[2176,128]{1,0:T(8,128)} %collective-permute-done.7.others, ...), custom_call_target="tpu_custom_call", output_to_operand_aliasing={{0}: (7, {})} | custom-call | tf_op jit(solution)/shard_map/pallas_call | solution.py:201
  (12 shorter events, 0.0 us)
Async XLA Ops:
  0.6 19.0 %collective-permute-start = (f32[32,512]{1,0:T(8,128)}, f32[32,512]{1,0:T(8,128)S(1)}, u32[]{:S(2)}, u32[]{:S(2)}) collective-permute-start(f32[32,512]{1,0:T(8,128)} %panel.1), channel_id=1, source_target_pairs={{0,256},{16,272},{32,353},{48,369},{64,482},{80,498},{96,291},{112... | collective-permute-start | bytes 196616 | tf_op jit(solution)/shard_map/ppermute | solution.py:61
  19.7 20.7 %collective-permute-start.2 = (f32[136,128]{1,0:T(8,128)S(1)}, f32[136,128]{1,0:T(8,128)S(1)}, u32[]{:S(2)}, u32[]{:S(2)}) collective-permute-start(f32[136,128]{1,0:T(8,128)S(1)} %maximum_maximum_fusion), channel_id=1, source_target_pairs={{0,384},{16,144},{32,416},{48,176},{64,448},{80,208},{96,480},{112... | collective-permute-start | bytes 208904 | tf_op jit(solution)/shard_map/ppermute | solution.py:61
  24.3 12.6 %collective-permute-start.1 = (f32[136,128]{1,0:T(8,128)S(1)}, f32[136,128]{1,0:T(8,128)S(1)}, u32[]{:S(2)}, u32[]{:S(2)}) collective-permute-start(f32[136,128]{1,0:T(8,128)S(1)} %maximum_maximum_fusion), channel_id=1, source_target_pairs={{0,128},{16,400},{32,160},{48,432},{64,192},{80,464},{96,224},{112... | collective-permute-start | bytes 208904 | tf_op jit(solution)/shard_map/ppermute | solution.py:61
  36.9 11.7 %collective-permute-start.3 = (f32[136,128]{1,0:T(8,128)S(1)}, f32[136,128]{1,0:T(8,128)S(1)}, u32[]{:S(2)}, u32[]{:S(2)}) collective-permute-start(f32[136,128]{1,0:T(8,128)S(1)} %collective-permute-done.1), channel_id=1, source_target_pairs={{0,128},{16,400},{32,160},{48,432},{64,192},{80,464},{96,224},{112... | collective-permute-start | bytes 208904 | tf_op jit(solution)/shard_map/ppermute | solution.py:61
  48.6 16.3 %collective-permute-start.4 = (f32[544,128]{1,0:T(8,128)S(1)}, f32[544,128]{1,0:T(8,128)S(1)}, u32[]{:S(2)}, u32[]{:S(2)}) collective-permute-start(f32[544,128]{1,0:T(8,128)S(1)} %constant_dynamic-update-slice_fusion.mine0), channel_id=1, source_target_pairs={{0,32},{16,496},{32,64},{48,16},{64,96},{80,48},{96,128},{112,80},... | collective-permute-start | bytes 835592 | tf_op jit(solution)/shard_map/ppermute | solution.py:61
  55.0 34.7 %all-to-all-start = ((f32[16,64,512]{2,1,0:T(8,128)}), f32[16,64,512]{2,1,0:T(8,128)}, u32[]{:S(2)}, u32[]{:S(2)}) async-start(f32[16,64,512]{2,1,0:T(8,128)} %shard_map.77), calls=%async_computation | async-start | bytes 4194304 | tf_op jit(solution)/shard_map/all_to_all | solution.py:232
  63.0 9.9 %collective-permute-start.5 = (f32[544,128]{1,0:T(8,128)S(1)}, f32[544,128]{1,0:T(8,128)S(1)}, u32[]{:S(2)}, u32[]{:S(2)}) collective-permute-start(f32[544,128]{1,0:T(8,128)S(1)} %constant_dynamic-update-slice_fusion.mine0), channel_id=1, source_target_pairs={{0,480},{16,48},{32,0},{48,80},{64,32},{80,112},{96,64},{112,144},... | collective-permute-start | bytes 835592 | tf_op jit(solution)/shard_map/ppermute | solution.py:61
  65.0 8.7 %collective-permute-start.6 = (f32[544,128]{1,0:T(8,128)S(1)}, f32[544,128]{1,0:T(8,128)S(1)}, u32[]{:S(2)}, u32[]{:S(2)}) collective-permute-start(f32[544,128]{1,0:T(8,128)S(1)} %collective-permute-done.4.mine1), channel_id=1, source_target_pairs={{0,32},{16,496},{32,64},{48,16},{64,96},{80,48},{96,128},{112,80},... | collective-permute-start | bytes 835592 | tf_op jit(solution)/shard_map/ppermute | solution.py:61
  74.8 18.3 %copy-start = (f32[512,1024]{1,0:T(8,128)S(1)}, f32[512,1024]{1,0:T(8,128)}, u32[]{:S(2)}) copy-start(f32[512,1024]{1,0:T(8,128)} %vin.3) | copy-start | bytes 6291460
  74.8 20.7 %collective-permute-start.7 = (f32[2176,128]{1,0:T(8,128)}, f32[2176,128]{1,0:T(8,128)}, u32[]{:S(2)}, u32[]{:S(2)}) collective-permute-start(f32[2176,128]{1,0:T(8,128)} %pad_maximum_fusion), channel_id=1, source_target_pairs={{0,16},{16,0},{32,48},{48,32},{64,80},{80,64},{96,112},{112,96},{1... | collective-permute-start | bytes 3342344 | tf_op jit(solution)/shard_map/ppermute | solution.py:61
  93.1 2.3 %copy-start.1 = (f32[512,64]{0,1:T(8,128)S(1)}, f32[512,64]{0,1:T(8,128)}, u32[]{:S(2)}) copy-start(f32[512,64]{0,1:T(8,128)} %param.9) | copy-start | bytes 393220
  93.1 2.3 %copy-start.2 = (s32[64]{0:T(128)S(1)}, s32[64]{0:T(128)}, u32[]{:S(2)}) copy-start(s32[64]{0:T(128)} %param.11) | copy-start | bytes 772

commit v7 on v5

--- a/solution.py
+++ b/solution.py
@@ -54,8 +54,9 @@
 PM2 = pairs(lambda x, y, z, k: (x, y, z + 2 if k == 0 else z - 2, k))
 
 
-def shift(d):
-    return pairs(lambda x, y, z, k: (x, y, z + d, k))
+def shift(d, core=None):
+    every = pairs(lambda x, y, z, k: (x, y, z + d, k))
+    return [p for p in every if core is None or p[0] // (X * Y) % CORES == core]
 
 
 def send(array, moves):
@@ -233,7 +234,11 @@
     gathered = lax.all_to_all(load, "col", 0, 0, tiled=True)
     fold = jnp.concatenate([fold_series[0:8], fold_series[8:16]], 1)
     base = jnp.concatenate([chunk, fold], 0)
-    near = jnp.concatenate([base] + [send(base, shift(d)) for d in (4, -4, 8)], 0)
+    across = send(base, shift(8, 0))
+    ahead = send(base, shift(-4))
+    behind = send(base, shift(4))
+    across = across + send(ahead, shift(-4, 1))
+    near = jnp.concatenate([base, behind, ahead, across], 0)
     mine = [near, send(near, shift(1)), send(near, shift(-1)), send(near, PM2)]
     halves = (shape(512, 512, dtype=half), shape(512, 512, dtype=half))
     weight = kernel(weight_body, halves, "v", "vv")(gathered)

time: 81.7 us -> 81.1 us (level)
  starting transfers between devices: 53.6 us -> 47.7 us
  waiting for transfers between devices: 13.4 us -> 18.7 us
    ppermute x8 -> x9, starting transfers between devices: 49.2 us -> 43.3 us  [send(): return lax.ppermute(array, AXES, moves)]
    ppermute x8 -> x9, waiting for transfers between devices: 13.4 us -> 18.7 us  [send(): return lax.ppermute(array, AXES, moves)]
  transfers between devices with their start and end apart: 9 -> 10, of which waited for: 4 -> 5; matrix products, arithmetic and copies ran while one was open for 2% -> 2% of each run, Pallas kernels for 10% -> 10%
where the time goes in v7:
time: 81.1 us; the launch traced here: 80.6 us
  starting transfers between devices  47.7 us (59%)
  waiting for transfers between devices  18.7 us (23%)
  Pallas kernels  12.1 us (15%)
  other arithmetic  1.23 us (2%)
  between operations  0.87 us (1%)
    ppermute x9, starting transfers between devices, send(): return lax.ppermute(array, AXES, moves)  43.3 us
    ppermute x9, waiting for transfers between devices, send(): return lax.ppermute(array, AXES, moves)  18.7 us
    pallas_call x4, Pallas kernels, call(): pl.pallas_call(body, out_shape=out, in_specs=[specs[m] for m in memory],...  12.1 us
    all_to_all x1, starting transfers between devices, step(): gathered = lax.all_to_all(load, 'col', 0, 0, tiled=True)  4.47 us
  transfers between devices with their start and end apart: 10, of which 5 were waited for; matrix products, arithmetic and copies ran while one was open for 2% of the time, Pallas kernels for 10%

profile of v7, /device:TPU:1, one launch (start us, length us, event | category | flops | bytes accessed | tf_op | source)
XLA Modules:
  0.0 80.6 jit_solution(13286161496060883848)
XLA Ops:
  0.6 16.3 %collective-permute-start = (f32[32,512]{1,0:T(8,128)}, f32[32,512]{1,0:T(8,128)S(1)}, u32[]{:S(2)}, u32[]{:S(2)}) collective-permute-start(f32[32,512]{1,0:T(8,128)} %panel.1), channel_id=1, source_target_pairs={{0,256},{16,272},{32,353},{48,369},{64,482},{80,498},{96,291},{112... | collective-permute-start | bytes 196616 | tf_op jit(solution)/shard_map/ppermute | solution.py:63
  16.9 2.3 %shard_map.77 = f32[16,64,512]{2,1,0:T(8,128)} custom-call(f32[32,512]{1,0:T(8,128)} %panel.1, f32[32,512]{1,0:T(8,128)} %bitcast.13), custom_call_target="tpu_custom_call" | custom-call | tf_op jit(solution)/shard_map/pallas_call | solution.py:203
  19.2 0.0 copy-start.3
  19.2 4.5 %all-to-all-start = ((f32[16,64,512]{2,1,0:T(8,128)}), f32[16,64,512]{2,1,0:T(8,128)}, u32[]{:S(2)}, u32[]{:S(2)}) async-start(f32[16,64,512]{2,1,0:T(8,128)} %shard_map.77), calls=%async_computation | async-start | bytes 4194304 | tf_op jit(solution)/shard_map/all_to_all | solution.py:234
  23.8 0.1 maximum_maximum_fusion
  23.8 0.7 collective-permute-start.3
  24.5 4.7 %collective-permute-start.2 = (f32[136,128]{1,0:T(8,128)S(1)}, f32[136,128]{1,0:T(8,128)S(1)}, u32[]{:S(2)}, u32[]{:S(2)}) collective-permute-start(f32[136,128]{1,0:T(8,128)S(1)} %maximum_maximum_fusion), channel_id=1, source_target_pairs={{0,384},{16,400},{32,416},{48,432},{64,448},{80,464},{96,480},{112... | collective-permute-start | bytes 208904 | tf_op jit(solution)/shard_map/ppermute | solution.py:63
  29.1 4.5 %collective-permute-start.1 = (f32[136,128]{1,0:T(8,128)S(1)}, f32[136,128]{1,0:T(8,128)S(1)}, u32[]{:S(2)}, u32[]{:S(2)}) collective-permute-start(f32[136,128]{1,0:T(8,128)S(1)} %maximum_maximum_fusion), channel_id=1, source_target_pairs={{0,128},{16,144},{32,160},{48,176},{64,192},{80,208},{96,224},{112... | collective-permute-start | bytes 208904 | tf_op jit(solution)/shard_map/ppermute | solution.py:63
  33.7 0.1 constant_dynamic-update-slice_fusion.2
  33.8 0.6 collective-permute-done.2
  34.4 4.0 %collective-permute-start.4 = (f32[136,128]{1,0:T(8,128)S(1)}, f32[136,128]{1,0:T(8,128)S(1)}, u32[]{:S(2)}, u32[]{:S(2)}) collective-permute-start(f32[136,128]{1,0:T(8,128)S(1)} %collective-permute-done.2), channel_id=1, source_target_pairs={{16,400},{48,432},{80,464},{112,496},{144,16},{176,48},{208,80},{2... | collective-permute-start | bytes 208904 | tf_op jit(solution)/shard_map/ppermute | solution.py:63
  38.5 9.5 %collective-permute-done.4 = f32[136,128]{1,0:T(8,128)S(1)} collective-permute-done((f32[136,128]{1,0:T(8,128)S(1)}, f32[136,128]{1,0:T(8,128)S(1)}, u32[]{:S(2)}, u32[]{:S(2)}) %collective-permute-start.4) | collective-permute-done | bytes 69664 | tf_op jit(solution)/shard_map/ppermute | solution.py:63
  48.0 3.6 %collective-permute-start.7 = (f32[544,128]{1,0:T(8,128)S(1)}, f32[544,128]{1,0:T(8,128)S(1)}, u32[]{:S(2)}, u32[]{:S(2)}) collective-permute-start(f32[544,128]{1,0:T(8,128)S(1)} %add_dynamic-update-slice_fusion.mine0), channel_id=1, source_target_pairs={{0,64},{16,464},{32,96},{48,496},{64,128},{80,16},{96,160},{112,48... | collective-permute-start | bytes 835592 | tf_op jit(solution)/shard_map/ppermute | solution.py:63
  51.6 1.9 %collective-permute-start.6 = (f32[544,128]{1,0:T(8,128)S(1)}, f32[544,128]{1,0:T(8,128)S(1)}, u32[]{:S(2)}, u32[]{:S(2)}) collective-permute-start(f32[544,128]{1,0:T(8,128)S(1)} %add_dynamic-update-slice_fusion.mine0), channel_id=1, source_target_pairs={{0,480},{16,496},{32,0},{48,16},{64,32},{80,48},{96,64},{112,80},{... | collective-permute-start | bytes 835592 | tf_op jit(solution)/shard_map/ppermute | solution.py:63
  53.6 3.4 %collective-permute-start.5 = (f32[544,128]{1,0:T(8,128)S(1)}, f32[544,128]{1,0:T(8,128)S(1)}, u32[]{:S(2)}, u32[]{:S(2)}) collective-permute-start(f32[544,128]{1,0:T(8,128)S(1)} %add_dynamic-update-slice_fusion.mine0), channel_id=1, source_target_pairs={{0,32},{16,48},{32,64},{48,80},{64,96},{80,112},{96,128},{112,144}... | collective-permute-start | bytes 835592 | tf_op jit(solution)/shard_map/ppermute | solution.py:63
  56.9 2.3 %collective-permute-done.7.mine3 = f32[544,128]{1,0:T(8,128)S(1)} collective-permute-done((f32[544,128]{1,0:T(8,128)S(1)}, f32[544,128]{1,0:T(8,128)S(1)}, u32[]{:S(2)}, u32[]{:S(2)}) %collective-permute-start.7) | collective-permute-done | bytes 278560 | tf_op jit(solution)/shard_map/ppermute | solution.py:63
  59.2 5.8 %collective-permute-done.6.mine2 = f32[544,128]{1,0:T(8,128)S(1)} collective-permute-done((f32[544,128]{1,0:T(8,128)S(1)}, f32[544,128]{1,0:T(8,128)S(1)}, u32[]{:S(2)}, u32[]{:S(2)}) %collective-permute-start.6) | collective-permute-done | bytes 278560 | tf_op jit(solution)/shard_map/ppermute | solution.py:63
  65.0 0.5 collective-permute-done.5.mine1
  65.4 1.1 %pad_maximum_fusion = f32[2176,128]{1,0:T(8,128)} fusion(f32[544,128]{1,0:T(8,128)S(1)} %collective-permute-done.7.mine3, f32[544,128]{1,0:T(8,128)S(1)} %collective-permute-done.6.mine2, f32[544,128]{1,0:T(8,128)S(1)} %collective-permute-done.5.mine1, f32[544,128]{1,0:T(8,128)S(1)} %add_dynamic-update-slice_fusion.mine0), kind=kLoop, calls=%fused_computation | loop fusion | flops 835584 | bytes 2228224 | tf_op jit(solution)/shard_map/concatenate | solution.py:246
  66.5 4.3 %collective-permute-start.8 = (f32[2176,128]{1,0:T(8,128)}, f32[2176,128]{1,0:T(8,128)}, u32[]{:S(2)}, u32[]{:S(2)}) collective-permute-start(f32[2176,128]{1,0:T(8,128)} %pad_maximum_fusion), channel_id=1, source_target_pairs={{0,16},{16,0},{32,48},{48,32},{64,80},{80,64},{96,112},{112,96},{1... | collective-permute-start | bytes 3342344 | tf_op jit(solution)/shard_map/ppermute | solution.py:63
  70.8 3.4 %shard_map.78 = (bf16[512,512]{1,0:T(8,128)(2,1)S(1)}, bf16[512,512]{1,0:T(8,128)(2,1)S(1)}) custom-call(f32[16,64,512]{2,1,0:T(8,128)} %all-to-all-done.gathered), custom_call_target="tpu_custom_call" | custom-call | tf_op jit(solution)/shard_map/pallas_call | solution.py:203
  74.2 0.0 copy-start.1
  74.2 2.3 %shard_map.79 = (f32[512,1024]{1,0:T(8,128)}, f32[512,128]{1,0:T(8,128)S(1)}) custom-call(bf16[512,512]{1,0:T(8,128)(2,1)S(1)} %get-tuple-element.8.wh, bf16[512,512]{1,0:T(8,128)(2,1)S(1)} %get-tuple-element.9.wl, f32[512,1024]{1,0:T(8,128)S(1)} %copy-done, f32[544,128]{1,0:T(8,128)S(1)} %add_dynamic-update-slice_fusion.mine0, ...), custom_call_target="tpu_custom_call" | custom-call | tf_op jit(solution)/shard_map/pallas_call | solution.py:203
  76.5 4.1 %shard_map.80 = (f32[512,1024]{1,0:T(8,128)}, f32[64,512]{1,0:T(8,128)}) custom-call(bf16[512,512]{1,0:T(8,128)(2,1)S(1)} %get-tuple-element.8.wh, bf16[512,512]{1,0:T(8,128)(2,1)S(1)} %get-tuple-element.9.wl, f32[512,1024]{1,0:T(8,128)S(1)} %copy-done, f32[2176,128]{1,0:T(8,128)} %collective-permute-done.8.others, ...), custom_call_target="tpu_custom_call", output_to_operand_aliasing={{0}: (7, {})} | custom-call | tf_op jit(solution)/shard_map/pallas_call | solution.py:203
  (16 shorter events, 0.1 us)
Async XLA Ops:
  0.6 23.1 %collective-permute-start = (f32[32,512]{1,0:T(8,128)}, f32[32,512]{1,0:T(8,128)S(1)}, u32[]{:S(2)}, u32[]{:S(2)}) collective-permute-start(f32[32,512]{1,0:T(8,128)} %panel.1), channel_id=1, source_target_pairs={{0,256},{16,272},{32,353},{48,369},{64,482},{80,498},{96,291},{112... | collective-permute-start | bytes 196616 | tf_op jit(solution)/shard_map/ppermute | solution.py:63
  19.2 4.5 %copy-start.3 = (f32[16,64]{1,0:T(8,128)S(1)}, f32[16,64]{1,0:T(8,128)}, u32[]{:S(2)}) copy-start(f32[16,64]{1,0:T(8,128)} %param.10) | copy-start | bytes 12292
  19.2 51.5 %all-to-all-start = ((f32[16,64,512]{2,1,0:T(8,128)}), f32[16,64,512]{2,1,0:T(8,128)}, u32[]{:S(2)}, u32[]{:S(2)}) async-start(f32[16,64,512]{2,1,0:T(8,128)} %shard_map.77), calls=%async_computation | async-start | bytes 4194304 | tf_op jit(solution)/shard_map/all_to_all | solution.py:234
  23.8 14.7 %collective-permute-start.3 = (f32[136,128]{1,0:T(8,128)S(1)}, f32[136,128]{1,0:T(8,128)S(1)}, u32[]{:S(2)}, u32[]{:S(2)}) collective-permute-start(f32[136,128]{1,0:T(8,128)S(1)} %maximum_maximum_fusion), channel_id=1, source_target_pairs={{0,256},{32,288},{64,320},{96,352},{128,384},{160,416},{192,448},{... | collective-permute-start | bytes 208904 | tf_op jit(solution)/shard_map/ppermute | solution.py:63
  24.5 9.9 %collective-permute-start.2 = (f32[136,128]{1,0:T(8,128)S(1)}, f32[136,128]{1,0:T(8,128)S(1)}, u32[]{:S(2)}, u32[]{:S(2)}) collective-permute-start(f32[136,128]{1,0:T(8,128)S(1)} %maximum_maximum_fusion), channel_id=1, source_target_pairs={{0,384},{16,400},{32,416},{48,432},{64,448},{80,464},{96,480},{112... | collective-permute-start | bytes 208904 | tf_op jit(solution)/shard_map/ppermute | solution.py:63
  29.1 9.3 %collective-permute-start.1 = (f32[136,128]{1,0:T(8,128)S(1)}, f32[136,128]{1,0:T(8,128)S(1)}, u32[]{:S(2)}, u32[]{:S(2)}) collective-permute-start(f32[136,128]{1,0:T(8,128)S(1)} %maximum_maximum_fusion), channel_id=1, source_target_pairs={{0,128},{16,144},{32,160},{48,176},{64,192},{80,208},{96,224},{112... | collective-permute-start | bytes 208904 | tf_op jit(solution)/shard_map/ppermute | solution.py:63
  34.4 13.6 %collective-permute-start.4 = (f32[136,128]{1,0:T(8,128)S(1)}, f32[136,128]{1,0:T(8,128)S(1)}, u32[]{:S(2)}, u32[]{:S(2)}) collective-permute-start(f32[136,128]{1,0:T(8,128)S(1)} %collective-permute-done.2), channel_id=1, source_target_pairs={{16,400},{48,432},{80,464},{112,496},{144,16},{176,48},{208,80},{2... | collective-permute-start | bytes 208904 | tf_op jit(solution)/shard_map/ppermute | solution.py:63
  48.0 11.2 %collective-permute-start.7 = (f32[544,128]{1,0:T(8,128)S(1)}, f32[544,128]{1,0:T(8,128)S(1)}, u32[]{:S(2)}, u32[]{:S(2)}) collective-permute-start(f32[544,128]{1,0:T(8,128)S(1)} %add_dynamic-update-slice_fusion.mine0), channel_id=1, source_target_pairs={{0,64},{16,464},{32,96},{48,496},{64,128},{80,16},{96,160},{112,48... | collective-permute-start | bytes 835592 | tf_op jit(solution)/shard_map/ppermute | solution.py:63
  51.6 13.3 %collective-permute-start.6 = (f32[544,128]{1,0:T(8,128)S(1)}, f32[544,128]{1,0:T(8,128)S(1)}, u32[]{:S(2)}, u32[]{:S(2)}) collective-permute-start(f32[544,128]{1,0:T(8,128)S(1)} %add_dynamic-update-slice_fusion.mine0), channel_id=1, source_target_pairs={{0,480},{16,496},{32,0},{48,16},{64,32},{80,48},{96,64},{112,80},{... | collective-permute-start | bytes 835592 | tf_op jit(solution)/shard_map/ppermute | solution.py:63
  53.6 11.9 %collective-permute-start.5 = (f32[544,128]{1,0:T(8,128)S(1)}, f32[544,128]{1,0:T(8,128)S(1)}, u32[]{:S(2)}, u32[]{:S(2)}) collective-permute-start(f32[544,128]{1,0:T(8,128)S(1)} %add_dynamic-update-slice_fusion.mine0), channel_id=1, source_target_pairs={{0,32},{16,48},{32,64},{48,80},{64,96},{80,112},{96,128},{112,144}... | collective-permute-start | bytes 835592 | tf_op jit(solution)/shard_map/ppermute | solution.py:63
  66.5 7.7 %copy-start = (f32[512,1024]{1,0:T(8,128)S(1)}, f32[512,1024]{1,0:T(8,128)}, u32[]{:S(2)}) copy-start(f32[512,1024]{1,0:T(8,128)} %vin.3) | copy-start | bytes 6291460
  66.5 10.0 %collective-permute-start.8 = (f32[2176,128]{1,0:T(8,128)}, f32[2176,128]{1,0:T(8,128)}, u32[]{:S(2)}, u32[]{:S(2)}) collective-permute-start(f32[2176,128]{1,0:T(8,128)} %pad_maximum_fusion), channel_id=1, source_target_pairs={{0,16},{16,0},{32,48},{48,32},{64,80},{80,64},{96,112},{112,96},{1... | collective-permute-start | bytes 3342344 | tf_op jit(solution)/shard_map/ppermute | solution.py:63
  74.2 2.3 %copy-start.1 = (f32[512,64]{0,1:T(8,128)S(1)}, f32[512,64]{0,1:T(8,128)}, u32[]{:S(2)}) copy-start(f32[512,64]{0,1:T(8,128)} %param.9) | copy-start | bytes 393220
  74.2 2.3 %copy-start.2 = (s32[64]{0:T(128)S(1)}, s32[64]{0:T(128)}, u32[]{:S(2)}) copy-start(s32[64]{0:T(128)} %param.11) | copy-start | bytes 772

commit v8 on v6

--- a/solution.py
+++ b/solution.py
@@ -51,6 +51,11 @@
 
 TURN = pairs(transpose_move)
 SWAP = pairs(lambda x, y, z, k: (x, y, z, 1 - k))
+PM2 = pairs(lambda x, y, z, k: (x, y, z + 2 if k == 0 else z - 2, k))
+
+
+def shift(d):
+    return pairs(lambda x, y, z, k: (x, y, z + d, k))
 
 
 def onward(d):
@@ -86,7 +91,6 @@
 
 
 BEYOND = (0, -4, 4, -8)
-AROUND = (0, -1, 1, -2)
 
 
 def where_am_i():
@@ -97,7 +101,8 @@
 def place(ref, base, group, core, z, col, high, low, fold):
     for slot in range(4):
         way = 1 - 2 * core
-        at = (z + way * (AROUND[group] + BEYOND[slot]) + 32) & 15
+        near = (0, -1, 1)[group] if group < 3 else -2 * way
+        at = (z + near + way * BEYOND[slot] + 32) & 15
         hop = 2 * ((at - col) & 15)
         px = (col // 4 + (jnp.int32(TABLE_X) >> hop)) & 3
         py = (col + (jnp.int32(TABLE_Y) >> hop)) & 3
@@ -235,9 +240,7 @@
     behind = send(base, onward(4))
     ahead = send(base, onward(-4))
     near = jnp.concatenate([base, behind, ahead, send(behind, onward(4))], 0)
-    behind = send(near, onward(1))
-    ahead = send(near, onward(-1))
-    mine = [near, behind, ahead, send(behind, onward(1))]
+    mine = [near, send(near, shift(1)), send(near, shift(-1)), send(near, PM2)]
     halves = (shape(512, 512, dtype=half), shape(512, 512, dtype=half))
     weight = kernel(weight_body, halves, "v", "vv")(gathered)
     held = lax.optimization_barrier(near)

time: 100 us -> 84.3 us (0.84)
  the two profiles are of different devices: /device:TPU:32 before, /device:TPU:1 now
where the time goes in v8:
time: 84.3 us; the launch traced here: 83.7 us
  starting transfers between devices  45.1 us (53%)
  waiting for transfers between devices  24.4 us (29%)
  Pallas kernels  12.1 us (14%)
  other arithmetic  1.22 us (1%)
  between operations  0.85 us (1%)
    ppermute x8, starting transfers between devices, send(): return lax.ppermute(array, AXES, moves)  40.6 us
    ppermute x8, waiting for transfers between devices, send(): return lax.ppermute(array, AXES, moves)  24.4 us
    pallas_call x4, Pallas kernels, call(): pl.pallas_call(body, out_shape=out, in_specs=[specs[m] for m in memory],...  12.1 us
    all_to_all x1, starting transfers between devices, step(): gathered = lax.all_to_all(load, 'col', 0, 0, tiled=True)  4.45 us
  transfers between devices with their start and end apart: 9, of which 5 were waited for; matrix products, arithmetic and copies ran while one was open for 1% of the time, Pallas kernels for 10%

profile of v8, /device:TPU:1, one launch (start us, length us, event | category | flops | bytes accessed | tf_op | source)
XLA Modules:
  0.0 83.7 jit_solution(7934599358929039625)
XLA Ops:
  0.6 16.3 %collective-permute-start = (f32[32,512]{1,0:T(8,128)}, f32[32,512]{1,0:T(8,128)S(1)}, u32[]{:S(2)}, u32[]{:S(2)}) collective-permute-start(f32[32,512]{1,0:T(8,128)} %panel.1), channel_id=1, source_target_pairs={{0,256},{16,272},{32,353},{48,369},{64,482},{80,498},{96,291},{112... | collective-permute-start | bytes 196616 | tf_op jit(solution)/shard_map/ppermute | solution.py:66
  16.9 2.3 %shard_map.77 = f32[16,64,512]{2,1,0:T(8,128)} custom-call(f32[32,512]{1,0:T(8,128)} %panel.1, f32[32,512]{1,0:T(8,128)} %bitcast.13), custom_call_target="tpu_custom_call" | custom-call | tf_op jit(solution)/shard_map/pallas_call | solution.py:206
  19.2 0.0 copy-start.3
  19.2 4.5 %all-to-all-start = ((f32[16,64,512]{2,1,0:T(8,128)}), f32[16,64,512]{2,1,0:T(8,128)}, u32[]{:S(2)}, u32[]{:S(2)}) async-start(f32[16,64,512]{2,1,0:T(8,128)} %shard_map.77), calls=%async_computation | async-start | bytes 4194304 | tf_op jit(solution)/shard_map/all_to_all | solution.py:237
  23.7 0.1 maximum_maximum_fusion
  23.8 4.5 %collective-permute-start.2 = (f32[136,128]{1,0:T(8,128)S(1)}, f32[136,128]{1,0:T(8,128)S(1)}, u32[]{:S(2)}, u32[]{:S(2)}) collective-permute-start(f32[136,128]{1,0:T(8,128)S(1)} %maximum_maximum_fusion), channel_id=1, source_target_pairs={{0,384},{16,144},{32,416},{48,176},{64,448},{80,208},{96,480},{112... | collective-permute-start | bytes 208904 | tf_op jit(solution)/shard_map/ppermute | solution.py:66
  28.3 4.7 %collective-permute-start.1 = (f32[136,128]{1,0:T(8,128)S(1)}, f32[136,128]{1,0:T(8,128)S(1)}, u32[]{:S(2)}, u32[]{:S(2)}) collective-permute-start(f32[136,128]{1,0:T(8,128)S(1)} %maximum_maximum_fusion), channel_id=1, source_target_pairs={{0,128},{16,400},{32,160},{48,432},{64,192},{80,464},{96,224},{112... | collective-permute-start | bytes 208904 | tf_op jit(solution)/shard_map/ppermute | solution.py:66
  33.0 0.1 constant_dynamic-update-slice_fusion.3
  33.1 8.0 %collective-permute-done.1 = f32[136,128]{1,0:T(8,128)S(1)} collective-permute-done((f32[136,128]{1,0:T(8,128)S(1)}, f32[136,128]{1,0:T(8,128)S(1)}, u32[]{:S(2)}, u32[]{:S(2)}) %collective-permute-start.1) | collective-permute-done | bytes 69664 | tf_op jit(solution)/shard_map/ppermute | solution.py:66
  41.1 2.9 %collective-permute-start.3 = (f32[136,128]{1,0:T(8,128)S(1)}, f32[136,128]{1,0:T(8,128)S(1)}, u32[]{:S(2)}, u32[]{:S(2)}) collective-permute-start(f32[136,128]{1,0:T(8,128)S(1)} %collective-permute-done.1), channel_id=1, source_target_pairs={{0,128},{16,400},{32,160},{48,432},{64,192},{80,464},{96,224},{112... | collective-permute-start | bytes 208904 | tf_op jit(solution)/shard_map/ppermute | solution.py:66
  44.0 7.5 %collective-permute-done.3 = f32[136,128]{1,0:T(8,128)S(1)} collective-permute-done((f32[136,128]{1,0:T(8,128)S(1)}, f32[136,128]{1,0:T(8,128)S(1)}, u32[]{:S(2)}, u32[]{:S(2)}) %collective-permute-start.3) | collective-permute-done | bytes 69664 | tf_op jit(solution)/shard_map/ppermute | solution.py:66
  51.5 2.3 %collective-permute-start.6 = (f32[544,128]{1,0:T(8,128)S(1)}, f32[544,128]{1,0:T(8,128)S(1)}, u32[]{:S(2)}, u32[]{:S(2)}) collective-permute-start(f32[544,128]{1,0:T(8,128)S(1)} %constant_dynamic-update-slice_fusion.mine0), channel_id=1, source_target_pairs={{0,64},{16,464},{32,96},{48,496},{64,128},{80,16},{96,160},{112,48... | collective-permute-start | bytes 835592 | tf_op jit(solution)/shard_map/ppermute | solution.py:66
  53.8 1.9 %collective-permute-start.5 = (f32[544,128]{1,0:T(8,128)S(1)}, f32[544,128]{1,0:T(8,128)S(1)}, u32[]{:S(2)}, u32[]{:S(2)}) collective-permute-start(f32[544,128]{1,0:T(8,128)S(1)} %constant_dynamic-update-slice_fusion.mine0), channel_id=1, source_target_pairs={{0,480},{16,496},{32,0},{48,16},{64,32},{80,48},{96,64},{112,80},{... | collective-permute-start | bytes 835592 | tf_op jit(solution)/shard_map/ppermute | solution.py:66
  55.7 3.4 %collective-permute-start.4 = (f32[544,128]{1,0:T(8,128)S(1)}, f32[544,128]{1,0:T(8,128)S(1)}, u32[]{:S(2)}, u32[]{:S(2)}) collective-permute-start(f32[544,128]{1,0:T(8,128)S(1)} %constant_dynamic-update-slice_fusion.mine0), channel_id=1, source_target_pairs={{0,32},{16,48},{32,64},{48,80},{64,96},{80,112},{96,128},{112,144}... | collective-permute-start | bytes 835592 | tf_op jit(solution)/shard_map/ppermute | solution.py:66
  59.1 1.0 %collective-permute-done.6.mine3 = f32[544,128]{1,0:T(8,128)S(1)} collective-permute-done((f32[544,128]{1,0:T(8,128)S(1)}, f32[544,128]{1,0:T(8,128)S(1)}, u32[]{:S(2)}, u32[]{:S(2)}) %collective-permute-start.6) | collective-permute-done | bytes 278560 | tf_op jit(solution)/shard_map/ppermute | solution.py:66
  60.0 6.5 %collective-permute-done.5.mine2 = f32[544,128]{1,0:T(8,128)S(1)} collective-permute-done((f32[544,128]{1,0:T(8,128)S(1)}, f32[544,128]{1,0:T(8,128)S(1)}, u32[]{:S(2)}, u32[]{:S(2)}) %collective-permute-start.5) | collective-permute-done | bytes 278560 | tf_op jit(solution)/shard_map/ppermute | solution.py:66
  66.5 1.5 %collective-permute-done.4.mine1 = f32[544,128]{1,0:T(8,128)S(1)} collective-permute-done((f32[544,128]{1,0:T(8,128)S(1)}, f32[544,128]{1,0:T(8,128)S(1)}, u32[]{:S(2)}, u32[]{:S(2)}) %collective-permute-start.4) | collective-permute-done | bytes 278560 | tf_op jit(solution)/shard_map/ppermute | solution.py:66
  68.1 1.1 %pad_maximum_fusion = f32[2176,128]{1,0:T(8,128)} fusion(f32[544,128]{1,0:T(8,128)S(1)} %collective-permute-done.6.mine3, f32[544,128]{1,0:T(8,128)S(1)} %collective-permute-done.5.mine2, f32[544,128]{1,0:T(8,128)S(1)} %collective-permute-done.4.mine1, f32[544,128]{1,0:T(8,128)S(1)} %constant_dynamic-update-slice_fusion.mine0), kind=kLoop, calls=%fused_computation | loop fusion | flops 835584 | bytes 2228224 | tf_op jit(solution)/shard_map/concatenate | solution.py:247
  69.1 4.7 %collective-permute-start.7 = (f32[2176,128]{1,0:T(8,128)}, f32[2176,128]{1,0:T(8,128)}, u32[]{:S(2)}, u32[]{:S(2)}) collective-permute-start(f32[2176,128]{1,0:T(8,128)} %pad_maximum_fusion), channel_id=1, source_target_pairs={{0,16},{16,0},{32,48},{48,32},{64,80},{80,64},{96,112},{112,96},{1... | collective-permute-start | bytes 3342344 | tf_op jit(solution)/shard_map/ppermute | solution.py:66
  73.9 3.4 %shard_map.78 = (bf16[512,512]{1,0:T(8,128)(2,1)S(1)}, bf16[512,512]{1,0:T(8,128)(2,1)S(1)}) custom-call(f32[16,64,512]{2,1,0:T(8,128)} %all-to-all-done.gathered), custom_call_target="tpu_custom_call" | custom-call | tf_op jit(solution)/shard_map/pallas_call | solution.py:206
  77.3 0.0 copy-start.1
  77.3 0.0 copy-start.2
  77.3 2.3 %shard_map.79 = (f32[512,1024]{1,0:T(8,128)}, f32[512,128]{1,0:T(8,128)S(1)}) custom-call(bf16[512,512]{1,0:T(8,128)(2,1)S(1)} %get-tuple-element.8.wh, bf16[512,512]{1,0:T(8,128)(2,1)S(1)} %get-tuple-element.9.wl, f32[512,1024]{1,0:T(8,128)S(1)} %copy-done, f32[544,128]{1,0:T(8,128)S(1)} %constant_dynamic-update-slice_fusion.mine0, ...), custom_call_target="tpu_custom_call" | custom-call | tf_op jit(solution)/shard_map/pallas_call | solution.py:206
  79.7 4.1 %shard_map.80 = (f32[512,1024]{1,0:T(8,128)}, f32[64,512]{1,0:T(8,128)}) custom-call(bf16[512,512]{1,0:T(8,128)(2,1)S(1)} %get-tuple-element.8.wh, bf16[512,512]{1,0:T(8,128)(2,1)S(1)} %get-tuple-element.9.wl, f32[512,1024]{1,0:T(8,128)S(1)} %copy-done, f32[2176,128]{1,0:T(8,128)} %collective-permute-done.7.others, ...), custom_call_target="tpu_custom_call", output_to_operand_aliasing={{0}: (7, {})} | custom-call | tf_op jit(solution)/shard_map/pallas_call | solution.py:206
  (14 shorter events, 0.1 us)
Async XLA Ops:
  0.6 23.1 %collective-permute-start = (f32[32,512]{1,0:T(8,128)}, f32[32,512]{1,0:T(8,128)S(1)}, u32[]{:S(2)}, u32[]{:S(2)}) collective-permute-start(f32[32,512]{1,0:T(8,128)} %panel.1), channel_id=1, source_target_pairs={{0,256},{16,272},{32,353},{48,369},{64,482},{80,498},{96,291},{112... | collective-permute-start | bytes 196616 | tf_op jit(solution)/shard_map/ppermute | solution.py:66
  19.2 4.5 %copy-start.3 = (f32[16,64]{1,0:T(8,128)S(1)}, f32[16,64]{1,0:T(8,128)}, u32[]{:S(2)}) copy-start(f32[16,64]{1,0:T(8,128)} %param.10) | copy-start | bytes 12292
  19.2 54.6 %all-to-all-start = ((f32[16,64,512]{2,1,0:T(8,128)}), f32[16,64,512]{2,1,0:T(8,128)}, u32[]{:S(2)}, u32[]{:S(2)}) async-start(f32[16,64,512]{2,1,0:T(8,128)} %shard_map.77), calls=%async_computation | async-start | bytes 4194304 | tf_op jit(solution)/shard_map/all_to_all | solution.py:237
  23.8 20.2 %collective-permute-start.2 = (f32[136,128]{1,0:T(8,128)S(1)}, f32[136,128]{1,0:T(8,128)S(1)}, u32[]{:S(2)}, u32[]{:S(2)}) collective-permute-start(f32[136,128]{1,0:T(8,128)S(1)} %maximum_maximum_fusion), channel_id=1, source_target_pairs={{0,384},{16,144},{32,416},{48,176},{64,448},{80,208},{96,480},{112... | collective-permute-start | bytes 208904 | tf_op jit(solution)/shard_map/ppermute | solution.py:66
  28.3 12.8 %collective-permute-start.1 = (f32[136,128]{1,0:T(8,128)S(1)}, f32[136,128]{1,0:T(8,128)S(1)}, u32[]{:S(2)}, u32[]{:S(2)}) collective-permute-start(f32[136,128]{1,0:T(8,128)S(1)} %maximum_maximum_fusion), channel_id=1, source_target_pairs={{0,128},{16,400},{32,160},{48,432},{64,192},{80,464},{96,224},{112... | collective-permute-start | bytes 208904 | tf_op jit(solution)/shard_map/ppermute | solution.py:66
  41.1 10.4 %collective-permute-start.3 = (f32[136,128]{1,0:T(8,128)S(1)}, f32[136,128]{1,0:T(8,128)S(1)}, u32[]{:S(2)}, u32[]{:S(2)}) collective-permute-start(f32[136,128]{1,0:T(8,128)S(1)} %collective-permute-done.1), channel_id=1, source_target_pairs={{0,128},{16,400},{32,160},{48,432},{64,192},{80,464},{96,224},{112... | collective-permute-start | bytes 208904 | tf_op jit(solution)/shard_map/ppermute | solution.py:66
  51.5 8.6 %collective-permute-start.6 = (f32[544,128]{1,0:T(8,128)S(1)}, f32[544,128]{1,0:T(8,128)S(1)}, u32[]{:S(2)}, u32[]{:S(2)}) collective-permute-start(f32[544,128]{1,0:T(8,128)S(1)} %constant_dynamic-update-slice_fusion.mine0), channel_id=1, source_target_pairs={{0,64},{16,464},{32,96},{48,496},{64,128},{80,16},{96,160},{112,48... | collective-permute-start | bytes 835592 | tf_op jit(solution)/shard_map/ppermute | solution.py:66
  53.8 12.8 %collective-permute-start.5 = (f32[544,128]{1,0:T(8,128)S(1)}, f32[544,128]{1,0:T(8,128)S(1)}, u32[]{:S(2)}, u32[]{:S(2)}) collective-permute-start(f32[544,128]{1,0:T(8,128)S(1)} %constant_dynamic-update-slice_fusion.mine0), channel_id=1, source_target_pairs={{0,480},{16,496},{32,0},{48,16},{64,32},{80,48},{96,64},{112,80},{... | collective-permute-start | bytes 835592 | tf_op jit(solution)/shard_map/ppermute | solution.py:66
  55.7 12.4 %collective-permute-start.4 = (f32[544,128]{1,0:T(8,128)S(1)}, f32[544,128]{1,0:T(8,128)S(1)}, u32[]{:S(2)}, u32[]{:S(2)}) collective-permute-start(f32[544,128]{1,0:T(8,128)S(1)} %constant_dynamic-update-slice_fusion.mine0), channel_id=1, source_target_pairs={{0,32},{16,48},{32,64},{48,80},{64,96},{80,112},{96,128},{112,144}... | collective-permute-start | bytes 835592 | tf_op jit(solution)/shard_map/ppermute | solution.py:66
  69.1 8.1 %copy-start = (f32[512,1024]{1,0:T(8,128)S(1)}, f32[512,1024]{1,0:T(8,128)}, u32[]{:S(2)}) copy-start(f32[512,1024]{1,0:T(8,128)} %vin.3) | copy-start | bytes 6291460
  69.1 10.5 %collective-permute-start.7 = (f32[2176,128]{1,0:T(8,128)}, f32[2176,128]{1,0:T(8,128)}, u32[]{:S(2)}, u32[]{:S(2)}) collective-permute-start(f32[2176,128]{1,0:T(8,128)} %pad_maximum_fusion), channel_id=1, source_target_pairs={{0,16},{16,0},{32,48},{48,32},{64,80},{80,64},{96,112},{112,96},{1... | collective-permute-start | bytes 3342344 | tf_op jit(solution)/shard_map/ppermute | solution.py:66
  77.3 2.4 %copy-start.1 = (f32[512,64]{0,1:T(8,128)S(1)}, f32[512,64]{0,1:T(8,128)}, u32[]{:S(2)}) copy-start(f32[512,64]{0,1:T(8,128)} %param.9) | copy-start | bytes 393220
  77.3 2.4 %copy-start.2 = (s32[64]{0:T(128)S(1)}, s32[64]{0:T(128)}, u32[]{:S(2)}) copy-start(s32[64]{0:T(128)} %param.11) | copy-start | bytes 772

commit v9 on v7

--- a/solution.py
+++ b/solution.py
@@ -116,9 +116,8 @@
         fold[pl.ds(first + 8, 8), :] = pltpu.roll(tile, 64, 1)
 
 
-def update(half, w, cols, vin, vout, out, sems, row, col):
+def update(half, w, cols, vin, vout, row, col, done):
     lower = 2 * col + half <= row
-    copies = []
     for n in range(2):
         part = slice(256 * n, 256 * n + 256)
         span = pl.ds(pl.multiple_of(512 * half + 256 * n, 256), 256)
@@ -132,10 +131,7 @@
         def _():
             vout[:, part] = vin[:, span]
 
-        copy = pltpu.make_async_copy(vout.at[:, part], out.at[:, span], sems.at[n])
-        copy.start()
-        copies.append(copy)
-    return copies
+        done(n, part, span)
 
 
 def begin(copies):
@@ -148,19 +144,28 @@
         copy.wait()
 
 
-def first_body(wh, wl, vin, mine0, mine1, mine2, mine3, out, fold, high, low, vout, sems):
+def first_body(wh, wl, vin, mine0, mine1, mine2, mine3, out, fold, high, low):
     row, col, z, k = where_am_i()
     for group, ref in enumerate((mine0, mine1, mine2, mine3)):
         place(ref, 0, group, k, z, col, high, low, fold)
-    end(update(k, (wh[...], wl[...]), (high, low), vin, vout, out, sems, row, col))
-
-
-def second_body(wh, wl, vin, others, half_fold, series, length, part, out, out_s, high, low, vout, fold, vsout, sems):
+    update(k, (wh[...], wl[...]), (high, low), vin, out, row, col, lambda n, part, span: None)
+
+
+def second_body(wh, wl, vin, other0, others, first, half_fold, series, length, out, out_s, high, low, vout, fold, vsout, sems):
     row, col, z, k = where_am_i()
-    for group in range(4):
-        place(others, 544 * group, group, 1 - k, z, col, high, low, fold)
+    writes = [pltpu.make_async_copy(first, out.at[:, pl.ds(pl.multiple_of(512 * k, 512), 512)], sems.at[3])]
+    begin(writes)
+    place(other0, 0, 0, 1 - k, z, col, high, low, fold)
+    for group in range(1, 4):
+        place(others, 544 * (group - 1), group, 1 - k, z, col, high, low, fold)
     w = (wh[...], wl[...])
-    writes = update(1 - k, w, (high, low), vin, vout, out, sems.at[0:2], row, col)
+
+    def done(n, part, span):
+        copy = pltpu.make_async_copy(vout.at[:, part], out.at[:, span], sems.at[n])
+        copy.start()
+        writes.append(copy)
+
+    update(1 - k, w, (high, low), vin, vout, row, col, done)
     for at in range(16):
         rows = pl.ds(pl.multiple_of(32 * at + 16 * k, 16), 16)
         fold[rows, :] = half_fold[rows, :]
@@ -242,21 +247,19 @@
     mine = [near, send(near, shift(1)), send(near, shift(-1)), send(near, PM2)]
     halves = (shape(512, 512, dtype=half), shape(512, 512, dtype=half))
     weight = kernel(weight_body, halves, "v", "vv")(gathered)
-    held = lax.optimization_barrier(near)
-    others = send(jnp.concatenate([held] + mine[1:], 0), SWAP)
+    other0 = send(near, SWAP)
+    others = send(jnp.concatenate(mine[1:], 0), SWAP)
     square = block(512, 512, dtype=half)
-    work = [square, square, block(512, 512)]
     part, half_fold = kernel(
-        first_body, (shape(512, 1024), shape(512, 128)), "vvvvvvv", "av", work + [sems(2)]
+        first_body, (shape(512, 512), shape(512, 128)), "vvvvvvv", "vv", [square, square]
     )(*weight, trailing, *mine)
     out, series = kernel(
         second_body,
         (shape(512, 1024), shape(64, 512)),
-        "vvvvvvva",
+        "vvvvvvvvv",
         "aa",
-        work + [block(512, 128), block(64, 512), sems(3)],
-        {7: 0},
-    )(*weight, trailing, others, half_fold, later_series.T, fold_len[None, :], part)
+        [square, square, block(512, 512), block(512, 128), block(64, 512), sems(4)],
+    )(*weight, trailing, other0, others, part, half_fold, later_series.T, fold_len[None, :])
     return out, series.T
 
 

time: 81.1 us -> 87.3 us (1.076)
  starting transfers between devices: 47.7 us -> 55.9 us
  waiting for transfers between devices: 18.7 us -> 17.6 us
  Pallas kernels: 12.1 us -> 11.2 us
    ppermute x9 -> x10, starting transfers between devices: 43.3 us -> 51.4 us  [send(): return lax.ppermute(array, AXES, moves)]
    ppermute x9 -> x10, waiting for transfers between devices: 18.7 us -> 17.6 us  [send(): return lax.ppermute(array, AXES, moves)]
    pallas_call x4, Pallas kernels: 12.1 us -> 11.2 us  [call(): pl.pallas_call(body, out_shape=out, in_specs=[specs[m] for m in memory],...]
  transfers between devices with their start and end apart: 10 -> 11, of which waited for: 5 -> 4; matrix products, arithmetic and copies ran while one was open for 2% -> 1% of each run, Pallas kernels for 10% -> 8%
where the time goes in v9:
time: 87.3 us; the launch traced here: 86.7 us
  starting transfers between devices  55.9 us (64%)
  waiting for transfers between devices  17.6 us (20%)
  Pallas kernels  11.2 us (13%)
  other arithmetic  1.12 us (1%)
  between operations  0.88 us (1%)
    ppermute x10, starting transfers between devices, send(): return lax.ppermute(array, AXES, moves)  51.4 us
    ppermute x10, waiting for transfers between devices, send(): return lax.ppermute(array, AXES, moves)  17.6 us
    pallas_call x4, Pallas kernels, call(): pl.pallas_call(body, out_shape=out, in_specs=[specs[m] for m in memory],...  11.2 us
    all_to_all x1, starting transfers between devices, step(): gathered = lax.all_to_all(load, 'col', 0, 0, tiled=True)  4.45 us
  transfers between devices with their start and end apart: 11, of which 4 were waited for; matrix products, arithmetic and copies ran while one was open for 1% of the time, Pallas kernels for 8%

profile of v9, /device:TPU:1, one launch (start us, length us, event | category | flops | bytes accessed | tf_op | source)
XLA Modules:
  0.0 86.7 jit_solution(8287654735992548601)
XLA Ops:
  0.6 16.3 %collective-permute-start = (f32[32,512]{1,0:T(8,128)}, f32[32,512]{1,0:T(8,128)S(1)}, u32[]{:S(2)}, u32[]{:S(2)}) collective-permute-start(f32[32,512]{1,0:T(8,128)} %panel.1), channel_id=1, source_target_pairs={{0,256},{16,272},{32,353},{48,369},{64,482},{80,498},{96,291},{112... | collective-permute-start | bytes 196616 | tf_op jit(solution)/shard_map/ppermute | solution.py:63
  16.9 2.3 %shard_map.77 = f32[16,64,512]{2,1,0:T(8,128)} custom-call(f32[32,512]{1,0:T(8,128)} %panel.1, f32[32,512]{1,0:T(8,128)} %bitcast.13), custom_call_target="tpu_custom_call" | custom-call | tf_op jit(solution)/shard_map/pallas_call | solution.py:208
  19.2 0.0 copy-start.3
  19.2 4.5 %all-to-all-start = ((f32[16,64,512]{2,1,0:T(8,128)}), f32[16,64,512]{2,1,0:T(8,128)}, u32[]{:S(2)}, u32[]{:S(2)}) async-start(f32[16,64,512]{2,1,0:T(8,128)} %shard_map.77), calls=%async_computation | async-start | bytes 4194304 | tf_op jit(solution)/shard_map/all_to_all | solution.py:239
  23.7 0.1 maximum_maximum_fusion
  23.8 4.5 %collective-permute-start.1 = (f32[136,128]{1,0:T(8,128)S(1)}, f32[136,128]{1,0:T(8,128)S(1)}, u32[]{:S(2)}, u32[]{:S(2)}) collective-permute-start(f32[136,128]{1,0:T(8,128)S(1)} %maximum_maximum_fusion), channel_id=1, source_target_pairs={{0,128},{16,144},{32,160},{48,176},{64,192},{80,208},{96,224},{112... | collective-permute-start | bytes 208904 | tf_op jit(solution)/shard_map/ppermute | solution.py:63
  28.3 4.7 %collective-permute-start.2 = (f32[136,128]{1,0:T(8,128)S(1)}, f32[136,128]{1,0:T(8,128)S(1)}, u32[]{:S(2)}, u32[]{:S(2)}) collective-permute-start(f32[136,128]{1,0:T(8,128)S(1)} %maximum_maximum_fusion), channel_id=1, source_target_pairs={{0,384},{16,400},{32,416},{48,432},{64,448},{80,464},{96,480},{112... | collective-permute-start | bytes 208904 | tf_op jit(solution)/shard_map/ppermute | solution.py:63
  33.0 0.7 collective-permute-start.3
  33.7 0.1 constant_dynamic-update-slice_fusion.2
  33.8 3.7 %collective-permute-done.2 = f32[136,128]{1,0:T(8,128)S(1)} collective-permute-done((f32[136,128]{1,0:T(8,128)S(1)}, f32[136,128]{1,0:T(8,128)S(1)}, u32[]{:S(2)}, u32[]{:S(2)}) %collective-permute-start.2) | collective-permute-done | bytes 69664 | tf_op jit(solution)/shard_map/ppermute | solution.py:63
  37.4 5.5 %collective-permute-start.4 = (f32[136,128]{1,0:T(8,128)S(1)}, f32[136,128]{1,0:T(8,128)S(1)}, u32[]{:S(2)}, u32[]{:S(2)}) collective-permute-start(f32[136,128]{1,0:T(8,128)S(1)} %collective-permute-done.2), channel_id=1, source_target_pairs={{16,400},{48,432},{80,464},{112,496},{144,16},{176,48},{208,80},{2... | collective-permute-start | bytes 208904 | tf_op jit(solution)/shard_map/ppermute | solution.py:63
  43.0 3.8 %collective-permute-done.4 = f32[136,128]{1,0:T(8,128)S(1)} collective-permute-done((f32[136,128]{1,0:T(8,128)S(1)}, f32[136,128]{1,0:T(8,128)S(1)}, u32[]{:S(2)}, u32[]{:S(2)}) %collective-permute-start.4) | collective-permute-done | bytes 69664 | tf_op jit(solution)/shard_map/ppermute | solution.py:63
  46.8 8.0 %collective-permute-start.6 = (f32[544,128]{1,0:T(8,128)S(1)}, f32[544,128]{1,0:T(8,128)S(1)}, u32[]{:S(2)}, u32[]{:S(2)}) collective-permute-start(f32[544,128]{1,0:T(8,128)S(1)} %add_dynamic-update-slice_fusion.mine0), channel_id=1, source_target_pairs={{0,32},{16,48},{32,64},{48,80},{64,96},{80,112},{96,128},{112,144}... | collective-permute-start | bytes 835592 | tf_op jit(solution)/shard_map/ppermute | solution.py:63
  54.8 2.4 %collective-permute-start.7 = (f32[544,128]{1,0:T(8,128)S(1)}, f32[544,128]{1,0:T(8,128)S(1)}, u32[]{:S(2)}, u32[]{:S(2)}) collective-permute-start(f32[544,128]{1,0:T(8,128)S(1)} %add_dynamic-update-slice_fusion.mine0), channel_id=1, source_target_pairs={{0,480},{16,496},{32,0},{48,16},{64,32},{80,48},{96,64},{112,80},{... | collective-permute-start | bytes 835592 | tf_op jit(solution)/shard_map/ppermute | solution.py:63
  57.2 5.1 %collective-permute-start.8 = (f32[544,128]{1,0:T(8,128)S(1)}, f32[544,128]{1,0:T(8,128)S(1)}, u32[]{:S(2)}, u32[]{:S(2)}) collective-permute-start(f32[544,128]{1,0:T(8,128)S(1)} %add_dynamic-update-slice_fusion.mine0), channel_id=1, source_target_pairs={{0,64},{16,464},{32,96},{48,496},{64,128},{80,16},{96,160},{112,48... | collective-permute-start | bytes 835592 | tf_op jit(solution)/shard_map/ppermute | solution.py:63
  62.3 1.6 %collective-permute-done.7.mine2 = f32[544,128]{1,0:T(8,128)S(1)} collective-permute-done((f32[544,128]{1,0:T(8,128)S(1)}, f32[544,128]{1,0:T(8,128)S(1)}, u32[]{:S(2)}, u32[]{:S(2)}) %collective-permute-start.7) | collective-permute-done | bytes 278560 | tf_op jit(solution)/shard_map/ppermute | solution.py:63
  64.0 8.5 %collective-permute-done.8.mine3 = f32[544,128]{1,0:T(8,128)S(1)} collective-permute-done((f32[544,128]{1,0:T(8,128)S(1)}, f32[544,128]{1,0:T(8,128)S(1)}, u32[]{:S(2)}, u32[]{:S(2)}) %collective-permute-start.8) | collective-permute-done | bytes 278560 | tf_op jit(solution)/shard_map/ppermute | solution.py:63
  72.5 1.0 %pad_maximum_fusion = f32[1632,128]{1,0:T(8,128)} fusion(f32[544,128]{1,0:T(8,128)S(1)} %collective-permute-done.8.mine3, f32[544,128]{1,0:T(8,128)S(1)} %collective-permute-done.7.mine2, f32[544,128]{1,0:T(8,128)S(1)} %collective-permute-done.6.mine1), kind=kLoop, calls=%fused_computation | loop fusion | flops 417792 | bytes 1671168 | tf_op jit(solution)/shard_map/concatenate | solution.py:251
  73.4 2.1 %collective-permute-start.9 = (f32[1632,128]{1,0:T(8,128)}, f32[1632,128]{1,0:T(8,128)}, u32[]{:S(2)}, u32[]{:S(2)}) collective-permute-start(f32[1632,128]{1,0:T(8,128)} %pad_maximum_fusion), channel_id=1, source_target_pairs={{0,16},{16,0},{32,48},{48,32},{64,80},{80,64},{96,112},{112,96},{1... | collective-permute-start | bytes 2506760 | tf_op jit(solution)/shard_map/ppermute | solution.py:63
  75.6 2.2 %collective-permute-start.5 = (f32[544,128]{1,0:T(8,128)S(1)}, f32[544,128]{1,0:T(8,128)S(1)}, u32[]{:S(2)}, u32[]{:S(2)}) collective-permute-start(f32[544,128]{1,0:T(8,128)S(1)} %add_dynamic-update-slice_fusion.mine0), channel_id=1, source_target_pairs={{0,16},{16,0},{32,48},{48,32},{64,80},{80,64},{96,112},{112,96},{1... | collective-permute-start | bytes 835592 | tf_op jit(solution)/shard_map/ppermute | solution.py:63
  77.8 3.4 %shard_map.78 = (bf16[512,512]{1,0:T(8,128)(2,1)S(1)}, bf16[512,512]{1,0:T(8,128)(2,1)S(1)}) custom-call(f32[16,64,512]{2,1,0:T(8,128)} %all-to-all-done.gathered), custom_call_target="tpu_custom_call" | custom-call | tf_op jit(solution)/shard_map/pallas_call | solution.py:208
  81.2 0.0 copy-start.2
  81.2 1.5 %shard_map.79 = (f32[512,512]{1,0:T(8,128)S(1)}, f32[512,128]{1,0:T(8,128)S(1)}) custom-call(bf16[512,512]{1,0:T(8,128)(2,1)S(1)} %get-tuple-element.8.wh, bf16[512,512]{1,0:T(8,128)(2,1)S(1)} %get-tuple-element.9.wl, f32[512,1024]{1,0:T(8,128)S(1)} %copy-done, f32[544,128]{1,0:T(8,128)S(1)} %add_dynamic-update-slice_fusion.mine0, ...), custom_call_target="tpu_custom_call" | custom-call | tf_op jit(solution)/shard_map/pallas_call | solution.py:208
  82.7 4.0 %shard_map.80 = (f32[512,1024]{1,0:T(8,128)}, f32[64,512]{1,0:T(8,128)}) custom-call(bf16[512,512]{1,0:T(8,128)(2,1)S(1)} %get-tuple-element.8.wh, bf16[512,512]{1,0:T(8,128)(2,1)S(1)} %get-tuple-element.9.wl, f32[512,1024]{1,0:T(8,128)S(1)} %copy-done, f32[544,128]{1,0:T(8,128)S(1)} %collective-permute-done.5.other0, ...), custom_call_target="tpu_custom_call" | custom-call | tf_op jit(solution)/shard_map/pallas_call | solution.py:208
  (18 shorter events, 0.1 us)
Async XLA Ops:
  0.6 23.1 %collective-permute-start = (f32[32,512]{1,0:T(8,128)}, f32[32,512]{1,0:T(8,128)S(1)}, u32[]{:S(2)}, u32[]{:S(2)}) collective-permute-start(f32[32,512]{1,0:T(8,128)} %panel.1), channel_id=1, source_target_pairs={{0,256},{16,272},{32,353},{48,369},{64,482},{80,498},{96,291},{112... | collective-permute-start | bytes 196616 | tf_op jit(solution)/shard_map/ppermute | solution.py:63
  19.2 4.5 %copy-start.3 = (f32[16,64]{1,0:T(8,128)S(1)}, f32[16,64]{1,0:T(8,128)}, u32[]{:S(2)}) copy-start(f32[16,64]{1,0:T(8,128)} %param.10) | copy-start | bytes 12292
  19.2 58.5 %all-to-all-start = ((f32[16,64,512]{2,1,0:T(8,128)}), f32[16,64,512]{2,1,0:T(8,128)}, u32[]{:S(2)}, u32[]{:S(2)}) async-start(f32[16,64,512]{2,1,0:T(8,128)} %shard_map.77), calls=%async_computation | async-start | bytes 4194304 | tf_op jit(solution)/shard_map/all_to_all | solution.py:239
  23.8 19.1 %collective-permute-start.1 = (f32[136,128]{1,0:T(8,128)S(1)}, f32[136,128]{1,0:T(8,128)S(1)}, u32[]{:S(2)}, u32[]{:S(2)}) collective-permute-start(f32[136,128]{1,0:T(8,128)S(1)} %maximum_maximum_fusion), channel_id=1, source_target_pairs={{0,128},{16,144},{32,160},{48,176},{64,192},{80,208},{96,224},{112... | collective-permute-start | bytes 208904 | tf_op jit(solution)/shard_map/ppermute | solution.py:63
  28.3 9.1 %collective-permute-start.2 = (f32[136,128]{1,0:T(8,128)S(1)}, f32[136,128]{1,0:T(8,128)S(1)}, u32[]{:S(2)}, u32[]{:S(2)}) collective-permute-start(f32[136,128]{1,0:T(8,128)S(1)} %maximum_maximum_fusion), channel_id=1, source_target_pairs={{0,384},{16,400},{32,416},{48,432},{64,448},{80,464},{96,480},{112... | collective-permute-start | bytes 208904 | tf_op jit(solution)/shard_map/ppermute | solution.py:63
  33.0 10.0 %collective-permute-start.3 = (f32[136,128]{1,0:T(8,128)S(1)}, f32[136,128]{1,0:T(8,128)S(1)}, u32[]{:S(2)}, u32[]{:S(2)}) collective-permute-start(f32[136,128]{1,0:T(8,128)S(1)} %maximum_maximum_fusion), channel_id=1, source_target_pairs={{0,256},{32,288},{64,320},{96,352},{128,384},{160,416},{192,448},{... | collective-permute-start | bytes 208904 | tf_op jit(solution)/shard_map/ppermute | solution.py:63
  33.8 47.4 %copy-start = (f32[512,1024]{1,0:T(8,128)S(1)}, f32[512,1024]{1,0:T(8,128)}, u32[]{:S(2)}) copy-start(f32[512,1024]{1,0:T(8,128)} %vin.3) | copy-start | bytes 6291460
  37.4 9.3 %collective-permute-start.4 = (f32[136,128]{1,0:T(8,128)S(1)}, f32[136,128]{1,0:T(8,128)S(1)}, u32[]{:S(2)}, u32[]{:S(2)}) collective-permute-start(f32[136,128]{1,0:T(8,128)S(1)} %collective-permute-done.2), channel_id=1, source_target_pairs={{16,400},{48,432},{80,464},{112,496},{144,16},{176,48},{208,80},{2... | collective-permute-start | bytes 208904 | tf_op jit(solution)/shard_map/ppermute | solution.py:63
  46.8 15.5 %collective-permute-start.6 = (f32[544,128]{1,0:T(8,128)S(1)}, f32[544,128]{1,0:T(8,128)S(1)}, u32[]{:S(2)}, u32[]{:S(2)}) collective-permute-start(f32[544,128]{1,0:T(8,128)S(1)} %add_dynamic-update-slice_fusion.mine0), channel_id=1, source_target_pairs={{0,32},{16,48},{32,64},{48,80},{64,96},{80,112},{96,128},{112,144}... | collective-permute-start | bytes 835592 | tf_op jit(solution)/shard_map/ppermute | solution.py:63
  54.8 9.1 %collective-permute-start.7 = (f32[544,128]{1,0:T(8,128)S(1)}, f32[544,128]{1,0:T(8,128)S(1)}, u32[]{:S(2)}, u32[]{:S(2)}) collective-permute-start(f32[544,128]{1,0:T(8,128)S(1)} %add_dynamic-update-slice_fusion.mine0), channel_id=1, source_target_pairs={{0,480},{16,496},{32,0},{48,16},{64,32},{80,48},{96,64},{112,80},{... | collective-permute-start | bytes 835592 | tf_op jit(solution)/shard_map/ppermute | solution.py:63
  57.2 15.3 %collective-permute-start.8 = (f32[544,128]{1,0:T(8,128)S(1)}, f32[544,128]{1,0:T(8,128)S(1)}, u32[]{:S(2)}, u32[]{:S(2)}) collective-permute-start(f32[544,128]{1,0:T(8,128)S(1)} %add_dynamic-update-slice_fusion.mine0), channel_id=1, source_target_pairs={{0,64},{16,464},{32,96},{48,496},{64,128},{80,16},{96,160},{112,48... | collective-permute-start | bytes 835592 | tf_op jit(solution)/shard_map/ppermute | solution.py:63
  73.4 9.3 %collective-permute-start.9 = (f32[1632,128]{1,0:T(8,128)}, f32[1632,128]{1,0:T(8,128)}, u32[]{:S(2)}, u32[]{:S(2)}) collective-permute-start(f32[1632,128]{1,0:T(8,128)} %pad_maximum_fusion), channel_id=1, source_target_pairs={{0,16},{16,0},{32,48},{48,32},{64,80},{80,64},{96,112},{112,96},{1... | collective-permute-start | bytes 2506760 | tf_op jit(solution)/shard_map/ppermute | solution.py:63
  75.6 7.1 %collective-permute-start.5 = (f32[544,128]{1,0:T(8,128)S(1)}, f32[544,128]{1,0:T(8,128)S(1)}, u32[]{:S(2)}, u32[]{:S(2)}) collective-permute-start(f32[544,128]{1,0:T(8,128)S(1)} %add_dynamic-update-slice_fusion.mine0), channel_id=1, source_target_pairs={{0,16},{16,0},{32,48},{48,32},{64,80},{80,64},{96,112},{112,96},{1... | collective-permute-start | bytes 835592 | tf_op jit(solution)/shard_map/ppermute | solution.py:63
  81.2 1.5 %copy-start.1 = (f32[512,64]{0,1:T(8,128)S(1)}, f32[512,64]{0,1:T(8,128)}, u32[]{:S(2)}) copy-start(f32[512,64]{0,1:T(8,128)} %param.9) | copy-start | bytes 393220
  81.2 1.5 %copy-start.2 = (s32[64]{0:T(128)S(1)}, s32[64]{0:T(128)}, u32[]{:S(2)}) copy-start(s32[64]{0:T(128)} %param.11) | copy-start | bytes 772

commit v10 on v7

--- a/solution.py
+++ b/solution.py
@@ -79,8 +79,11 @@
     return dot(ah, bh) + (dot(ah, bl) + dot(al, bh))
 
 
-def weight_body(gathered, out_high, out_low):
-    inverse = split(gathered[:, 32:64, :].reshape(512, 512))
+def weight_body(gathered, other, out_high, out_low, inv):
+    k = lax.axis_index("row") % 2
+    inv[:, k] = gathered[:, 32:48, :]
+    inv[:, 1 - k] = other[...]
+    inverse = split(inv[...].reshape(512, 512))
     solved = dot3(split(gathered[:, 0:32, :].reshape(512, 512)), inverse, NN)
     high, low = split(dot3(split(solved), inverse, NT))
     out_high[...] = high
@@ -174,9 +177,10 @@
 
 
 def spread_body(panel, stripe, out, stage, sems):
+    k = lax.axis_index("row") % 2
     loads = [
         pltpu.make_async_copy(panel, stage.at[0:32, :], sems.at[16]),
-        pltpu.make_async_copy(stripe, stage.at[32:64, :], sems.at[17]),
+        pltpu.make_async_copy(stripe.at[pl.ds(pl.multiple_of(16 * k, 16), 16), :], stage.at[32:48, :], sems.at[17]),
     ]
     begin(loads)
     end(loads)
@@ -229,7 +233,7 @@
     half = jnp.bfloat16
     chunk = tile_order(send(panel, TURN))
     load = kernel(
-        spread_body, shape(16, 64, 512), "aa", "a", [block(64, 512), sems(18)], room=0
+        spread_body, shape(16, 48, 512), "aa", "a", [block(48, 512), sems(18)], room=0
     )(panel, inv_factor.T)
     gathered = lax.all_to_all(load, "col", 0, 0, tiled=True)
     fold = jnp.concatenate([fold_series[0:8], fold_series[8:16]], 1)
@@ -241,7 +245,8 @@
     near = jnp.concatenate([base, behind, ahead, across], 0)
     mine = [near, send(near, shift(1)), send(near, shift(-1)), send(near, PM2)]
     halves = (shape(512, 512, dtype=half), shape(512, 512, dtype=half))
-    weight = kernel(weight_body, halves, "v", "vv")(gathered)
+    other = send(gathered[:, 32:, :], SWAP)
+    weight = kernel(weight_body, halves, "vv", "vv", [block(16, 2, 16, 512)])(gathered, other)
     held = lax.optimization_barrier(near)
     others = send(jnp.concatenate([held] + mine[1:], 0), SWAP)
     square = block(512, 512, dtype=half)

time: 81.1 us -> 82.6 us (1.018)
  starting transfers between devices: 47.7 us -> 55.3 us
  waiting for transfers between devices: 18.7 us -> 14.2 us
  Pallas kernels: 12.1 us -> 10.4 us
    ppermute x9 -> x10, starting transfers between devices: 43.3 us -> 51.6 us  [send(): return lax.ppermute(array, AXES, moves)]
    ppermute x9 -> x10, waiting for transfers between devices: 18.7 us -> 14.2 us  [send(): return lax.ppermute(array, AXES, moves)]
    pallas_call x4, Pallas kernels: 12.1 us -> 10.4 us  [call(): pl.pallas_call(body, out_shape=out, in_specs=[specs[m] for m in memory],...]
  transfers between devices with their start and end apart: 10 -> 11, of which waited for: 5 -> 6; matrix products, arithmetic and copies ran while one was open for 2% -> 2% of each run, Pallas kernels for 10% -> 8%
where the time goes in v10:
time: 82.6 us; the launch traced here: 82.1 us
  starting transfers between devices  55.3 us (67%)
  waiting for transfers between devices  14.2 us (17%)
  Pallas kernels  10.4 us (13%)
  other arithmetic  1.25 us (2%)
  between operations  0.87 us (1%)
    ppermute x10, starting transfers between devices, send(): return lax.ppermute(array, AXES, moves)  51.6 us
    ppermute x10, waiting for transfers between devices, send(): return lax.ppermute(array, AXES, moves)  14.2 us
    pallas_call x4, Pallas kernels, call(): pl.pallas_call(body, out_shape=out, in_specs=[specs[m] for m in memory],...  10.4 us
    all_to_all x1, starting transfers between devices, step(): gathered = lax.all_to_all(load, 'col', 0, 0, tiled=True)  3.72 us
  transfers between devices with their start and end apart: 11, of which 6 were waited for; matrix products, arithmetic and copies ran while one was open for 2% of the time, Pallas kernels for 8%

profile of v10, /device:TPU:1, one launch (start us, length us, event | category | flops | bytes accessed | tf_op | source)
XLA Modules:
  0.0 82.1 jit_solution(5024676832170223280)
XLA Ops:
  0.6 16.3 %collective-permute-start.1 = (f32[32,512]{1,0:T(8,128)}, f32[32,512]{1,0:T(8,128)S(1)}, u32[]{:S(2)}, u32[]{:S(2)}) collective-permute-start(f32[32,512]{1,0:T(8,128)} %panel.1), channel_id=1, source_target_pairs={{0,256},{16,272},{32,353},{48,369},{64,482},{80,498},{96,291},{112... | collective-permute-start | bytes 196616 | tf_op jit(solution)/shard_map/ppermute | solution.py:63
  16.9 2.1 %shard_map.77 = f32[16,48,512]{2,1,0:T(8,128)} custom-call(f32[32,512]{1,0:T(8,128)} %panel.1, f32[32,512]{1,0:T(8,128)} %bitcast.13), custom_call_target="tpu_custom_call" | custom-call | tf_op jit(solution)/shard_map/pallas_call | solution.py:207
  19.1 3.7 %all-to-all-start = ((f32[16,48,512]{2,1,0:T(8,128)}), f32[16,48,512]{2,1,0:T(8,128)S(1)}, u32[]{:S(2)}, u32[]{:S(2)}) async-start(f32[16,48,512]{2,1,0:T(8,128)} %shard_map.77), calls=%async_computation | async-start | bytes 3145728 | tf_op jit(solution)/shard_map/all_to_all | solution.py:238
  22.8 0.1 maximum_maximum_fusion
  22.9 0.7 collective-permute-start.4
  23.5 5.4 %collective-permute-start.3 = (f32[136,128]{1,0:T(8,128)S(1)}, f32[136,128]{1,0:T(8,128)S(1)}, u32[]{:S(2)}, u32[]{:S(2)}) collective-permute-start(f32[136,128]{1,0:T(8,128)S(1)} %maximum_maximum_fusion), channel_id=1, source_target_pairs={{0,384},{16,400},{32,416},{48,432},{64,448},{80,464},{96,480},{112... | collective-permute-start | bytes 208904 | tf_op jit(solution)/shard_map/ppermute | solution.py:63
  28.9 3.8 %collective-permute-start.2 = (f32[136,128]{1,0:T(8,128)S(1)}, f32[136,128]{1,0:T(8,128)S(1)}, u32[]{:S(2)}, u32[]{:S(2)}) collective-permute-start(f32[136,128]{1,0:T(8,128)S(1)} %maximum_maximum_fusion), channel_id=1, source_target_pairs={{0,128},{16,144},{32,160},{48,176},{64,192},{80,208},{96,224},{112... | collective-permute-start | bytes 208904 | tf_op jit(solution)/shard_map/ppermute | solution.py:63
  32.8 0.1 constant_dynamic-update-slice_fusion.2
  32.8 5.3 %collective-permute-start.5 = (f32[136,128]{1,0:T(8,128)S(1)}, f32[136,128]{1,0:T(8,128)S(1)}, u32[]{:S(2)}, u32[]{:S(2)}) collective-permute-start(f32[136,128]{1,0:T(8,128)S(1)} %collective-permute-done.3), channel_id=1, source_target_pairs={{16,400},{48,432},{80,464},{112,496},{144,16},{176,48},{208,80},{2... | collective-permute-start | bytes 208904 | tf_op jit(solution)/shard_map/ppermute | solution.py:63
  38.2 0.7 collective-permute-done.2
  38.9 3.2 %collective-permute-done.5 = f32[136,128]{1,0:T(8,128)S(1)} collective-permute-done((f32[136,128]{1,0:T(8,128)S(1)}, f32[136,128]{1,0:T(8,128)S(1)}, u32[]{:S(2)}, u32[]{:S(2)}) %collective-permute-start.5) | collective-permute-done | bytes 69664 | tf_op jit(solution)/shard_map/ppermute | solution.py:63
  42.2 9.4 %collective-permute-start.8 = (f32[544,128]{1,0:T(8,128)S(1)}, f32[544,128]{1,0:T(8,128)S(1)}, u32[]{:S(2)}, u32[]{:S(2)}) collective-permute-start(f32[544,128]{1,0:T(8,128)S(1)} %add_dynamic-update-slice_fusion.mine0), channel_id=1, source_target_pairs={{0,64},{16,464},{32,96},{48,496},{64,128},{80,16},{96,160},{112,48... | collective-permute-start | bytes 835592 | tf_op jit(solution)/shard_map/ppermute | solution.py:63
  51.6 1.9 %collective-permute-start.7 = (f32[544,128]{1,0:T(8,128)S(1)}, f32[544,128]{1,0:T(8,128)S(1)}, u32[]{:S(2)}, u32[]{:S(2)}) collective-permute-start(f32[544,128]{1,0:T(8,128)S(1)} %add_dynamic-update-slice_fusion.mine0), channel_id=1, source_target_pairs={{0,480},{16,496},{32,0},{48,16},{64,32},{80,48},{96,64},{112,80},{... | collective-permute-start | bytes 835592 | tf_op jit(solution)/shard_map/ppermute | solution.py:63
  53.5 3.4 %collective-permute-start.6 = (f32[544,128]{1,0:T(8,128)S(1)}, f32[544,128]{1,0:T(8,128)S(1)}, u32[]{:S(2)}, u32[]{:S(2)}) collective-permute-start(f32[544,128]{1,0:T(8,128)S(1)} %add_dynamic-update-slice_fusion.mine0), channel_id=1, source_target_pairs={{0,32},{16,48},{32,64},{48,80},{64,96},{80,112},{96,128},{112,144}... | collective-permute-start | bytes 835592 | tf_op jit(solution)/shard_map/ppermute | solution.py:63
  56.9 1.4 %collective-permute-done.8.mine3 = f32[544,128]{1,0:T(8,128)S(1)} collective-permute-done((f32[544,128]{1,0:T(8,128)S(1)}, f32[544,128]{1,0:T(8,128)S(1)}, u32[]{:S(2)}, u32[]{:S(2)}) %collective-permute-start.8) | collective-permute-done | bytes 278560 | tf_op jit(solution)/shard_map/ppermute | solution.py:63
  58.2 6.1 %collective-permute-done.7.mine2 = f32[544,128]{1,0:T(8,128)S(1)} collective-permute-done((f32[544,128]{1,0:T(8,128)S(1)}, f32[544,128]{1,0:T(8,128)S(1)}, u32[]{:S(2)}, u32[]{:S(2)}) %collective-permute-start.7) | collective-permute-done | bytes 278560 | tf_op jit(solution)/shard_map/ppermute | solution.py:63
  64.3 0.9 %collective-permute-done.6.mine1 = f32[544,128]{1,0:T(8,128)S(1)} collective-permute-done((f32[544,128]{1,0:T(8,128)S(1)}, f32[544,128]{1,0:T(8,128)S(1)}, u32[]{:S(2)}, u32[]{:S(2)}) %collective-permute-start.6) | collective-permute-done | bytes 278560 | tf_op jit(solution)/shard_map/ppermute | solution.py:63
  65.3 1.1 %pad_maximum_fusion = f32[2176,128]{1,0:T(8,128)} fusion(f32[544,128]{1,0:T(8,128)S(1)} %collective-permute-done.8.mine3, f32[544,128]{1,0:T(8,128)S(1)} %collective-permute-done.7.mine2, f32[544,128]{1,0:T(8,128)S(1)} %collective-permute-done.6.mine1, f32[544,128]{1,0:T(8,128)S(1)} %add_dynamic-update-slice_fusion.mine0), kind=kLoop, calls=%fused_computation | loop fusion | flops 835584 | bytes 2228224 | tf_op jit(solution)/shard_map/concatenate | solution.py:251
  66.3 3.4 %collective-permute-start.9 = (f32[2176,128]{1,0:T(8,128)}, f32[2176,128]{1,0:T(8,128)}, u32[]{:S(2)}, u32[]{:S(2)}) collective-permute-start(f32[2176,128]{1,0:T(8,128)} %pad_maximum_fusion), channel_id=1, source_target_pairs={{0,16},{16,0},{32,48},{48,32},{64,80},{80,64},{96,112},{112,96},{1... | collective-permute-start | bytes 3342344 | tf_op jit(solution)/shard_map/ppermute | solution.py:63
  69.8 2.1 %collective-permute-start = (f32[16,16,512]{2,1,0:T(8,128)S(1)}, f32[16,16,512]{2,1,0:T(8,128)S(1)}, u32[]{:S(2)}, u32[]{:S(2)}) collective-permute-start(f32[16,16,512]{2,1,0:T(8,128)S(1)} %slice.12), channel_id=1, source_target_pairs={{0,16},{16,0},{32,48},{48,32},{64,80},{80,64},{96,112},{112,96},{1... | collective-permute-start | bytes 1572872 | tf_op jit(solution)/shard_map/ppermute | solution.py:63
  71.9 1.9 %collective-permute-done.other = f32[16,16,512]{2,1,0:T(8,128)S(1)} collective-permute-done((f32[16,16,512]{2,1,0:T(8,128)S(1)}, f32[16,16,512]{2,1,0:T(8,128)S(1)}, u32[]{:S(2)}, u32[]{:S(2)}) %collective-permute-start) | collective-permute-done | bytes 524320 | tf_op jit(solution)/shard_map/ppermute | solution.py:63
  73.8 1.9 %shard_map.78 = (bf16[512,512]{1,0:T(8,128)(2,1)S(1)}, bf16[512,512]{1,0:T(8,128)(2,1)S(1)}) custom-call(f32[16,48,512]{2,1,0:T(8,128)S(1)} %all-to-all-done.gathered, f32[16,16,512]{2,1,0:T(8,128)S(1)} %collective-permute-done.other), custom_call_target="tpu_custom_call" | custom-call | tf_op jit(solution)/shard_map/pallas_call | solution.py:207
  75.7 2.3 %shard_map.79 = (f32[512,1024]{1,0:T(8,128)}, f32[512,128]{1,0:T(8,128)S(1)}) custom-call(bf16[512,512]{1,0:T(8,128)(2,1)S(1)} %get-tuple-element.8.wh, bf16[512,512]{1,0:T(8,128)(2,1)S(1)} %get-tuple-element.9.wl, f32[512,1024]{1,0:T(8,128)S(1)} %copy-done, f32[544,128]{1,0:T(8,128)S(1)} %add_dynamic-update-slice_fusion.mine0, ...), custom_call_target="tpu_custom_call" | custom-call | tf_op jit(solution)/shard_map/pallas_call | solution.py:207
  78.0 4.1 %shard_map.80 = (f32[512,1024]{1,0:T(8,128)}, f32[64,512]{1,0:T(8,128)}) custom-call(bf16[512,512]{1,0:T(8,128)(2,1)S(1)} %get-tuple-element.8.wh, bf16[512,512]{1,0:T(8,128)(2,1)S(1)} %get-tuple-element.9.wl, f32[512,1024]{1,0:T(8,128)S(1)} %copy-done, f32[2176,128]{1,0:T(8,128)} %collective-permute-done.9.others, ...), custom_call_target="tpu_custom_call", output_to_operand_aliasing={{0}: (7, {})} | custom-call | tf_op jit(solution)/shard_map/pallas_call | solution.py:207
  (19 shorter events, 0.1 us)
Async XLA Ops:
  0.6 22.2 %collective-permute-start.1 = (f32[32,512]{1,0:T(8,128)}, f32[32,512]{1,0:T(8,128)S(1)}, u32[]{:S(2)}, u32[]{:S(2)}) collective-permute-start(f32[32,512]{1,0:T(8,128)} %panel.1), channel_id=1, source_target_pairs={{0,256},{16,272},{32,353},{48,369},{64,482},{80,498},{96,291},{112... | collective-permute-start | bytes 196616 | tf_op jit(solution)/shard_map/ppermute | solution.py:63
  19.0 3.7 %copy-start.3 = (f32[16,64]{1,0:T(8,128)S(1)}, f32[16,64]{1,0:T(8,128)}, u32[]{:S(2)}) copy-start(f32[16,64]{1,0:T(8,128)} %param.10) | copy-start | bytes 12292
  19.1 50.7 %all-to-all-start = ((f32[16,48,512]{2,1,0:T(8,128)}), f32[16,48,512]{2,1,0:T(8,128)S(1)}, u32[]{:S(2)}, u32[]{:S(2)}) async-start(f32[16,48,512]{2,1,0:T(8,128)} %shard_map.77), calls=%async_computation | async-start | bytes 3145728 | tf_op jit(solution)/shard_map/all_to_all | solution.py:238
  22.9 16.0 %collective-permute-start.4 = (f32[136,128]{1,0:T(8,128)S(1)}, f32[136,128]{1,0:T(8,128)S(1)}, u32[]{:S(2)}, u32[]{:S(2)}) collective-permute-start(f32[136,128]{1,0:T(8,128)S(1)} %maximum_maximum_fusion), channel_id=1, source_target_pairs={{0,256},{32,288},{64,320},{96,352},{128,384},{160,416},{192,448},{... | collective-permute-start | bytes 208904 | tf_op jit(solution)/shard_map/ppermute | solution.py:63
  23.5 9.3 %collective-permute-start.3 = (f32[136,128]{1,0:T(8,128)S(1)}, f32[136,128]{1,0:T(8,128)S(1)}, u32[]{:S(2)}, u32[]{:S(2)}) collective-permute-start(f32[136,128]{1,0:T(8,128)S(1)} %maximum_maximum_fusion), channel_id=1, source_target_pairs={{0,384},{16,400},{32,416},{48,432},{64,448},{80,464},{96,480},{112... | collective-permute-start | bytes 208904 | tf_op jit(solution)/shard_map/ppermute | solution.py:63
  28.9 10.0 %collective-permute-start.2 = (f32[136,128]{1,0:T(8,128)S(1)}, f32[136,128]{1,0:T(8,128)S(1)}, u32[]{:S(2)}, u32[]{:S(2)}) collective-permute-start(f32[136,128]{1,0:T(8,128)S(1)} %maximum_maximum_fusion), channel_id=1, source_target_pairs={{0,128},{16,144},{32,160},{48,176},{64,192},{80,208},{96,224},{112... | collective-permute-start | bytes 208904 | tf_op jit(solution)/shard_map/ppermute | solution.py:63
  32.8 9.3 %collective-permute-start.5 = (f32[136,128]{1,0:T(8,128)S(1)}, f32[136,128]{1,0:T(8,128)S(1)}, u32[]{:S(2)}, u32[]{:S(2)}) collective-permute-start(f32[136,128]{1,0:T(8,128)S(1)} %collective-permute-done.3), channel_id=1, source_target_pairs={{16,400},{48,432},{80,464},{112,496},{144,16},{176,48},{208,80},{2... | collective-permute-start | bytes 208904 | tf_op jit(solution)/shard_map/ppermute | solution.py:63
  42.2 16.1 %collective-permute-start.8 = (f32[544,128]{1,0:T(8,128)S(1)}, f32[544,128]{1,0:T(8,128)S(1)}, u32[]{:S(2)}, u32[]{:S(2)}) collective-permute-start(f32[544,128]{1,0:T(8,128)S(1)} %add_dynamic-update-slice_fusion.mine0), channel_id=1, source_target_pairs={{0,64},{16,464},{32,96},{48,496},{64,128},{80,16},{96,160},{112,48... | collective-permute-start | bytes 835592 | tf_op jit(solution)/shard_map/ppermute | solution.py:63
  51.6 12.7 %collective-permute-start.7 = (f32[544,128]{1,0:T(8,128)S(1)}, f32[544,128]{1,0:T(8,128)S(1)}, u32[]{:S(2)}, u32[]{:S(2)}) collective-permute-start(f32[544,128]{1,0:T(8,128)S(1)} %add_dynamic-update-slice_fusion.mine0), channel_id=1, source_target_pairs={{0,480},{16,496},{32,0},{48,16},{64,32},{80,48},{96,64},{112,80},{... | collective-permute-start | bytes 835592 | tf_op jit(solution)/shard_map/ppermute | solution.py:63
  53.5 11.7 %collective-permute-start.6 = (f32[544,128]{1,0:T(8,128)S(1)}, f32[544,128]{1,0:T(8,128)S(1)}, u32[]{:S(2)}, u32[]{:S(2)}) collective-permute-start(f32[544,128]{1,0:T(8,128)S(1)} %add_dynamic-update-slice_fusion.mine0), channel_id=1, source_target_pairs={{0,32},{16,48},{32,64},{48,80},{64,96},{80,112},{96,128},{112,144}... | collective-permute-start | bytes 835592 | tf_op jit(solution)/shard_map/ppermute | solution.py:63
  66.3 11.7 %collective-permute-start.9 = (f32[2176,128]{1,0:T(8,128)}, f32[2176,128]{1,0:T(8,128)}, u32[]{:S(2)}, u32[]{:S(2)}) collective-permute-start(f32[2176,128]{1,0:T(8,128)} %pad_maximum_fusion), channel_id=1, source_target_pairs={{0,16},{16,0},{32,48},{48,32},{64,80},{80,64},{96,112},{112,96},{1... | collective-permute-start | bytes 3342344 | tf_op jit(solution)/shard_map/ppermute | solution.py:63
  69.8 5.8 %copy-start = (f32[512,1024]{1,0:T(8,128)S(1)}, f32[512,1024]{1,0:T(8,128)}, u32[]{:S(2)}) copy-start(f32[512,1024]{1,0:T(8,128)} %vin.3) | copy-start | bytes 6291460
  69.8 3.9 %collective-permute-start = (f32[16,16,512]{2,1,0:T(8,128)S(1)}, f32[16,16,512]{2,1,0:T(8,128)S(1)}, u32[]{:S(2)}, u32[]{:S(2)}) collective-permute-start(f32[16,16,512]{2,1,0:T(8,128)S(1)} %slice.12), channel_id=1, source_target_pairs={{0,16},{16,0},{32,48},{48,32},{64,80},{80,64},{96,112},{112,96},{1... | collective-permute-start | bytes 1572872 | tf_op jit(solution)/shard_map/ppermute | solution.py:63
  75.7 2.3 %copy-start.1 = (f32[512,64]{0,1:T(8,128)S(1)}, f32[512,64]{0,1:T(8,128)}, u32[]{:S(2)}) copy-start(f32[512,64]{0,1:T(8,128)} %param.9) | copy-start | bytes 393220
  75.7 2.3 %copy-start.2 = (s32[64]{0:T(128)S(1)}, s32[64]{0:T(128)}, u32[]{:S(2)}) copy-start(s32[64]{0:T(128)} %param.11) | copy-start | bytes 772
